TPU v7x, 256 devices: a whole 4x4x8 slice. The times are simulated.
256 devices in a mesh: seq: 64 (over x, z, core), head: 4 (over y).
Axes of the slice: x: 4, y: 4, z: 8, core: 2. Of those that a mesh axis runs over, the one named last changes fastest.
Arguments:
- queries: bfloat16 [16384, 8192], P('seq', 'head'), may hold values from -200 to 200
- keys: bfloat16 [16384, 1024], P('seq', 'head'), may hold values from -6 to 6
- values: bfloat16 [16384, 1024], P('seq', 'head'), may hold values from -6 to 6
- output_gradient: bfloat16 [16384, 8192], P('seq', 'head'), may hold values from -6 to 6
- lengths: int32 [32], replicated, may hold values from 1 to 1024, 16384 in all
Outputs:
- attn_out: bfloat16 [16384, 8192], P(('seq', 'head'))
- d_queries: bfloat16 [16384, 8192], P('seq', 'head')
- key_gradient: bfloat16 [16384, 1024], P('seq', 'head')
- value_gradient: bfloat16 [16384, 1024], P('seq', 'head')
Inputs may be any that keep to these rules, and one draw needn't show every extreme that they name: 32 lengths that sum to 16384; the longest is exactly 1024.
All inputs are finite; a program needn't handle non-finite values.
Results may differ from a plain program's by a relative error of at most 0.035.
Values may be sent and summed in bfloat16 or wider, within the bound.
No kernel may reach another device: no remote copies, remote signals or barrier semaphores. Data moves between devices by JAX's collectives and lax.ppermute only.
A program may use at most 128 MiB of HBM per device.

v0:
```python
import math

import jax
import jax.numpy as jnp
from jax import lax
from jax.sharding import PartitionSpec as P

HEAD_WIDTH = 128
REACH = 4


def shifted(value, axis, steps):
    count = lax.axis_size(axis)
    initial, last = (max(0, -steps), min(count, count - steps))
    return lax.ppermute(value, axis, [(source, source + steps) for source in range(initial, last)])


def doc_numbers(positions, ends):
    return jnp.sum((positions[:, None] >= ends[None, :]).astype(jnp.int32), axis=1)


def on_device(queries, keys, values, output_gradient, lengths):
    rows = queries.shape[0]
    kv_heads = keys.shape[1] // HEAD_WIDTH
    query_group = queries.shape[1] // keys.shape[1]
    scale = 1.0 / math.sqrt(HEAD_WIDTH)
    here = lax.axis_index("seq")
    ends = jnp.cumsum(lengths)
    offsets = jnp.arange(rows, dtype=jnp.int32)
    query_pos = here * rows + offsets
    query_doc = doc_numbers(query_pos, ends)
    query_tensor_four = queries.reshape(rows, kv_heads, query_group, HEAD_WIDTH)
    output_cotangent = output_gradient.reshape(rows, kv_heads, query_group, HEAD_WIDTH)
    local_pair = jnp.stack((keys, values))

    def block_mask(dist):
        key_pos = (here - dist) * rows + offsets
        same = query_doc[:, None] == doc_numbers(key_pos, ends)[None, :]
        return same & (key_pos[None, :] >= 0) & (key_pos[None, :] <= query_pos[:, None])

    masks = [block_mask(dist) for dist in range(REACH + 1)]

    def scores_of(pair, allowed):
        key_tensor_three = pair[0].reshape(rows, kv_heads, HEAD_WIDTH)
        raw = (
            jnp.einsum(
                "qhgd,khd->hgqk",
                query_tensor_four,
                key_tensor_three,
                preferred_element_type=jnp.float32,
            )
            * scale
        )
        return jnp.where(allowed[None, None], raw, -jnp.inf)

    def all_scores(pairs):
        result = [scores_of(pairs[0], masks[0])]
        for dist in range(1, REACH + 1):
            result.append(scores_of(pairs[dist], masks[dist]))
        return result

    pairs = [local_pair] + [shifted(local_pair, "seq", dist) for dist in range(1, REACH + 1)]
    scores = all_scores(pairs)
    top = scores[0].max(axis=-1)
    for dist in range(1, REACH + 1):
        top = jnp.maximum(top, scores[dist].max(axis=-1))
    total = jnp.zeros_like(top)
    for dist in range(REACH + 1):
        total = total + jnp.sum(jnp.exp(scores[dist] - top[..., None]), axis=-1)
    lse = top + jnp.log(total)

    def out_part(score, pair):
        value_tensor_three = pair[1].reshape(rows, kv_heads, HEAD_WIDTH)
        probs_b = jnp.exp(score - lse[..., None]).astype(jnp.bfloat16)
        return jnp.einsum(
            "hgqk,khd->qhgd", probs_b, value_tensor_three, preferred_element_type=jnp.float32
        )

    out_sum = out_part(scores[0], pairs[0])
    for dist in range(1, REACH + 1):
        out_sum = out_sum + out_part(scores[dist], pairs[dist])
    out_heads = out_sum.astype(jnp.bfloat16)
    delta = jnp.transpose(
        jnp.sum(output_cotangent.astype(jnp.float32) * out_heads.astype(jnp.float32), axis=-1),
        (1, 2, 0),
    )
    back_pairs = [local_pair] + [shifted(local_pair, "seq", dist) for dist in range(1, REACH + 1)]
    back_scores = all_scores(back_pairs)

    def grads_of(score, pair):
        key_tensor_three = pair[0].reshape(rows, kv_heads, HEAD_WIDTH)
        value_tensor_three = pair[1].reshape(rows, kv_heads, HEAD_WIDTH)
        probs = jnp.exp(score - lse[..., None])
        probs_b = probs.astype(jnp.bfloat16)
        dprobs = jnp.einsum(
            "qhgd,khd->hgqk",
            output_cotangent,
            value_tensor_three,
            preferred_element_type=jnp.float32,
        )
        dscores = (probs * (dprobs - delta[..., None])).astype(jnp.bfloat16)
        dq_part = (
            jnp.einsum(
                "hgqk,khd->qhgd", dscores, key_tensor_three, preferred_element_type=jnp.float32
            )
            * scale
        )
        dk_part = (
            jnp.einsum(
                "hgqk,qhgd->khd", dscores, query_tensor_four, preferred_element_type=jnp.float32
            )
            * scale
        )
        dv_part = jnp.einsum(
            "hgqk,qhgd->khd", probs_b, output_cotangent, preferred_element_type=jnp.float32
        )
        return (
            dq_part,
            jnp.stack(
                (
                    dk_part.reshape(rows, kv_heads * HEAD_WIDTH),
                    dv_part.reshape(rows, kv_heads * HEAD_WIDTH),
                )
            ),
        )

    dq_total, kv_total = grads_of(back_scores[0], back_pairs[0])
    for dist in range(1, REACH + 1):
        dq_part, kv_part = grads_of(back_scores[dist], back_pairs[dist])
        dq_total = dq_total + dq_part
        kv_total = kv_total + shifted(kv_part.astype(jnp.bfloat16), "seq", -dist).astype(
            kv_part.dtype
        )
    attn_out = lax.all_to_all(
        out_heads.reshape(rows, kv_heads * query_group * HEAD_WIDTH),
        "head",
        split_axis=0,
        concat_axis=1,
        tiled=True,
    )
    d_queries = dq_total.reshape(rows, kv_heads * query_group * HEAD_WIDTH).astype(jnp.bfloat16)
    key_gradient = kv_total[0].astype(jnp.bfloat16)
    value_gradient = kv_total[1].astype(jnp.bfloat16)
    return (attn_out, d_queries, key_gradient, value_gradient)


def solution(mesh):
    placed = (P("seq", "head"), P("seq", "head"), P("seq", "head"), P("seq", "head"), P())
    return jax.shard_map(
        on_device,
        mesh=mesh,
        in_specs=placed,
        out_specs=(P(("seq", "head"), None), P("seq", "head"), P("seq", "head"), P("seq", "head")),
        check_vma=False,
    )
```

profile of v0, /device:TPU:6, one launch (start us, length us, event | category | flops | bytes accessed | tf_op | source)
XLA Modules:
  0.0 139.7 jit_solution(12239925132816919337)
XLA Ops:
  3.5 5.2 %collective-permute-start.3 = (bf16[2,256,256]{1,2,0:T(8,128)(2,1)}, bf16[2,256,256]{1,2,0:T(8,128)(2,1)}, u32[]{:S(2)}, u32[]{:S(2)}) collective-permute-start(bf16[2,256,256]{1,2,0:T(8,128)(2,1)} %pad_maximum_fusion), channel_id=1, source_target_pairs={{0,16},{4,20},{8,24},{12,28},{16,32},{20,36},{24,40},{28,44},{32,4... | collective-permute-start | bytes 786440 | tf_op jit(solution)/shard_map/ppermute | solution.py:15
  8.7 3.0 %collective-permute-start.2 = (bf16[2,256,256]{1,2,0:T(8,128)(2,1)}, bf16[2,256,256]{1,2,0:T(8,128)(2,1)}, u32[]{:S(2)}, u32[]{:S(2)}) collective-permute-start(bf16[2,256,256]{1,2,0:T(8,128)(2,1)} %pad_maximum_fusion), channel_id=1, source_target_pairs={{0,12},{4,16},{8,20},{12,24},{16,28},{20,32},{24,36},{28,40},{32,4... | collective-permute-start | bytes 786440 | tf_op jit(solution)/shard_map/ppermute | solution.py:15
  11.6 5.0 %collective-permute-start.1 = (bf16[2,256,256]{1,2,0:T(8,128)(2,1)}, bf16[2,256,256]{1,2,0:T(8,128)(2,1)}, u32[]{:S(2)}, u32[]{:S(2)}) collective-permute-start(bf16[2,256,256]{1,2,0:T(8,128)(2,1)} %pad_maximum_fusion), channel_id=1, source_target_pairs={{0,8},{4,12},{8,16},{12,20},{16,24},{20,28},{24,32},{28,36},{32,40... | collective-permute-start | bytes 786440 | tf_op jit(solution)/shard_map/ppermute | solution.py:15
  16.7 3.0 %collective-permute-start = (bf16[2,256,256]{1,2,0:T(8,128)(2,1)}, bf16[2,256,256]{1,2,0:T(8,128)(2,1)}, u32[]{:S(2)}, u32[]{:S(2)}) collective-permute-start(bf16[2,256,256]{1,2,0:T(8,128)(2,1)} %pad_maximum_fusion), channel_id=1, source_target_pairs={{0,4},{4,8},{8,12},{12,16},{16,20},{20,24},{24,28},{28,32},{32,36}... | collective-permute-start | bytes 786440 | tf_op jit(solution)/shard_map/ppermute | solution.py:15
  32.5 5.8 %collective-permute-done.1 = bf16[2,256,256]{1,2,0:T(8,128)(2,1)} collective-permute-done((bf16[2,256,256]{1,2,0:T(8,128)(2,1)}, bf16[2,256,256]{1,2,0:T(8,128)(2,1)}, u32[]{:S(2)}, u32[]{:S(2)}) %collective-permute-start.1) | collective-permute-done | bytes 262176 | tf_op jit(solution)/shard_map/ppermute | solution.py:15
  42.4 5.0 %exponential_reduce_fusion.3 = (f32[2,8,256]{2,1,0:T(8,128)S(1)}, f32[2,8,256]{2,1,0:T(8,128)S(1)}, f32[2,8,256]{2,1,0:T(8,128)S(1)}, f32[2,8,256]{2,1,0:T(8,128)S(1)}, f32[2,8,256]{2,1,0:T(8,128)S(1)}) fusion(f32[2,256,256,8]{2,1,3,0:T(8,128)S(1)} %get-tuple-element.54, f32[2,8,256]{2,1,0:T(8,128)S(1)} %maximum_maximum_fusion, ...), kind=kLoop, calls=%fused_computation.28 | loop fusion | flops 20951040 | bytes 21397504 | tf_op jit(solution)/shard_map/reduce_sum | solution.py:69
  52.1 1.8 %fusion.27 = bf16[2,256,128]{1,2,0:T(8,128)(2,1)} fusion(bf16[256,2,8,128]{0,3,2,1:T(8,128)(2,1)S(1)} %bitcast.359, f32[2,256,256,8]{2,1,3,0:T(8,128)S(1)} %get-tuple-element.54, f32[2,8,256]{2,1,0:T(8,128)S(1)} %log_add_fusion, pred[256,256]{0,1:T(8,128)(4,1)S(1)} %get-tuple-element.40), kind=kOutput, calls=%fused_computation.65 | convolution fusion | flops 272695296 | bytes 5455872 | tf_op jit(solution)/shard_map/hgqk,qhgd->khd/dot_general | solution.py:114
  53.9 2.7 %multiply_reduce_fusion = (f32[256,2,8]{0,2,1:T(8,128)S(1)}, bf16[256,2,8,128]{0,3,2,1:T(8,128)(2,1)}) fusion(bf16[256,2048]{0,1:T(8,128)(2,1)S(1)} %copy.222, bf16[256,2,128,1]{0,2,3,1:T(8,128)(2,1)S(1)} %bitcast.380, f32[2,256,256,8]{2,1,3,0:T(8,128)S(1)} %get-tuple-element.46, f32[2,8,256]{2,1,0:T(8,128)S(1)} %log_add_fusion, ...), kind=kOutput, calls=%fused_computation.50 | convolution fusion | flops 277344256 | bytes 14909440 | tf_op jit(solution)/shard_map/hgqk,khd->qhgd/dot_general | solution.py:75
  59.4 1.8 %fusion.28 = bf16[2,256,128]{1,2,0:T(8,128)(2,1)} fusion(bf16[256,2,8,128]{0,3,2,1:T(8,128)(2,1)S(1)} %bitcast.362, f32[2,256,256,8]{2,1,3,0:T(8,128)S(1)} %get-tuple-element.50, f32[2,8,256]{2,1,0:T(8,128)S(1)} %log_add_fusion, pred[256,256]{0,1:T(8,128)(4,1)S(1)} %get-tuple-element.44), kind=kOutput, calls=%fused_computation.66 | convolution fusion | flops 272695296 | bytes 5455872 | tf_op jit(solution)/shard_map/hgqk,qhgd->khd/dot_general | solution.py:114
  62.6 1.8 %fusion.29 = bf16[2,256,128]{1,2,0:T(8,128)(2,1)} fusion(bf16[256,2,8,128]{0,3,2,1:T(8,128)(2,1)S(1)} %bitcast.364, f32[2,256,256,8]{2,1,3,0:T(8,128)S(1)} %get-tuple-element.48, f32[2,8,256]{2,1,0:T(8,128)S(1)} %log_add_fusion, pred[256,256]{0,1:T(8,128)(4,1)S(1)} %get-tuple-element.41), kind=kOutput, calls=%fused_computation.67 | convolution fusion | flops 272695296 | bytes 5455872 | tf_op jit(solution)/shard_map/hgqk,qhgd->khd/dot_general | solution.py:114
  64.5 3.0 %fusion.1 = bf16[2,8,256,256]{2,3,1,0:T(8,128)(2,1)S(1)} fusion(f32[2,256,256,8]{2,1,3,0:T(8,128)S(1)} %get-tuple-element.46, bf16[256,2,128,1]{0,2,3,1:T(8,128)(2,1)S(1)} %bitcast.381, bf16[256,2,8,128]{0,3,2,1:T(8,128)(2,1)} %bitcast.365, f32[2,8,256]{2,1,0:T(8,128)S(1)} %bitcast.404, f32[2,8,256]{2,1,0:T(8,128)S(1)} %log_add_fusion, ...), kind=kOutput, calls=%fused_computation.2 | convolution fusion | flops 274726912 | bytes 7569408 | tf_op jit(solution)/shard_map/qhgd,khd->hgqk/dot_general | solution.py:95
  67.4 1.8 %fusion.30 = bf16[2,256,128]{1,2,0:T(8,128)(2,1)} fusion(bf16[256,2,8,128]{0,3,2,1:T(8,128)(2,1)S(1)} %bitcast.366, f32[2,256,256,8]{2,1,3,0:T(8,128)S(1)} %get-tuple-element.46, f32[2,8,256]{2,1,0:T(8,128)S(1)} %log_add_fusion, pred[256,256]{0,1:T(8,128)(4,1)S(1)} %get-tuple-element.42), kind=kOutput, calls=%fused_computation.68 | convolution fusion | flops 272695296 | bytes 5455872 | tf_op jit(solution)/shard_map/hgqk,qhgd->khd/dot_general | solution.py:114
  72.2 1.8 %fusion.81 = f32[2,8,256,128]{2,3,1,0:T(8,128)} fusion(bf16[256,2,128,1]{0,2,3,1:T(8,128)(2,1)S(1)} %copy.283, bf16[2,8,256,256]{2,3,1,0:T(8,128)(2,1)S(1)} %fusion.9), kind=kOutput, calls=%fused_computation.139 | convolution fusion | flops 268435456 | bytes 4325376 | tf_op jit(solution)/shard_map/hgqk,khd->qhgd/dot_general | solution.py:103
  75.5 1.8 %fusion.78 = f32[2,128,8,256]{3,1,2,0:T(8,128)} fusion(bf16[256,2,128,1]{0,2,3,1:T(8,128)(2,1)S(1)} %bitcast.377, bf16[2,8,256,256]{2,3,1,0:T(8,128)(2,1)S(1)} %fusion.7), kind=kOutput, calls=%fused_computation.136 | convolution fusion | flops 268435456 | bytes 4325376 | tf_op jit(solution)/shard_map/hgqk,khd->qhgd/dot_general | solution.py:103
  81.3 1.9 %fusion.80 = f32[2,128,8,256]{3,1,2,0:T(8,128)} fusion(bf16[256,2,128,1]{0,2,3,1:T(8,128)(2,1)S(1)} %bitcast.373, bf16[2,8,256,256]{2,3,1,0:T(8,128)(2,1)S(1)} %fusion.3), kind=kOutput, calls=%fused_computation.138 | convolution fusion | flops 268435456 | bytes 4325376 | tf_op jit(solution)/shard_map/hgqk,khd->qhgd/dot_general | solution.py:103
  88.2 1.9 %collective-permute-start.4 = (bf16[2,256,256]{2,1,0:T(8,128)(2,1)}, bf16[2,256,256]{2,1,0:T(8,128)(2,1)}, u32[]{:S(2)}, u32[]{:S(2)}) collective-permute-start(bf16[2,256,256]{2,1,0:T(8,128)(2,1)} %pad_maximum_fusion.1), channel_id=1, source_target_pairs={{4,0},{8,4},{12,8},{16,12},{20,16},{24,20},{28,24},{32,28},{36,32}... | collective-permute-start | bytes 786440 | tf_op jit(solution)/shard_map/ppermute | solution.py:15
  95.1 3.2 %collective-permute-start.5 = (bf16[2,256,256]{2,1,0:T(8,128)(2,1)}, bf16[2,256,256]{2,1,0:T(8,128)(2,1)}, u32[]{:S(2)}, u32[]{:S(2)}) collective-permute-start(bf16[2,256,256]{2,1,0:T(8,128)(2,1)} %pad_maximum_fusion.2), channel_id=1, source_target_pairs={{8,0},{12,4},{16,8},{20,12},{24,16},{28,20},{32,24},{36,28},{40,32... | collective-permute-start | bytes 786440 | tf_op jit(solution)/shard_map/ppermute | solution.py:15
  101.8 4.2 %collective-permute-start.6 = (bf16[2,256,256]{2,1,0:T(8,128)(2,1)}, bf16[2,256,256]{2,1,0:T(8,128)(2,1)}, u32[]{:S(2)}, u32[]{:S(2)}) collective-permute-start(bf16[2,256,256]{2,1,0:T(8,128)(2,1)} %pad_maximum_fusion.3), channel_id=1, source_target_pairs={{12,0},{16,4},{20,8},{24,12},{28,16},{32,20},{36,24},{40,28},{44,3... | collective-permute-start | bytes 786440 | tf_op jit(solution)/shard_map/ppermute | solution.py:15
  108.6 4.3 %collective-permute-start.7 = (bf16[2,256,256]{2,1,0:T(8,128)(2,1)}, bf16[2,256,256]{2,1,0:T(8,128)(2,1)}, u32[]{:S(2)}, u32[]{:S(2)}) collective-permute-start(bf16[2,256,256]{2,1,0:T(8,128)(2,1)} %pad_maximum_fusion.4), channel_id=1, source_target_pairs={{16,0},{20,4},{24,8},{28,12},{32,16},{36,20},{40,24},{44,28},{48,3... | collective-permute-start | bytes 786440 | tf_op jit(solution)/shard_map/ppermute | solution.py:15
  114.7 1.9 %copy.220 = bf16[256,2,8,128]{3,2,1,0:T(8,128)(2,1)S(1)} copy(bf16[256,2,8,128]{0,3,2,1:T(8,128)(2,1)} %get-tuple-element.56) | data formatting | bytes 2097152 | tf_op jit(solution)/shard_map/convert_element_type | solution.py:82
  117.9 4.5 %all-to-all-start = ((bf16[4,64,2048]{2,1,0:T(8,128)(2,1)}), bf16[4,64,2048]{2,1,0:T(8,128)(2,1)}, u32[]{:S(2)}, u32[]{:S(2)}) async-start(bf16[4,64,2048]{2,1,0:T(8,128)(2,1)} %all_to_all.14), calls=%async_computation | async-start | bytes 2097152 | tf_op jit(solution)/shard_map/all_to_all | solution.py:134
  122.4 4.6 %fusion.20 = bf16[256,2,8,128]{0,3,2,1:T(8,128)(2,1)S(1)} fusion(f32[2,128,8,256]{3,1,2,0:T(8,128)} %fusion.80, f32[2,128,8,256]{3,1,2,0:T(8,128)} %fusion.79, f32[2,128,8,256]{3,1,2,0:T(8,128)} %fusion.78, f32[2,8,256,128]{2,3,1,0:T(8,128)} %fusion.81, bf16[256,2,128,1]{0,2,3,1:T(8,128)(2,1)S(1)} %bitcast.371, bf16[2,8,256,256]{2,3,1,0:T(8,128)(2,1)S(1)} %fusion.1), kind=kOutput, calls=%fused_computation.41 | convolution fusion | flops 273678336 | bytes 11665408 | tf_op jit(solution)/shard_map/hgqk,khd->qhgd/dot_general | solution.py:103
  132.1 5.3 %all-to-all-done = bf16[4,64,2048]{2,1,0:T(8,128)(2,1)} async-done(((bf16[4,64,2048]{2,1,0:T(8,128)(2,1)}), bf16[4,64,2048]{2,1,0:T(8,128)(2,1)}, u32[]{:S(2)}, u32[]{:S(2)}) %all-to-all-start) | async-done | bytes 1048608 | tf_op jit(solution)/shard_map/all_to_all | solution.py:134
  137.4 2.3 %copy.345 = bf16[4,8,8,2048]{3,2,0,1:T(8,128)(2,1)} copy(bf16[4,8,8,2048]{3,2,1,0:T(8,128)(2,1)} %bitcast.149) | data formatting | bytes 2097152 | tf_op jit(solution)/shard_map/all_to_all | solution.py:134
  (87 shorter events, 61.0 us)
Async XLA Ops:
  0.6 24.4 %copy-start.6 = (bf16[256,2048]{1,0:T(8,128)(2,1)S(1)}, bf16[256,2048]{1,0:T(8,128)(2,1)}, u32[]{:S(2)}) copy-start(bf16[256,2048]{1,0:T(8,128)(2,1)} %param.8) | copy-start | bytes 3145732
  3.5 23.7 %collective-permute-start.3 = (bf16[2,256,256]{1,2,0:T(8,128)(2,1)}, bf16[2,256,256]{1,2,0:T(8,128)(2,1)}, u32[]{:S(2)}, u32[]{:S(2)}) collective-permute-start(bf16[2,256,256]{1,2,0:T(8,128)(2,1)} %pad_maximum_fusion), channel_id=1, source_target_pairs={{0,16},{4,20},{8,24},{12,28},{16,32},{20,36},{24,40},{28,44},{32,4... | collective-permute-start | bytes 786440 | tf_op jit(solution)/shard_map/ppermute | solution.py:15
  8.7 22.0 %collective-permute-start.2 = (bf16[2,256,256]{1,2,0:T(8,128)(2,1)}, bf16[2,256,256]{1,2,0:T(8,128)(2,1)}, u32[]{:S(2)}, u32[]{:S(2)}) collective-permute-start(bf16[2,256,256]{1,2,0:T(8,128)(2,1)} %pad_maximum_fusion), channel_id=1, source_target_pairs={{0,12},{4,16},{8,20},{12,24},{16,28},{20,32},{24,36},{28,40},{32,4... | collective-permute-start | bytes 786440 | tf_op jit(solution)/shard_map/ppermute | solution.py:15
  11.6 26.6 %collective-permute-start.1 = (bf16[2,256,256]{1,2,0:T(8,128)(2,1)}, bf16[2,256,256]{1,2,0:T(8,128)(2,1)}, u32[]{:S(2)}, u32[]{:S(2)}) collective-permute-start(bf16[2,256,256]{1,2,0:T(8,128)(2,1)} %pad_maximum_fusion), channel_id=1, source_target_pairs={{0,8},{4,12},{8,16},{12,20},{16,24},{20,28},{24,32},{28,36},{32,40... | collective-permute-start | bytes 786440 | tf_op jit(solution)/shard_map/ppermute | solution.py:15
  16.7 23.9 %collective-permute-start = (bf16[2,256,256]{1,2,0:T(8,128)(2,1)}, bf16[2,256,256]{1,2,0:T(8,128)(2,1)}, u32[]{:S(2)}, u32[]{:S(2)}) collective-permute-start(bf16[2,256,256]{1,2,0:T(8,128)(2,1)} %pad_maximum_fusion), channel_id=1, source_target_pairs={{0,4},{4,8},{8,12},{12,16},{16,20},{20,24},{24,28},{28,32},{32,36}... | collective-permute-start | bytes 786440 | tf_op jit(solution)/shard_map/ppermute | solution.py:15
  25.5 37.1 %copy-start.2 = (bf16[256,2048]{0,1:T(8,128)(2,1)}, bf16[256,2048]{0,1:T(8,128)(2,1)S(1)}, u32[]{:S(2)}) copy-start(bf16[256,2048]{0,1:T(8,128)(2,1)S(1)} %copy.222) | copy-start | bytes 3145732
  27.2 42.1 %copy-start = (f32[2,256,256,8]{2,1,3,0:T(8,128)}, f32[2,256,256,8]{2,1,3,0:T(8,128)S(1)}, u32[]{:S(2)}) copy-start(f32[2,256,256,8]{2,1,3,0:T(8,128)S(1)} %get-tuple-element.52) | copy-start | bytes 12582916
  42.4 5.1 %copy-start.7 = (bf16[256,2,128,1]{0,2,3,1:T(8,128)(2,1)S(1)}, bf16[256,2,128,1]{0,2,3,1:T(8,128)(2,1)}, u32[]{:S(2)}) copy-start(bf16[256,2,128,1]{0,2,3,1:T(8,128)(2,1)} %copy.271) | copy-start | bytes 393220
  64.5 3.0 %copy-start.3 = (bf16[256,2048]{0,1:T(8,128)(2,1)S(1)}, bf16[256,2048]{0,1:T(8,128)(2,1)}, u32[]{:S(2)}) copy-start(bf16[256,2048]{0,1:T(8,128)(2,1)} %copy-done.2) | copy-start | bytes 3145732
  88.2 41.9 %collective-permute-start.4 = (bf16[2,256,256]{2,1,0:T(8,128)(2,1)}, bf16[2,256,256]{2,1,0:T(8,128)(2,1)}, u32[]{:S(2)}, u32[]{:S(2)}) collective-permute-start(bf16[2,256,256]{2,1,0:T(8,128)(2,1)} %pad_maximum_fusion.1), channel_id=1, source_target_pairs={{4,0},{8,4},{12,8},{16,12},{20,16},{24,20},{28,24},{32,28},{36,32}... | collective-permute-start | bytes 786440 | tf_op jit(solution)/shard_map/ppermute | solution.py:15
  95.1 34.9 %collective-permute-start.5 = (bf16[2,256,256]{2,1,0:T(8,128)(2,1)}, bf16[2,256,256]{2,1,0:T(8,128)(2,1)}, u32[]{:S(2)}, u32[]{:S(2)}) collective-permute-start(bf16[2,256,256]{2,1,0:T(8,128)(2,1)} %pad_maximum_fusion.2), channel_id=1, source_target_pairs={{8,0},{12,4},{16,8},{20,12},{24,16},{28,20},{32,24},{36,28},{40,32... | collective-permute-start | bytes 786440 | tf_op jit(solution)/shard_map/ppermute | solution.py:15
  101.8 28.3 %collective-permute-start.6 = (bf16[2,256,256]{2,1,0:T(8,128)(2,1)}, bf16[2,256,256]{2,1,0:T(8,128)(2,1)}, u32[]{:S(2)}, u32[]{:S(2)}) collective-permute-start(bf16[2,256,256]{2,1,0:T(8,128)(2,1)} %pad_maximum_fusion.3), channel_id=1, source_target_pairs={{12,0},{16,4},{20,8},{24,12},{28,16},{32,20},{36,24},{40,28},{44,3... | collective-permute-start | bytes 786440 | tf_op jit(solution)/shard_map/ppermute | solution.py:15
  108.6 21.4 %collective-permute-start.7 = (bf16[2,256,256]{2,1,0:T(8,128)(2,1)}, bf16[2,256,256]{2,1,0:T(8,128)(2,1)}, u32[]{:S(2)}, u32[]{:S(2)}) collective-permute-start(bf16[2,256,256]{2,1,0:T(8,128)(2,1)} %pad_maximum_fusion.4), channel_id=1, source_target_pairs={{16,0},{20,4},{24,8},{28,12},{32,16},{36,20},{40,24},{44,28},{48,3... | collective-permute-start | bytes 786440 | tf_op jit(solution)/shard_map/ppermute | solution.py:15
  117.9 19.5 %all-to-all-start = ((bf16[4,64,2048]{2,1,0:T(8,128)(2,1)}), bf16[4,64,2048]{2,1,0:T(8,128)(2,1)}, u32[]{:S(2)}, u32[]{:S(2)}) async-start(bf16[4,64,2048]{2,1,0:T(8,128)(2,1)} %all_to_all.14), calls=%async_computation | async-start | bytes 2097152 | tf_op jit(solution)/shard_map/all_to_all | solution.py:134
  122.4 4.7 %copy-start.1 = (f32[2,256,256,8]{2,1,3,0:T(8,128)S(1)}, f32[2,256,256,8]{2,1,3,0:T(8,128)}, u32[]{:S(2)}) copy-start(f32[2,256,256,8]{2,1,3,0:T(8,128)} %copy-done) | copy-start | bytes 12582916
  122.4 4.9 %copy-start.4 = (bf16[256,2048]{0,1:T(8,128)(2,1)S(1)}, bf16[256,2048]{0,1:T(8,128)(2,1)}, u32[]{:S(2)}) copy-start(bf16[256,2048]{0,1:T(8,128)(2,1)} %copy-done.2) | copy-start | bytes 3145732
  127.3 2.7 %copy-start.5 = (f32[1,256,256]{2,1,0:T(8,128)S(1)}, f32[1,256,256]{2,1,0:T(8,128)}, u32[]{:S(2)}) copy-start(f32[1,256,256]{2,1,0:T(8,128)} %copy.242) | copy-start | bytes 786436
where the time goes:
time: 141 us; the launch traced here: 140 us
  matrix products  46.2 us (33%)
  starting transfers between devices  34.3 us (24%)
  local copies, waits for them, and re-layouts  31.2 us (22%)
  other arithmetic  13.9 us (10%)
  waiting for transfers between devices  12.9 us (9%)
    ppermute x8, starting transfers between devices, shifted(): lax.ppermute(value, axis, [(source, source + steps) for source in range(i...  29.9 us
    dot_general x5, matrix products, grads_of(): jnp.einsum('hgqk,khd->qhgd', dscores, key_tensor_three, preferred_element...  11.8 us
    another operation x10, local copies, waits for them, and re-layouts, grads_of(): jnp.stack((dk_part.reshape(rows, kv_heads * HEAD_WIDTH), dv_part.reshape(...  11.4 us
    dot_general x5, matrix products, grads_of(): jnp.einsum('qhgd,khd->hgqk', output_cotangent, value_tensor_three, prefer...  8.62 us
    dot_general x5, matrix products, grads_of(): jnp.einsum('hgqk,qhgd->khd', probs_b, output_cotangent, preferred_element...  8.41 us
    ppermute x8, waiting for transfers between devices, shifted(): lax.ppermute(value, axis, [(source, source + steps) for source in range(i...  7.62 us
    dot_general x5, matrix products, out_part(): jnp.einsum('hgqk,khd->qhgd', probs_b, value_tensor_three, preferred_eleme...  7.23 us
    dot_general x5, matrix products, grads_of(): jnp.einsum('hgqk,qhgd->khd', dscores, query_tensor_four, preferred_elemen...  6.08 us
  transfers between devices with their start and end apart: 9, of which 4 were waited for; matrix products, arithmetic and copies ran while one was open for 27% of the time, Pallas kernels for 0%

commit v1 on v0

v1 whole, which is shorter than its diff:
```python
import functools
import math

import jax
import jax.numpy as jnp
from jax import lax
from jax.experimental import pallas as pl
from jax.experimental.pallas import tpu as pltpu
from jax.sharding import PartitionSpec as P

HEAD_WIDTH = 128
REACH = 4
NEG = -1e30
LOG2E = 1.4426950408889634
HEADS_PER_STEP = 4


def dot(a, b):
    return lax.dot_general(a, b, (((1,), (0,)), ((), ())), preferred_element_type=jnp.float32)


def dot_t(a, b):
    return lax.dot_general(a, b, (((1,), (1,)), ((), ())), preferred_element_type=jnp.float32)


def shifted(value, steps):
    count = lax.axis_size("seq")
    initial, last = (max(0, -steps), min(count, count - steps))
    return lax.ppermute(value, "seq", [(source, source + steps) for source in range(initial, last)])


def attention_kernel(scale, lens, here, *refs):
    q_ref, g_ref = refs[0:2]
    far_refs = refs[2 : 2 + REACH]
    k_ref, v_ref = refs[2 + REACH : 4 + REACH]
    outs = refs[-(6 + REACH) :]
    o_ref, dq_ref = outs[0:2]
    part_refs = outs[2 : 2 + REACH]
    own_ref = outs[2 + REACH]
    bias, dkt, dvt = outs[3 + REACH : 6 + REACH]
    rows, width = k_ref.shape
    blocks = REACH + 1
    step = pl.program_id(0)

    @pl.when(step == 0)
    def _():
        base = here[0] * rows
        row = lax.broadcasted_iota(jnp.int32, (rows, width), 0)
        col = lax.broadcasted_iota(jnp.int32, (rows, width), 1)

        def one(i, carry):
            end, start = carry
            end = end + lens[i]
            return end, jnp.where(row >= end - base, end - base, start)

        _, start = lax.fori_loop(
            0, lens.shape[0], one, (jnp.int32(0), jnp.full((rows, width), -base, jnp.int32))
        )
        for t in range(blocks * rows // width):
            pos = col + (t * width - REACH * rows)
            bias[:, t * width : (t + 1) * width] = jnp.where(
                (pos >= start) & (pos <= row), 0.0, NEG
            ).astype(jnp.float32)
        dkt[...] = jnp.zeros_like(dkt)
        dvt[...] = jnp.zeros_like(dvt)

    def key(b):
        return far_refs[b][:, :width] if b < REACH else k_ref[...]

    def val(b):
        return far_refs[b][:, width:] if b < REACH else v_ref[...]

    for h in range(q_ref.shape[1] // width):
        at = slice(h * width, (h + 1) * width)
        q, g = q_ref[:, at], g_ref[:, at]
        s = [dot_t(q, key(b)) + bias[:, b * rows : (b + 1) * rows] for b in range(blocks)]
        top = functools.reduce(jnp.maximum, s).max(axis=1, keepdims=True)
        p = [jnp.exp2((x - top) * (scale * LOG2E)) for x in s]
        total = functools.reduce(jnp.add, p).sum(axis=1, keepdims=True)
        pb = [x.astype(jnp.bfloat16) for x in p]
        o = functools.reduce(jnp.add, [dot(pb[b], val(b)) for b in range(blocks)])
        inverse = 1.0 / total
        o = o * inverse
        o_ref[:, at] = o.astype(jnp.bfloat16)
        gs = (g.astype(jnp.float32) * inverse).astype(jnp.bfloat16)
        delta = jnp.sum(gs.astype(jnp.float32) * o, axis=1, keepdims=True)
        qt, gt = q.T, gs.T
        dq = jnp.zeros((rows, width), jnp.float32)
        for b in range(blocks):
            ds = (p[b] * (dot_t(gs, val(b)) - delta)).astype(jnp.bfloat16)
            dq = dq + dot(ds, key(b))
            dkt[:, b * rows : (b + 1) * rows] += dot(qt, ds)
            dvt[:, b * rows : (b + 1) * rows] += dot(gt, pb[b])
        dq_ref[:, at] = (dq * scale).astype(jnp.bfloat16)

    @pl.when(step == pl.num_programs(0) - 1)
    def _():
        for b in range(blocks):
            at = slice(b * rows, (b + 1) * rows)
            dk = dkt[:, at].T * scale
            dv = dvt[:, at].T
            ref = part_refs[b] if b < REACH else own_ref
            ref[:, :width] = dk.astype(ref.dtype)
            ref[:, width:] = dv.astype(ref.dtype)


def attention(group, lens, here, q, g, keys, values, far, dq_before):
    rows, width = q.shape[0], HEAD_WIDTH
    groups = keys.shape[1] // width
    per_group = q.shape[1] // width // groups
    steps = per_group // HEADS_PER_STEP
    cols = HEADS_PER_STEP * width
    into = pl.BlockSpec((rows, cols), lambda i, *_: (0, group * steps + i))
    out = pl.BlockSpec((rows, cols), lambda i, *_: (0, i))
    own = pl.BlockSpec((rows, width), lambda i, *_: (0, group))
    block = pl.BlockSpec((rows, 2 * width), lambda i, *_: (0, 0))
    extra = [] if dq_before is None else [dq_before]
    alias = {} if dq_before is None else {2 + 2 + REACH + 2: 1}
    flops = 6 * 2 * rows * (REACH + 1) * rows * width * per_group
    return pl.pallas_call(
        functools.partial(attention_kernel, 1.0 / math.sqrt(width)),
        grid_spec=pltpu.PrefetchScalarGridSpec(
            num_scalar_prefetch=2,
            grid=(steps,),
            in_specs=[into, into]
            + [block] * REACH
            + [own, own]
            + [pl.BlockSpec(memory_space=pl.ANY)] * len(extra),
            out_specs=[out, into] + [block] * (REACH + 1),
            scratch_shapes=[
                pltpu.VMEM((rows, (REACH + 1) * rows), jnp.float32),
                pltpu.VMEM((width, (REACH + 1) * rows), jnp.float32),
                pltpu.VMEM((width, (REACH + 1) * rows), jnp.float32),
            ],
        ),
        out_shape=[
            jax.ShapeDtypeStruct((rows, per_group * width), jnp.bfloat16),
            jax.ShapeDtypeStruct(q.shape, jnp.bfloat16),
        ]
        + [jax.ShapeDtypeStruct((rows, 2 * width), jnp.bfloat16)] * REACH
        + [jax.ShapeDtypeStruct((rows, 2 * width), jnp.float32)],
        input_output_aliases=alias,
        compiler_params=pltpu.CompilerParams(vmem_limit_bytes=40 << 20),
        cost_estimate=pl.CostEstimate(flops=flops, bytes_accessed=4 << 20, transcendentals=0),
        name="attention",
    )(lens, here, q, g, *far, keys, values, *extra)


def on_device(queries, keys, values, output_gradient, lengths):
    rows = queries.shape[0]
    width = HEAD_WIDTH
    groups = keys.shape[1] // width
    here = lax.axis_index("seq").reshape(1).astype(jnp.int32)
    fars = []
    for g in range(groups):
        at = slice(g * width, (g + 1) * width)
        pack = jnp.concatenate((keys[:, at], values[:, at]), axis=1)
        fars.append([shifted(pack, dist) for dist in range(REACH, 0, -1)])
    d_queries = None
    heads, sums = [], []
    for g in range(groups):
        out, d_queries, *parts = attention(
            g, lengths, here, queries, output_gradient, keys, values, fars[g], d_queries
        )
        total = parts[REACH]
        for b in range(REACH):
            total = total + shifted(parts[b], b - REACH).astype(jnp.float32)
        sums.append(total)
        split = lax.axis_size("head")
        heads.append(
            lax.all_to_all(
                out.reshape(split, rows // split, out.shape[1]), "head", split_axis=0, concat_axis=0
            )
        )
    both = jnp.stack(heads, axis=2)
    attn_out = jnp.transpose(both, (1, 0, 2, 3)).reshape(both.shape[1], -1)
    key_gradient = jnp.concatenate([s[:, :width] for s in sums], axis=1).astype(jnp.bfloat16)
    value_gradient = jnp.concatenate([s[:, width:] for s in sums], axis=1).astype(jnp.bfloat16)
    return (attn_out, d_queries, key_gradient, value_gradient)


def solution(mesh):
    placed = (P("seq", "head"), P("seq", "head"), P("seq", "head"), P("seq", "head"), P())
    return jax.shard_map(
        on_device,
        mesh=mesh,
        in_specs=placed,
        out_specs=(P(("seq", "head"), None), P("seq", "head"), P("seq", "head"), P("seq", "head")),
        check_vma=False,
    )
```

time: 141 us -> 123 us (0.87)
  the two profiles are of different devices: /device:TPU:6 before, /device:TPU:3 now
where the time goes in v1:
time: 123 us; the launch traced here: 122 us
  starting transfers between devices  61.6 us (50%)
  Pallas kernels  31.8 us (26%)
  waiting for transfers between devices  17.4 us (14%)
  local copies, waits for them, and re-layouts  6.8 us (6%)
  other arithmetic  3.37 us (3%)
    ppermute x16, starting transfers between devices, shifted(): lax.ppermute(value, 'seq', [(source, source + steps) for source in range(...  52.7 us
    pallas_call x2, Pallas kernels, attention(): pl.pallas_call(functools.partial(attention_kernel, 1.0 / math.sqrt(width)...  31.8 us
    all_to_all x2, starting transfers between devices, on_device(): lax.all_to_all(out.reshape(split, rows // split, out.shape[1]), 'head', s...  8.84 us
    ppermute x16, waiting for transfers between devices, shifted(): lax.ppermute(value, 'seq', [(source, source + steps) for source in range(...  8.74 us
    all_to_all x2, waiting for transfers between devices, on_device(): lax.all_to_all(out.reshape(split, rows // split, out.shape[1]), 'head', s...  8.64 us
    unnamed x16, local copies, waits for them, and re-layouts  3.12 us
  transfers between devices with their start and end apart: 18, of which 4 were waited for; matrix products, arithmetic and copies ran while one was open for 2% of the time, Pallas kernels for 26%

profile of v1, /device:TPU:3, one launch (start us, length us, event | category | flops | bytes accessed | tf_op | source)
XLA Modules:
  0.0 121.9 jit_solution(15051313599505320703)
XLA Ops:
  1.6 4.1 %collective-permute-start.3 = (bf16[256,256]{1,0:T(8,128)(2,1)S(1)}, bf16[256,256]{1,0:T(8,128)(2,1)S(1)}, u32[]{:S(2)}, u32[]{:S(2)}) collective-permute-start(bf16[256,256]{1,0:T(8,128)(2,1)S(1)} %pad_maximum_fusion), channel_id=1, source_target_pairs={{0,4},{4,8},{8,12},{12,16},{16,20},{20,24},{24,28},{28,32},{32,36}... | collective-permute-start | bytes 393224 | tf_op jit(solution)/shard_map/ppermute | solution.py:29
  5.7 3.5 %collective-permute-start.2 = (bf16[256,256]{1,0:T(8,128)(2,1)S(1)}, bf16[256,256]{1,0:T(8,128)(2,1)S(1)}, u32[]{:S(2)}, u32[]{:S(2)}) collective-permute-start(bf16[256,256]{1,0:T(8,128)(2,1)S(1)} %pad_maximum_fusion), channel_id=1, source_target_pairs={{0,8},{4,12},{8,16},{12,20},{16,24},{20,28},{24,32},{28,36},{32,40... | collective-permute-start | bytes 393224 | tf_op jit(solution)/shard_map/ppermute | solution.py:29
  9.3 3.6 %collective-permute-start.1 = (bf16[256,256]{1,0:T(8,128)(2,1)S(1)}, bf16[256,256]{1,0:T(8,128)(2,1)S(1)}, u32[]{:S(2)}, u32[]{:S(2)}) collective-permute-start(bf16[256,256]{1,0:T(8,128)(2,1)S(1)} %pad_maximum_fusion), channel_id=1, source_target_pairs={{0,12},{4,16},{8,20},{12,24},{16,28},{20,32},{24,36},{28,40},{32,4... | collective-permute-start | bytes 393224 | tf_op jit(solution)/shard_map/ppermute | solution.py:29
  12.8 5.2 %collective-permute-start = (bf16[256,256]{1,0:T(8,128)(2,1)S(1)}, bf16[256,256]{1,0:T(8,128)(2,1)S(1)}, u32[]{:S(2)}, u32[]{:S(2)}) collective-permute-start(bf16[256,256]{1,0:T(8,128)(2,1)S(1)} %pad_maximum_fusion), channel_id=1, source_target_pairs={{0,16},{4,20},{8,24},{12,28},{16,32},{20,36},{24,40},{28,44},{32,4... | collective-permute-start | bytes 393224 | tf_op jit(solution)/shard_map/ppermute | solution.py:29
  18.8 3.2 %collective-permute-start.7 = (bf16[256,256]{1,0:T(8,128)(2,1)}, bf16[256,256]{1,0:T(8,128)(2,1)S(1)}, u32[]{:S(2)}, u32[]{:S(2)}) collective-permute-start(bf16[256,256]{1,0:T(8,128)(2,1)} %pad_maximum_fusion.1), channel_id=1, source_target_pairs={{0,4},{4,8},{8,12},{12,16},{16,20},{20,24},{24,28},{28,32},{32,36}... | collective-permute-start | bytes 393224 | tf_op jit(solution)/shard_map/ppermute | solution.py:29
  22.0 2.6 %collective-permute-start.6 = (bf16[256,256]{1,0:T(8,128)(2,1)}, bf16[256,256]{1,0:T(8,128)(2,1)S(1)}, u32[]{:S(2)}, u32[]{:S(2)}) collective-permute-start(bf16[256,256]{1,0:T(8,128)(2,1)} %pad_maximum_fusion.1), channel_id=1, source_target_pairs={{0,8},{4,12},{8,16},{12,20},{16,24},{20,28},{24,32},{28,36},{32,40... | collective-permute-start | bytes 393224 | tf_op jit(solution)/shard_map/ppermute | solution.py:29
  24.6 1.9 %collective-permute-start.5 = (bf16[256,256]{1,0:T(8,128)(2,1)}, bf16[256,256]{1,0:T(8,128)(2,1)S(1)}, u32[]{:S(2)}, u32[]{:S(2)}) collective-permute-start(bf16[256,256]{1,0:T(8,128)(2,1)} %pad_maximum_fusion.1), channel_id=1, source_target_pairs={{0,12},{4,16},{8,20},{12,24},{16,28},{20,32},{24,36},{28,40},{32,4... | collective-permute-start | bytes 393224 | tf_op jit(solution)/shard_map/ppermute | solution.py:29
  26.6 2.9 %collective-permute-start.4 = (bf16[256,256]{1,0:T(8,128)(2,1)}, bf16[256,256]{1,0:T(8,128)(2,1)S(1)}, u32[]{:S(2)}, u32[]{:S(2)}) collective-permute-start(bf16[256,256]{1,0:T(8,128)(2,1)} %pad_maximum_fusion.1), channel_id=1, source_target_pairs={{0,16},{4,20},{8,24},{12,28},{16,32},{20,36},{24,40},{28,44},{32,4... | collective-permute-start | bytes 393224 | tf_op jit(solution)/shard_map/ppermute | solution.py:29
  32.0 15.9 %attention.2 = (bf16[256,1024]{1,0:T(8,128)(2,1)}, bf16[256,2048]{1,0:T(8,128)(2,1)}, bf16[256,256]{1,0:T(8,128)(2,1)S(1)}, bf16[256,256]{1,0:T(8,128)(2,1)S(1)}...) custom-call(s32[32]{0:T(128)S(1)} %copy-done.7, s32[1]{0:T(128)} %bitcast.here, ...), custom_call_target="tpu_custom_call" | custom-call | flops 4026531840 | bytes 4194304 | tf_op jit(solution)/shard_map/attention/pallas_call | solution.py:120
  48.6 4.3 %all-to-all-start = ((bf16[4,64,1024]{2,1,0:T(8,128)(2,1)}), bf16[4,64,1024]{2,1,0:T(8,128)(2,1)}, u32[]{:S(2)}, u32[]{:S(2)}) async-start(bf16[4,64,1024]{2,1,0:T(8,128)(2,1)} %bitcast.1), calls=%async_computation | async-start | bytes 1048576 | tf_op jit(solution)/shard_map/all_to_all | solution.py:171
  52.9 5.4 %collective-permute-start.8 = (bf16[256,256]{1,0:T(8,128)(2,1)}, bf16[256,256]{1,0:T(8,128)(2,1)S(1)}, u32[]{:S(2)}, u32[]{:S(2)}) collective-permute-start(bf16[256,256]{1,0:T(8,128)(2,1)} %copy-done.6), channel_id=1, source_target_pairs={{16,0},{20,4},{24,8},{28,12},{32,16},{36,20},{40,24},{44,28},{48,3... | collective-permute-start | bytes 393224 | tf_op jit(solution)/shard_map/ppermute | solution.py:29
  58.2 4.5 %collective-permute-start.9 = (bf16[256,256]{1,0:T(8,128)(2,1)S(1)}, bf16[256,256]{1,0:T(8,128)(2,1)S(1)}, u32[]{:S(2)}, u32[]{:S(2)}) collective-permute-start(bf16[256,256]{1,0:T(8,128)(2,1)S(1)} %get-tuple-element.24), channel_id=1, source_target_pairs={{12,0},{16,4},{20,8},{24,12},{28,16},{32,20},{36,24},{40,28},{44,3... | collective-permute-start | bytes 393224 | tf_op jit(solution)/shard_map/ppermute | solution.py:29
  62.7 2.6 %collective-permute-start.10 = (bf16[256,256]{1,0:T(8,128)(2,1)S(1)}, bf16[256,256]{1,0:T(8,128)(2,1)S(1)}, u32[]{:S(2)}, u32[]{:S(2)}) collective-permute-start(bf16[256,256]{1,0:T(8,128)(2,1)S(1)} %get-tuple-element.25), channel_id=1, source_target_pairs={{8,0},{12,4},{16,8},{20,12},{24,16},{28,20},{32,24},{36,28},{40,32... | collective-permute-start | bytes 393224 | tf_op jit(solution)/shard_map/ppermute | solution.py:29
  65.4 3.3 %collective-permute-start.11 = (bf16[256,256]{1,0:T(8,128)(2,1)S(1)}, bf16[256,256]{1,0:T(8,128)(2,1)S(1)}, u32[]{:S(2)}, u32[]{:S(2)}) collective-permute-start(bf16[256,256]{1,0:T(8,128)(2,1)S(1)} %get-tuple-element.26), channel_id=1, source_target_pairs={{4,0},{8,4},{12,8},{16,12},{20,16},{24,20},{28,24},{32,28},{36,32}... | collective-permute-start | bytes 393224 | tf_op jit(solution)/shard_map/ppermute | solution.py:29
  68.7 15.9 %attention.3 = (bf16[256,1024]{1,0:T(8,128)(2,1)}, bf16[256,2048]{1,0:T(8,128)(2,1)}, bf16[256,256]{1,0:T(8,128)(2,1)S(1)}, bf16[256,256]{1,0:T(8,128)(2,1)S(1)}...) custom-call(s32[32]{0:T(128)S(1)} %copy-done.7, ...), custom_call_target="tpu_custom_call", output_to_operand_aliasing={{1}: (10, {})} | custom-call | flops 4026531840 | bytes 4194304 | tf_op jit(solution)/shard_map/attention/pallas_call | solution.py:120
  84.7 3.1 %collective-permute-start.12 = (bf16[256,256]{1,0:T(8,128)(2,1)S(1)}, bf16[256,256]{1,0:T(8,128)(2,1)S(1)}, u32[]{:S(2)}, u32[]{:S(2)}) collective-permute-start(bf16[256,256]{1,0:T(8,128)(2,1)S(1)} %get-tuple-element.28), channel_id=1, source_target_pairs={{16,0},{20,4},{24,8},{28,12},{32,16},{36,20},{40,24},{44,28},{48,3... | collective-permute-start | bytes 393224 | tf_op jit(solution)/shard_map/ppermute | solution.py:29
  87.8 2.5 %collective-permute-start.13 = (bf16[256,256]{1,0:T(8,128)(2,1)S(1)}, bf16[256,256]{1,0:T(8,128)(2,1)S(1)}, u32[]{:S(2)}, u32[]{:S(2)}) collective-permute-start(bf16[256,256]{1,0:T(8,128)(2,1)S(1)} %get-tuple-element.29), channel_id=1, source_target_pairs={{12,0},{16,4},{20,8},{24,12},{28,16},{32,20},{36,24},{40,28},{44,3... | collective-permute-start | bytes 393224 | tf_op jit(solution)/shard_map/ppermute | solution.py:29
  90.3 1.9 %collective-permute-start.14 = (bf16[256,256]{1,0:T(8,128)(2,1)S(1)}, bf16[256,256]{1,0:T(8,128)(2,1)S(1)}, u32[]{:S(2)}, u32[]{:S(2)}) collective-permute-start(bf16[256,256]{1,0:T(8,128)(2,1)S(1)} %get-tuple-element.30), channel_id=1, source_target_pairs={{8,0},{12,4},{16,8},{20,12},{24,16},{28,20},{32,24},{36,28},{40,32... | collective-permute-start | bytes 393224 | tf_op jit(solution)/shard_map/ppermute | solution.py:29
  92.2 2.4 %collective-permute-start.15 = (bf16[256,256]{1,0:T(8,128)(2,1)S(1)}, bf16[256,256]{1,0:T(8,128)(2,1)S(1)}, u32[]{:S(2)}, u32[]{:S(2)}) collective-permute-start(bf16[256,256]{1,0:T(8,128)(2,1)S(1)} %get-tuple-element.31), channel_id=1, source_target_pairs={{4,0},{8,4},{12,8},{16,12},{20,16},{24,20},{28,24},{32,28},{36,32}... | collective-permute-start | bytes 393224 | tf_op jit(solution)/shard_map/ppermute | solution.py:29
  94.7 5.0 %collective-permute-done.13 = bf16[256,256]{1,0:T(8,128)(2,1)S(1)} collective-permute-done((bf16[256,256]{1,0:T(8,128)(2,1)S(1)}, bf16[256,256]{1,0:T(8,128)(2,1)S(1)}, u32[]{:S(2)}, u32[]{:S(2)}) %collective-permute-start.13) | collective-permute-done | bytes 131104 | tf_op jit(solution)/shard_map/ppermute | solution.py:29
  101.2 2.3 %collective-permute-done.15 = bf16[256,256]{1,0:T(8,128)(2,1)S(1)} collective-permute-done((bf16[256,256]{1,0:T(8,128)(2,1)S(1)}, bf16[256,256]{1,0:T(8,128)(2,1)S(1)}, u32[]{:S(2)}, u32[]{:S(2)}) %collective-permute-start.15) | collective-permute-done | bytes 131104 | tf_op jit(solution)/shard_map/ppermute | solution.py:29
  103.6 4.5 %all-to-all-start.1 = ((bf16[4,64,1024]{2,1,0:T(8,128)(2,1)}), bf16[4,64,1024]{2,1,0:T(8,128)(2,1)S(1)}, u32[]{:S(2)}, u32[]{:S(2)}) async-start(bf16[4,64,1024]{2,1,0:T(8,128)(2,1)} %bitcast.3), calls=%async_computation.1 | async-start | bytes 1048576 | tf_op jit(solution)/shard_map/all_to_all | solution.py:171
  109.5 8.6 %all-to-all-done.1 = bf16[4,64,1024]{2,1,0:T(8,128)(2,1)S(1)} async-done(((bf16[4,64,1024]{2,1,0:T(8,128)(2,1)}), bf16[4,64,1024]{2,1,0:T(8,128)(2,1)S(1)}, u32[]{:S(2)}, u32[]{:S(2)}) %all-to-all-start.1) | async-done | bytes 524320 | tf_op jit(solution)/shard_map/all_to_all | solution.py:171
  120.3 1.6 %reshape.23 = bf16[64,8192]{1,0:T(8,128)(2,1)} reshape(bf16[64,4,2,1024]{3,2,1,0:T(2,128)(2,1)S(1)} %copy.10) | data formatting | bytes 2097152 | tf_op jit(solution)/shard_map/reshape | solution.py:176
  (42 shorter events, 10.1 us)
Async XLA Ops:
  1.6 20.4 %collective-permute-start.3 = (bf16[256,256]{1,0:T(8,128)(2,1)S(1)}, bf16[256,256]{1,0:T(8,128)(2,1)S(1)}, u32[]{:S(2)}, u32[]{:S(2)}) collective-permute-start(bf16[256,256]{1,0:T(8,128)(2,1)S(1)} %pad_maximum_fusion), channel_id=1, source_target_pairs={{0,4},{4,8},{8,12},{12,16},{16,20},{20,24},{24,28},{28,32},{32,36}... | collective-permute-start | bytes 393224 | tf_op jit(solution)/shard_map/ppermute | solution.py:29
  5.7 18.9 %collective-permute-start.2 = (bf16[256,256]{1,0:T(8,128)(2,1)S(1)}, bf16[256,256]{1,0:T(8,128)(2,1)S(1)}, u32[]{:S(2)}, u32[]{:S(2)}) collective-permute-start(bf16[256,256]{1,0:T(8,128)(2,1)S(1)} %pad_maximum_fusion), channel_id=1, source_target_pairs={{0,8},{4,12},{8,16},{12,20},{16,24},{20,28},{24,32},{28,36},{32,40... | collective-permute-start | bytes 393224 | tf_op jit(solution)/shard_map/ppermute | solution.py:29
  9.3 17.3 %collective-permute-start.1 = (bf16[256,256]{1,0:T(8,128)(2,1)S(1)}, bf16[256,256]{1,0:T(8,128)(2,1)S(1)}, u32[]{:S(2)}, u32[]{:S(2)}) collective-permute-start(bf16[256,256]{1,0:T(8,128)(2,1)S(1)} %pad_maximum_fusion), channel_id=1, source_target_pairs={{0,12},{4,16},{8,20},{12,24},{16,28},{20,32},{24,36},{28,40},{32,4... | collective-permute-start | bytes 393224 | tf_op jit(solution)/shard_map/ppermute | solution.py:29
  12.8 16.7 %collective-permute-start = (bf16[256,256]{1,0:T(8,128)(2,1)S(1)}, bf16[256,256]{1,0:T(8,128)(2,1)S(1)}, u32[]{:S(2)}, u32[]{:S(2)}) collective-permute-start(bf16[256,256]{1,0:T(8,128)(2,1)S(1)} %pad_maximum_fusion), channel_id=1, source_target_pairs={{0,16},{4,20},{8,24},{12,28},{16,32},{20,36},{24,40},{28,44},{32,4... | collective-permute-start | bytes 393224 | tf_op jit(solution)/shard_map/ppermute | solution.py:29
  18.1 11.5 %copy-start = (bf16[256,256]{1,0:T(8,128)(2,1)S(1)}, bf16[256,256]{1,0:T(8,128)(2,1)}, u32[]{:S(2)}) copy-start(bf16[256,256]{1,0:T(8,128)(2,1)} %refs_6_.3) | copy-start | bytes 393220
  18.1 11.5 %copy-start.1 = (bf16[256,256]{1,0:T(8,128)(2,1)S(1)}, bf16[256,256]{1,0:T(8,128)(2,1)}, u32[]{:S(2)}) copy-start(bf16[256,256]{1,0:T(8,128)(2,1)} %refs_7_.3) | copy-start | bytes 393220
  18.8 39.5 %collective-permute-start.7 = (bf16[256,256]{1,0:T(8,128)(2,1)}, bf16[256,256]{1,0:T(8,128)(2,1)S(1)}, u32[]{:S(2)}, u32[]{:S(2)}) collective-permute-start(bf16[256,256]{1,0:T(8,128)(2,1)} %pad_maximum_fusion.1), channel_id=1, source_target_pairs={{0,4},{4,8},{8,12},{12,16},{16,20},{20,24},{24,28},{28,32},{32,36}... | collective-permute-start | bytes 393224 | tf_op jit(solution)/shard_map/ppermute | solution.py:29
  22.0 7.6 %copy-start.7 = (s32[32]{0:T(128)S(1)}, s32[32]{0:T(128)}, u32[]{:S(2)}) copy-start(s32[32]{0:T(128)} %lens.3) | copy-start | bytes 388
  22.0 40.8 %collective-permute-start.6 = (bf16[256,256]{1,0:T(8,128)(2,1)}, bf16[256,256]{1,0:T(8,128)(2,1)S(1)}, u32[]{:S(2)}, u32[]{:S(2)}) collective-permute-start(bf16[256,256]{1,0:T(8,128)(2,1)} %pad_maximum_fusion.1), channel_id=1, source_target_pairs={{0,8},{4,12},{8,16},{12,20},{16,24},{20,28},{24,32},{28,36},{32,40... | collective-permute-start | bytes 393224 | tf_op jit(solution)/shard_map/ppermute | solution.py:29
  24.6 40.7 %collective-permute-start.5 = (bf16[256,256]{1,0:T(8,128)(2,1)}, bf16[256,256]{1,0:T(8,128)(2,1)S(1)}, u32[]{:S(2)}, u32[]{:S(2)}) collective-permute-start(bf16[256,256]{1,0:T(8,128)(2,1)} %pad_maximum_fusion.1), channel_id=1, source_target_pairs={{0,12},{4,16},{8,20},{12,24},{16,28},{20,32},{24,36},{28,40},{32,4... | collective-permute-start | bytes 393224 | tf_op jit(solution)/shard_map/ppermute | solution.py:29
  26.6 42.1 %collective-permute-start.4 = (bf16[256,256]{1,0:T(8,128)(2,1)}, bf16[256,256]{1,0:T(8,128)(2,1)S(1)}, u32[]{:S(2)}, u32[]{:S(2)}) collective-permute-start(bf16[256,256]{1,0:T(8,128)(2,1)} %pad_maximum_fusion.1), channel_id=1, source_target_pairs={{0,16},{4,20},{8,24},{12,28},{16,32},{20,36},{24,40},{28,44},{32,4... | collective-permute-start | bytes 393224 | tf_op jit(solution)/shard_map/ppermute | solution.py:29
  29.6 1.2 %copy-start.2 = (bf16[256,2048]{1,0:T(8,128)(2,1)S(1)}, bf16[256,2048]{1,0:T(8,128)(2,1)}, u32[]{:S(2)}) copy-start(bf16[256,2048]{1,0:T(8,128)(2,1)} %refs_0_.3) | copy-start | bytes 3145732
  32.0 36.7 %copy-start.5 = (bf16[256,2048]{1,0:T(8,128)(2,1)S(1)}, bf16[256,2048]{1,0:T(8,128)(2,1)}, u32[]{:S(2)}) copy-start(bf16[256,2048]{1,0:T(8,128)(2,1)} %refs_1_.3) | copy-start | bytes 3145732
  48.5 20.2 %copy-start.3 = (bf16[256,2048]{1,0:T(8,128)(2,1)S(1)}, bf16[256,2048]{1,0:T(8,128)(2,1)}, u32[]{:S(2)}) copy-start(bf16[256,2048]{1,0:T(8,128)(2,1)} %refs_0_.3) | copy-start | bytes 3145732
  48.6 55.0 %all-to-all-start = ((bf16[4,64,1024]{2,1,0:T(8,128)(2,1)}), bf16[4,64,1024]{2,1,0:T(8,128)(2,1)}, u32[]{:S(2)}, u32[]{:S(2)}) async-start(bf16[4,64,1024]{2,1,0:T(8,128)(2,1)} %bitcast.1), calls=%async_computation | async-start | bytes 1048576 | tf_op jit(solution)/shard_map/all_to_all | solution.py:171
  52.9 34.9 %collective-permute-start.8 = (bf16[256,256]{1,0:T(8,128)(2,1)}, bf16[256,256]{1,0:T(8,128)(2,1)S(1)}, u32[]{:S(2)}, u32[]{:S(2)}) collective-permute-start(bf16[256,256]{1,0:T(8,128)(2,1)} %copy-done.6), channel_id=1, source_target_pairs={{16,0},{20,4},{24,8},{28,12},{32,16},{36,20},{40,24},{44,28},{48,3... | collective-permute-start | bytes 393224 | tf_op jit(solution)/shard_map/ppermute | solution.py:29
  58.2 32.0 %collective-permute-start.9 = (bf16[256,256]{1,0:T(8,128)(2,1)S(1)}, bf16[256,256]{1,0:T(8,128)(2,1)S(1)}, u32[]{:S(2)}, u32[]{:S(2)}) collective-permute-start(bf16[256,256]{1,0:T(8,128)(2,1)S(1)} %get-tuple-element.24), channel_id=1, source_target_pairs={{12,0},{16,4},{20,8},{24,12},{28,16},{32,20},{36,24},{40,28},{44,3... | collective-permute-start | bytes 393224 | tf_op jit(solution)/shard_map/ppermute | solution.py:29
  62.7 29.4 %collective-permute-start.10 = (bf16[256,256]{1,0:T(8,128)(2,1)S(1)}, bf16[256,256]{1,0:T(8,128)(2,1)S(1)}, u32[]{:S(2)}, u32[]{:S(2)}) collective-permute-start(bf16[256,256]{1,0:T(8,128)(2,1)S(1)} %get-tuple-element.25), channel_id=1, source_target_pairs={{8,0},{12,4},{16,8},{20,12},{24,16},{28,20},{32,24},{36,28},{40,32... | collective-permute-start | bytes 393224 | tf_op jit(solution)/shard_map/ppermute | solution.py:29
  65.4 29.2 %collective-permute-start.11 = (bf16[256,256]{1,0:T(8,128)(2,1)S(1)}, bf16[256,256]{1,0:T(8,128)(2,1)S(1)}, u32[]{:S(2)}, u32[]{:S(2)}) collective-permute-start(bf16[256,256]{1,0:T(8,128)(2,1)S(1)} %get-tuple-element.26), channel_id=1, source_target_pairs={{4,0},{8,4},{12,8},{16,12},{20,16},{24,20},{28,24},{32,28},{36,32}... | collective-permute-start | bytes 393224 | tf_op jit(solution)/shard_map/ppermute | solution.py:29
  84.7 10.1 %collective-permute-start.12 = (bf16[256,256]{1,0:T(8,128)(2,1)S(1)}, bf16[256,256]{1,0:T(8,128)(2,1)S(1)}, u32[]{:S(2)}, u32[]{:S(2)}) collective-permute-start(bf16[256,256]{1,0:T(8,128)(2,1)S(1)} %get-tuple-element.28), channel_id=1, source_target_pairs={{16,0},{20,4},{24,8},{28,12},{32,16},{36,20},{40,24},{44,28},{48,3... | collective-permute-start | bytes 393224 | tf_op jit(solution)/shard_map/ppermute | solution.py:29
  87.8 12.0 %collective-permute-start.13 = (bf16[256,256]{1,0:T(8,128)(2,1)S(1)}, bf16[256,256]{1,0:T(8,128)(2,1)S(1)}, u32[]{:S(2)}, u32[]{:S(2)}) collective-permute-start(bf16[256,256]{1,0:T(8,128)(2,1)S(1)} %get-tuple-element.29), channel_id=1, source_target_pairs={{12,0},{16,4},{20,8},{24,12},{28,16},{32,20},{36,24},{40,28},{44,3... | collective-permute-start | bytes 393224 | tf_op jit(solution)/shard_map/ppermute | solution.py:29
  90.3 10.9 %collective-permute-start.14 = (bf16[256,256]{1,0:T(8,128)(2,1)S(1)}, bf16[256,256]{1,0:T(8,128)(2,1)S(1)}, u32[]{:S(2)}, u32[]{:S(2)}) collective-permute-start(bf16[256,256]{1,0:T(8,128)(2,1)S(1)} %get-tuple-element.30), channel_id=1, source_target_pairs={{8,0},{12,4},{16,8},{20,12},{24,16},{28,20},{32,24},{36,28},{40,32... | collective-permute-start | bytes 393224 | tf_op jit(solution)/shard_map/ppermute | solution.py:29
  92.2 11.3 %collective-permute-start.15 = (bf16[256,256]{1,0:T(8,128)(2,1)S(1)}, bf16[256,256]{1,0:T(8,128)(2,1)S(1)}, u32[]{:S(2)}, u32[]{:S(2)}) collective-permute-start(bf16[256,256]{1,0:T(8,128)(2,1)S(1)} %get-tuple-element.31), channel_id=1, source_target_pairs={{4,0},{8,4},{12,8},{16,12},{20,16},{24,20},{28,24},{32,28},{36,32}... | collective-permute-start | bytes 393224 | tf_op jit(solution)/shard_map/ppermute | solution.py:29
  103.6 14.5 %all-to-all-start.1 = ((bf16[4,64,1024]{2,1,0:T(8,128)(2,1)}), bf16[4,64,1024]{2,1,0:T(8,128)(2,1)S(1)}, u32[]{:S(2)}, u32[]{:S(2)}) async-start(bf16[4,64,1024]{2,1,0:T(8,128)(2,1)} %bitcast.3), calls=%async_computation.1 | async-start | bytes 1048576 | tf_op jit(solution)/shard_map/all_to_all | solution.py:171
  (2 other events, 1.9 us)

commit v2 on v1

v2 whole, which is shorter than its diff:
```python
import functools
import math

import jax
import jax.numpy as jnp
from jax import lax
from jax.experimental import pallas as pl
from jax.experimental.pallas import tpu as pltpu
from jax.sharding import PartitionSpec as P

HEAD_WIDTH = 128
REACH = 4
NEG = -1e30
LOG2E = 1.4426950408889634


def dot(a, b):
    return lax.dot_general(a, b, (((1,), (0,)), ((), ())), preferred_element_type=jnp.float32)


def dot_t(a, b):
    return lax.dot_general(a, b, (((1,), (1,)), ((), ())), preferred_element_type=jnp.float32)


def moved(value, to):
    count = lax.axis_size("seq")
    return lax.ppermute(value, "seq", [(source, to(source) % count) for source in range(count)])


def up(value, steps):
    return moved(value, lambda source: source + steps)


def swapped(value):
    return moved(value, lambda source: source ^ 1)


def mask_kernel(lens, here, bias):
    rows, width = bias.shape[0], HEAD_WIDTH
    base = here[0] * rows
    row = lax.broadcasted_iota(jnp.int32, (rows, width), 0)
    col = lax.broadcasted_iota(jnp.int32, (rows, width), 1)

    def one(i, carry):
        end, start = carry
        end = end + lens[i]
        return end, jnp.where(row >= end - base, end - base, start)

    _, start = lax.fori_loop(
        0, lens.shape[0], one, (jnp.int32(0), jnp.full((rows, width), -base, jnp.int32))
    )
    for t in range(bias.shape[1] // width):
        pos = col + (t * width - REACH * rows)
        bias[:, t * width : (t + 1) * width] = jnp.where(
            (pos >= start) & (pos <= row), 0.0, NEG
        ).astype(jnp.float32)


def mask(lengths, here, rows):
    return pl.pallas_call(
        mask_kernel,
        in_specs=[pl.BlockSpec(memory_space=pltpu.SMEM)] * 2,
        out_specs=pl.BlockSpec(memory_space=pltpu.VMEM),
        out_shape=jax.ShapeDtypeStruct((rows, (REACH + 1) * rows), jnp.float32),
        cost_estimate=pl.CostEstimate(flops=1 << 20, bytes_accessed=1 << 20, transcendentals=0),
        name="mask",
    )(lengths, here)


def attention_kernel(scale, *refs):
    q_ref, g_ref, two_ref, four_ref, odd_ref, k_ref, v_ref, bias_ref = refs[0:8]
    o_ref, dq_ref, two_out, four_out, odd_out, own_out, k_all, v_all = refs[-8:]
    rows, width = k_ref.shape
    far = ((four_ref, 0), (odd_ref, 1), (two_ref, 0), (odd_ref, 0))
    for b, (ref, place) in enumerate(far):
        at = slice(b * rows, (b + 1) * rows)
        k_all[at, :] = ref[:, 2 * place * width : (2 * place + 1) * width]
        v_all[at, :] = ref[:, (2 * place + 1) * width : (2 * place + 2) * width]
    k_all[REACH * rows :, :] = k_ref[...]
    v_all[REACH * rows :, :] = v_ref[...]
    k, v, bias = k_all[...], v_all[...], bias_ref[...]
    dk = dv = None
    for h in range(q_ref.shape[1] // width):
        at = slice(h * width, (h + 1) * width)
        q, g = q_ref[:, at], g_ref[:, at]
        s = dot_t(q, k) + bias
        p = jnp.exp2((s - s.max(axis=1, keepdims=True)) * (scale * LOG2E))
        inverse = 1.0 / p.sum(axis=1, keepdims=True)
        pb = p.astype(jnp.bfloat16)
        o = dot(pb, v) * inverse
        o_ref[:, at] = o.astype(jnp.bfloat16)
        gs = (g.astype(jnp.float32) * inverse).astype(jnp.bfloat16)
        delta = jnp.sum(gs.astype(jnp.float32) * o, axis=1, keepdims=True)
        ds = (p * (dot_t(gs, v) - delta)).astype(jnp.bfloat16)
        dq_ref[:, at] = (dot(ds, k) * scale).astype(jnp.bfloat16)
        dk_part, dv_part = dot(q.T, ds), dot(gs.T, pb)
        dk, dv = (dk_part, dv_part) if dk is None else (dk + dk_part, dv + dv_part)
    parts = ((four_out, 0), (odd_out, 1), (two_out, 0), (odd_out, 0), (own_out, 0))
    for b, (ref, place) in enumerate(parts):
        at = slice(b * rows, (b + 1) * rows)
        for which, grad in enumerate((dk[:, at].T * scale, dv[:, at].T)):
            to = slice((2 * place + which) * width, (2 * place + which + 1) * width)
            ref[:, to] = grad.astype(ref.dtype)


def attention(group, q, g, keys, values, far, bias, before):
    rows, width = q.shape[0], HEAD_WIDTH
    groups = keys.shape[1] // width
    per_group = q.shape[1] // width // groups
    heads = pl.BlockSpec((rows, per_group * width), lambda i: (0, group))
    own = pl.BlockSpec((rows, width), lambda i: (0, group))
    one = pl.BlockSpec((rows, 2 * width), lambda i: (0, 0))
    pair = pl.BlockSpec((rows, 4 * width), lambda i: (0, 0))
    flops = 6 * 2 * rows * (REACH + 1) * rows * width * per_group
    return pl.pallas_call(
        functools.partial(attention_kernel, 1.0 / math.sqrt(width)),
        grid=(1,),
        in_specs=[heads, heads, one, one, pair, own, own, pl.BlockSpec(bias.shape, lambda i: (0, 0))]
        + [pl.BlockSpec(memory_space=pl.ANY)] * len(before),
        out_specs=[heads, heads, one, one, pair, one],
        scratch_shapes=[pltpu.VMEM(((REACH + 1) * rows, width), jnp.bfloat16)] * 2,
        out_shape=[
            jax.ShapeDtypeStruct(q.shape, jnp.bfloat16),
            jax.ShapeDtypeStruct(q.shape, jnp.bfloat16),
            jax.ShapeDtypeStruct((rows, 2 * width), jnp.float32),
            jax.ShapeDtypeStruct((rows, 2 * width), jnp.float32),
            jax.ShapeDtypeStruct((rows, 4 * width), jnp.bfloat16),
            jax.ShapeDtypeStruct((rows, 2 * width), jnp.float32),
        ],
        input_output_aliases={8 + i: i for i in range(len(before))},
        compiler_params=pltpu.CompilerParams(vmem_limit_bytes=40 << 20),
        cost_estimate=pl.CostEstimate(flops=flops, bytes_accessed=4 << 20, transcendentals=0),
        name="attention",
    )(q, g, *far, keys, values, bias, *before)


def on_device(queries, keys, values, output_gradient, lengths):
    rows = queries.shape[0]
    width = HEAD_WIDTH
    groups = keys.shape[1] // width
    place = lax.axis_index("seq")
    even = place % 2 == 0
    packs, twos, fours, fars = [], [], [], []
    for g in range(groups):
        at = slice(g * width, (g + 1) * width)
        packs.append(jnp.concatenate((keys[:, at], values[:, at]), axis=1))
    for pack in packs:
        twos.append(up(pack, 2))
        fours.append(up(pack, 4))
    bias = mask(lengths, place.reshape(1).astype(jnp.int32), rows)
    for pack, two, four in zip(packs, twos, fours):
        near = jnp.where(even, pack, two)
        far = jnp.where(even, two, four)
        fars.append((two, four, swapped(jnp.concatenate((near, far), axis=1))))
    before = ()
    sums = []
    for g in range(groups):
        out, d_queries, two, four, odd, own = attention(
            g, queries, output_gradient, keys, values, fars[g], bias, before
        )
        before = (out, d_queries)
        other = swapped(odd).astype(jnp.float32)
        one, three = other[:, : 2 * width], other[:, 2 * width :]
        two = (two + jnp.where(even, three, one)).astype(jnp.bfloat16)
        four = (four + jnp.where(even, 0.0, three)).astype(jnp.bfloat16)
        own = own + jnp.where(even, one, 0.0)
        sums.append(own + up(two, -2).astype(jnp.float32) + up(four, -4).astype(jnp.float32))
    split = lax.axis_size("head")
    got = lax.all_to_all(
        out.reshape(split, rows // split, out.shape[1]), "head", split_axis=0, concat_axis=0
    )
    attn_out = jnp.transpose(got, (1, 0, 2)).reshape(got.shape[1], -1)
    key_gradient = jnp.concatenate([s[:, :width] for s in sums], axis=1).astype(jnp.bfloat16)
    value_gradient = jnp.concatenate([s[:, width:] for s in sums], axis=1).astype(jnp.bfloat16)
    return (attn_out, d_queries, key_gradient, value_gradient)


def solution(mesh):
    placed = (P("seq", "head"), P("seq", "head"), P("seq", "head"), P("seq", "head"), P())
    return jax.shard_map(
        on_device,
        mesh=mesh,
        in_specs=placed,
        out_specs=(P(("seq", "head"), None), P("seq", "head"), P("seq", "head"), P("seq", "head")),
        check_vma=False,
    )
```

time: 123 us -> 79.7 us (0.65)
  the two profiles are of different devices: /device:TPU:3 before, /device:TPU:1 now
where the time goes in v2:
time: 79.7 us; the launch traced here: 79.4 us
  starting transfers between devices  25.9 us (32%)
  Pallas kernels  23.8 us (30%)
  waiting for transfers between devices  22.8 us (29%)
  local copies, waits for them, and re-layouts  3.25 us (4%)
  other arithmetic  2.87 us (4%)
    ppermute x12, waiting for transfers between devices, moved(): lax.ppermute(value, 'seq', [(source, to(source) % count) for source in ra...  22.8 us
    ppermute x12, starting transfers between devices, moved(): lax.ppermute(value, 'seq', [(source, to(source) % count) for source in ra...  21.7 us
    pallas_call x2, Pallas kernels, attention(): pl.pallas_call(functools.partial(attention_kernel, 1.0 / math.sqrt(width)...  20.9 us
    all_to_all x1, starting transfers between devices, on_device(): lax.all_to_all(out.reshape(split, rows // split, out.shape[1]), 'head', s...  4.18 us
    pallas_call x1, Pallas kernels, mask(): pl.pallas_call(mask_kernel, in_specs=[pl.BlockSpec(memory_space=pltpu.SME...  2.91 us
  transfers between devices with their start and end apart: 13, of which 6 were waited for; matrix products, arithmetic and copies ran while one was open for 4% of the time, Pallas kernels for 30%

profile of v2, /device:TPU:1, one launch (start us, length us, event | category | flops | bytes accessed | tf_op | source)
XLA Modules:
  0.0 79.4 jit_solution(12903295793220042815)
XLA Ops:
  0.6 1.0 %fusion.2 = (bf16[256,128]{1,0:T(8,128)(2,1)S(1)}, bf16[256,128]{1,0:T(8,128)(2,1)S(1)}, bf16[256,128]{1,0:T(8,128)(2,1)S(1)}, bf16[256,128]{1,0:T(8,128)(2,1)S(1)}) fusion(bf16[256,256]{1,0:T(8,128)(2,1)} %refs_5_.3, bf16[256,256]{1,0:T(8,128)(2,1)} %refs_6_.3), kind=kLoop, calls=%fused_computation.18 | loop fusion | bytes 524288 | tf_op jit(solution)/shard_map/slice | solution.py:146
  1.6 2.5 %collective-permute-start.3 = (bf16[256,256]{1,0:T(8,128)(2,1)S(1)}, bf16[256,256]{1,0:T(8,128)(2,1)S(1)}, u32[]{:S(2)}, u32[]{:S(2)}) collective-permute-start(bf16[256,256]{1,0:T(8,128)(2,1)S(1)} %pad_maximum_fusion.3), channel_id=1, source_target_pairs={{0,8},{4,12},{8,16},{12,20},{16,24},{20,28},{24,32},{28,36},{32,40... | collective-permute-start | bytes 393224 | tf_op jit(solution)/shard_map/ppermute | solution.py:27
  4.2 3.0 %collective-permute-start.4 = (bf16[256,256]{1,0:T(8,128)(2,1)S(1)}, bf16[256,256]{1,0:T(8,128)(2,1)S(1)}, u32[]{:S(2)}, u32[]{:S(2)}) collective-permute-start(bf16[256,256]{1,0:T(8,128)(2,1)S(1)} %pad_maximum_fusion.3), channel_id=1, source_target_pairs={{0,16},{4,20},{8,24},{12,28},{16,32},{20,36},{24,40},{28,44},{32,4... | collective-permute-start | bytes 393224 | tf_op jit(solution)/shard_map/ppermute | solution.py:27
  7.2 2.9 %collective-permute-start = (bf16[256,256]{1,0:T(8,128)(2,1)S(1)}, bf16[256,256]{1,0:T(8,128)(2,1)S(1)}, u32[]{:S(2)}, u32[]{:S(2)}) collective-permute-start(bf16[256,256]{1,0:T(8,128)(2,1)S(1)} %pad_maximum_fusion.2), channel_id=1, source_target_pairs={{0,8},{4,12},{8,16},{12,20},{16,24},{20,28},{24,32},{28,36},{32,40... | collective-permute-start | bytes 393224 | tf_op jit(solution)/shard_map/ppermute | solution.py:27
  10.1 1.2 %collective-permute-start.1 = (bf16[256,256]{1,0:T(8,128)(2,1)S(1)}, bf16[256,256]{1,0:T(8,128)(2,1)S(1)}, u32[]{:S(2)}, u32[]{:S(2)}) collective-permute-start(bf16[256,256]{1,0:T(8,128)(2,1)S(1)} %pad_maximum_fusion.2), channel_id=1, source_target_pairs={{0,16},{4,20},{8,24},{12,28},{16,32},{20,36},{24,40},{28,44},{32,4... | collective-permute-start | bytes 393224 | tf_op jit(solution)/shard_map/ppermute | solution.py:27
  11.3 2.9 %mask.1.refs_7_ = f32[256,1280]{1,0:T(8,128)} custom-call(s32[32]{0:T(128)} %lens.1, s32[1]{0:T(128)} %bitcast.here), custom_call_target="tpu_custom_call" | custom-call | flops 1048576 | bytes 1048576 | tf_op jit(solution)/shard_map/mask/pallas_call | solution.py:60
  14.2 3.8 %collective-permute-done.4.refs_3_ = bf16[256,256]{1,0:T(8,128)(2,1)S(1)} collective-permute-done((bf16[256,256]{1,0:T(8,128)(2,1)S(1)}, bf16[256,256]{1,0:T(8,128)(2,1)S(1)}, u32[]{:S(2)}, u32[]{:S(2)}) %collective-permute-start.4) | collective-permute-done | bytes 131104 | tf_op jit(solution)/shard_map/ppermute | solution.py:27
  18.1 4.4 %collective-permute-start.5 = (bf16[256,512]{1,0:T(8,128)(2,1)S(1)}, bf16[256,512]{1,0:T(8,128)(2,1)S(1)}, u32[]{:S(2)}, u32[]{:S(2)}) collective-permute-start(bf16[256,512]{1,0:T(8,128)(2,1)S(1)} %pad_maximum_fusion.1), channel_id=1, source_target_pairs={{0,4},{4,0},{8,12},{12,8},{16,20},{20,16},{24,28},{28,24},{32,36},... | collective-permute-start | bytes 786440 | tf_op jit(solution)/shard_map/ppermute | solution.py:27
  22.6 3.9 %collective-permute-done.1.refs_3_ = bf16[256,256]{1,0:T(8,128)(2,1)S(1)} collective-permute-done((bf16[256,256]{1,0:T(8,128)(2,1)S(1)}, bf16[256,256]{1,0:T(8,128)(2,1)S(1)}, u32[]{:S(2)}, u32[]{:S(2)}) %collective-permute-start.1) | collective-permute-done | bytes 131104 | tf_op jit(solution)/shard_map/ppermute | solution.py:27
  26.5 1.9 %collective-permute-start.2 = (bf16[256,512]{1,0:T(8,128)(2,1)S(1)}, bf16[256,512]{1,0:T(8,128)(2,1)S(1)}, u32[]{:S(2)}, u32[]{:S(2)}) collective-permute-start(bf16[256,512]{1,0:T(8,128)(2,1)S(1)} %pad_maximum_fusion), channel_id=1, source_target_pairs={{0,4},{4,0},{8,12},{12,8},{16,20},{20,16},{24,28},{28,24},{32,36},... | collective-permute-start | bytes 786440 | tf_op jit(solution)/shard_map/ppermute | solution.py:27
  28.5 1.2 %copy-done.4 = bf16[256,2048]{1,0:T(8,128)(2,1)S(1)} copy-done((bf16[256,2048]{1,0:T(8,128)(2,1)S(1)}, bf16[256,2048]{1,0:T(8,128)(2,1)}, u32[]{:S(2)}) %copy-start.4) | copy-done | bytes 1048600
  29.7 10.5 %attention.2 = (bf16[256,2048]{1,0:T(8,128)(2,1)}, bf16[256,2048]{1,0:T(8,128)(2,1)}, f32[256,256]{1,0:T(8,128)S(1)}, f32[256,256]{1,0:T(8,128)S(1)}, bf16[256,5...) custom-call(bf16[256,2048]{1,0:T(8,128)(2,1)S(1)} %copy-done.3, bf16[256,2048]{1,0:T(8,128)(2,1)S(1)} %copy-done.4, ...), custom_call_target="tpu_custom_call" | custom-call | flops 4026531840 | bytes 4194304 | tf_op jit(solution)/shard_map/attention/pallas_call | solution.py:115
  40.3 10.4 %attention.3 = (bf16[256,2048]{1,0:T(8,128)(2,1)}, bf16[256,2048]{1,0:T(8,128)(2,1)}, f32[256,256]{1,0:T(8,128)S(1)}, f32[256,256]{1,0:T(8,128)S(1)}, bf16[256,5...) custom-call(bf16[256,2048]{1,0:T(8,128)(2,1)S(1)} %copy-done.3, ...), custom_call_target="tpu_custom_call", output_to_operand_aliasing={{0}: (8, {}), {1}: (9, {})} | custom-call | flops 4026531840 | bytes 4194304 | tf_op jit(solution)/shard_map/attention/pallas_call | solution.py:115
  50.6 0.5 collective-permute-start.9
  51.1 4.2 %all-to-all-start = ((bf16[4,64,2048]{2,1,0:T(8,128)(2,1)}), bf16[4,64,2048]{2,1,0:T(8,128)(2,1)S(1)}, u32[]{:S(2)}, u32[]{:S(2)}) async-start(bf16[4,64,2048]{2,1,0:T(8,128)(2,1)} %bitcast.1), calls=%async_computation | async-start | bytes 2097152 | tf_op jit(solution)/shard_map/all_to_all | solution.py:169
  55.3 1.0 %convert_element_type.32 = f32[256,512]{1,0:T(8,128)S(1)} convert(bf16[256,512]{1,0:T(8,128)(2,1)} %collective-permute-done.6) | non-fusion elementwise | flops 131072 | bytes 786432 | tf_op jit(solution)/shard_map/convert_element_type | solution.py:162
  56.4 2.7 %collective-permute-start.7 = (bf16[256,256]{1,0:T(8,128)(2,1)S(1)}, bf16[256,256]{1,0:T(8,128)(2,1)S(1)}, u32[]{:S(2)}, u32[]{:S(2)}) collective-permute-start(bf16[256,256]{1,0:T(8,128)(2,1)S(1)} %get-tuple-element.28), channel_id=1, source_target_pairs={{0,248},{4,252},{8,0},{12,4},{16,8},{20,12},{24,16},{28,20},{32,24... | collective-permute-start | bytes 393224 | tf_op jit(solution)/shard_map/ppermute | solution.py:27
  59.1 2.4 %collective-permute-start.8 = (bf16[256,256]{1,0:T(8,128)(2,1)S(1)}, bf16[256,256]{1,0:T(8,128)(2,1)S(1)}, u32[]{:S(2)}, u32[]{:S(2)}) collective-permute-start(bf16[256,256]{1,0:T(8,128)(2,1)S(1)} %get-tuple-element.29), channel_id=1, source_target_pairs={{0,240},{4,244},{8,248},{12,252},{16,0},{20,4},{24,8},{28,12},{32,... | collective-permute-start | bytes 393224 | tf_op jit(solution)/shard_map/ppermute | solution.py:27
  62.0 6.5 %collective-permute-done.8 = bf16[256,256]{1,0:T(8,128)(2,1)S(1)} collective-permute-done((bf16[256,256]{1,0:T(8,128)(2,1)S(1)}, bf16[256,256]{1,0:T(8,128)(2,1)S(1)}, u32[]{:S(2)}, u32[]{:S(2)}) %collective-permute-start.8) | collective-permute-done | bytes 131104 | tf_op jit(solution)/shard_map/ppermute | solution.py:27
  68.6 1.8 %collective-permute-done.10 = bf16[256,256]{1,0:T(8,128)(2,1)S(1)} collective-permute-done((bf16[256,256]{1,0:T(8,128)(2,1)S(1)}, bf16[256,256]{1,0:T(8,128)(2,1)S(1)}, u32[]{:S(2)}, u32[]{:S(2)}) %collective-permute-start.10) | collective-permute-done | bytes 131104 | tf_op jit(solution)/shard_map/ppermute | solution.py:27
  70.4 6.5 %collective-permute-done.11 = bf16[256,256]{1,0:T(8,128)(2,1)S(1)} collective-permute-done((bf16[256,256]{1,0:T(8,128)(2,1)S(1)}, bf16[256,256]{1,0:T(8,128)(2,1)S(1)}, u32[]{:S(2)}, u32[]{:S(2)}) %collective-permute-start.11) | collective-permute-done | bytes 131104 | tf_op jit(solution)/shard_map/ppermute | solution.py:27
  77.0 0.7 pad_maximum_fusion.5
  77.7 0.7 pad_maximum_fusion.4
  78.4 1.0 %copy.12 = bf16[4,8,8,2048]{3,2,0,1:T(8,128)(2,1)} copy(bf16[4,8,8,2048]{3,2,1,0:T(8,128)(2,1)S(1)} %bitcast.5) | data formatting | bytes 2097152 | tf_op jit(solution)/shard_map/reshape | solution.py:172
  (33 shorter events, 1.0 us)
Async XLA Ops:
  1.6 12.6 %collective-permute-start.3 = (bf16[256,256]{1,0:T(8,128)(2,1)S(1)}, bf16[256,256]{1,0:T(8,128)(2,1)S(1)}, u32[]{:S(2)}, u32[]{:S(2)}) collective-permute-start(bf16[256,256]{1,0:T(8,128)(2,1)S(1)} %pad_maximum_fusion.3), channel_id=1, source_target_pairs={{0,8},{4,12},{8,16},{12,20},{16,24},{20,28},{24,32},{28,36},{32,40... | collective-permute-start | bytes 393224 | tf_op jit(solution)/shard_map/ppermute | solution.py:27
  4.2 13.9 %collective-permute-start.4 = (bf16[256,256]{1,0:T(8,128)(2,1)S(1)}, bf16[256,256]{1,0:T(8,128)(2,1)S(1)}, u32[]{:S(2)}, u32[]{:S(2)}) collective-permute-start(bf16[256,256]{1,0:T(8,128)(2,1)S(1)} %pad_maximum_fusion.3), channel_id=1, source_target_pairs={{0,16},{4,20},{8,24},{12,28},{16,32},{20,36},{24,40},{28,44},{32,4... | collective-permute-start | bytes 393224 | tf_op jit(solution)/shard_map/ppermute | solution.py:27
  7.2 15.4 %collective-permute-start = (bf16[256,256]{1,0:T(8,128)(2,1)S(1)}, bf16[256,256]{1,0:T(8,128)(2,1)S(1)}, u32[]{:S(2)}, u32[]{:S(2)}) collective-permute-start(bf16[256,256]{1,0:T(8,128)(2,1)S(1)} %pad_maximum_fusion.2), channel_id=1, source_target_pairs={{0,8},{4,12},{8,16},{12,20},{16,24},{20,28},{24,32},{28,36},{32,40... | collective-permute-start | bytes 393224 | tf_op jit(solution)/shard_map/ppermute | solution.py:27
  10.1 16.4 %collective-permute-start.1 = (bf16[256,256]{1,0:T(8,128)(2,1)S(1)}, bf16[256,256]{1,0:T(8,128)(2,1)S(1)}, u32[]{:S(2)}, u32[]{:S(2)}) collective-permute-start(bf16[256,256]{1,0:T(8,128)(2,1)S(1)} %pad_maximum_fusion.2), channel_id=1, source_target_pairs={{0,16},{4,20},{8,24},{12,28},{16,32},{20,36},{24,40},{28,44},{32,4... | collective-permute-start | bytes 393224 | tf_op jit(solution)/shard_map/ppermute | solution.py:27
  11.3 17.1 %copy-start.3 = (bf16[256,2048]{1,0:T(8,128)(2,1)S(1)}, bf16[256,2048]{1,0:T(8,128)(2,1)}, u32[]{:S(2)}) copy-start(bf16[256,2048]{1,0:T(8,128)(2,1)} %refs_0_.3) | copy-start | bytes 3145732
  14.2 14.2 %copy-start = (f32[256,1280]{1,0:T(8,128)S(1)}, f32[256,1280]{1,0:T(8,128)}, u32[]{:S(2)}) copy-start(f32[256,1280]{1,0:T(8,128)} %mask.1.refs_7_) | copy-start | bytes 3932164
  14.2 14.2 %copy-start.1 = (bf16[256,256]{1,0:T(8,128)(2,1)S(1)}, bf16[256,256]{1,0:T(8,128)(2,1)}, u32[]{:S(2)}) copy-start(bf16[256,256]{1,0:T(8,128)(2,1)} %refs_5_.3) | copy-start | bytes 393220
  14.2 14.2 %copy-start.2 = (bf16[256,256]{1,0:T(8,128)(2,1)S(1)}, bf16[256,256]{1,0:T(8,128)(2,1)}, u32[]{:S(2)}) copy-start(bf16[256,256]{1,0:T(8,128)(2,1)} %refs_6_.3) | copy-start | bytes 393220
  18.1 10.3 %collective-permute-start.5 = (bf16[256,512]{1,0:T(8,128)(2,1)S(1)}, bf16[256,512]{1,0:T(8,128)(2,1)S(1)}, u32[]{:S(2)}, u32[]{:S(2)}) collective-permute-start(bf16[256,512]{1,0:T(8,128)(2,1)S(1)} %pad_maximum_fusion.1), channel_id=1, source_target_pairs={{0,4},{4,0},{8,12},{12,8},{16,20},{20,16},{24,28},{28,24},{32,36},... | collective-permute-start | bytes 786440 | tf_op jit(solution)/shard_map/ppermute | solution.py:27
  26.5 13.7 %collective-permute-start.2 = (bf16[256,512]{1,0:T(8,128)(2,1)S(1)}, bf16[256,512]{1,0:T(8,128)(2,1)S(1)}, u32[]{:S(2)}, u32[]{:S(2)}) collective-permute-start(bf16[256,512]{1,0:T(8,128)(2,1)S(1)} %pad_maximum_fusion), channel_id=1, source_target_pairs={{0,4},{4,0},{8,12},{12,8},{16,20},{20,16},{24,28},{28,24},{32,36},... | collective-permute-start | bytes 786440 | tf_op jit(solution)/shard_map/ppermute | solution.py:27
  28.4 1.2 %copy-start.4 = (bf16[256,2048]{1,0:T(8,128)(2,1)S(1)}, bf16[256,2048]{1,0:T(8,128)(2,1)}, u32[]{:S(2)}) copy-start(bf16[256,2048]{1,0:T(8,128)(2,1)} %refs_1_.3) | copy-start | bytes 3145732
  40.2 15.1 %collective-permute-start.6 = (bf16[256,512]{1,0:T(8,128)(2,1)S(1)}, bf16[256,512]{1,0:T(8,128)(2,1)}, u32[]{:S(2)}, u32[]{:S(2)}) collective-permute-start(bf16[256,512]{1,0:T(8,128)(2,1)S(1)} %get-tuple-element.21), channel_id=1, source_target_pairs={{0,4},{4,0},{8,12},{12,8},{16,20},{20,16},{24,28},{28,24},{32,36},... | collective-permute-start | bytes 786440 | tf_op jit(solution)/shard_map/ppermute | solution.py:27
  50.6 10.8 %collective-permute-start.9 = (bf16[256,512]{1,0:T(8,128)(2,1)S(1)}, bf16[256,512]{1,0:T(8,128)(2,1)S(1)}, u32[]{:S(2)}, u32[]{:S(2)}) collective-permute-start(bf16[256,512]{1,0:T(8,128)(2,1)S(1)} %get-tuple-element.25), channel_id=1, source_target_pairs={{0,4},{4,0},{8,12},{12,8},{16,20},{20,16},{24,28},{28,24},{32,36},... | collective-permute-start | bytes 786440 | tf_op jit(solution)/shard_map/ppermute | solution.py:27
  51.1 27.3 %all-to-all-start = ((bf16[4,64,2048]{2,1,0:T(8,128)(2,1)}), bf16[4,64,2048]{2,1,0:T(8,128)(2,1)S(1)}, u32[]{:S(2)}, u32[]{:S(2)}) async-start(bf16[4,64,2048]{2,1,0:T(8,128)(2,1)} %bitcast.1), calls=%async_computation | async-start | bytes 2097152 | tf_op jit(solution)/shard_map/all_to_all | solution.py:169
  56.4 5.6 %collective-permute-start.7 = (bf16[256,256]{1,0:T(8,128)(2,1)S(1)}, bf16[256,256]{1,0:T(8,128)(2,1)S(1)}, u32[]{:S(2)}, u32[]{:S(2)}) collective-permute-start(bf16[256,256]{1,0:T(8,128)(2,1)S(1)} %get-tuple-element.28), channel_id=1, source_target_pairs={{0,248},{4,252},{8,0},{12,4},{16,8},{20,12},{24,16},{28,20},{32,24... | collective-permute-start | bytes 393224 | tf_op jit(solution)/shard_map/ppermute | solution.py:27
  59.1 9.4 %collective-permute-start.8 = (bf16[256,256]{1,0:T(8,128)(2,1)S(1)}, bf16[256,256]{1,0:T(8,128)(2,1)S(1)}, u32[]{:S(2)}, u32[]{:S(2)}) collective-permute-start(bf16[256,256]{1,0:T(8,128)(2,1)S(1)} %get-tuple-element.29), channel_id=1, source_target_pairs={{0,240},{4,244},{8,248},{12,252},{16,0},{20,4},{24,8},{28,12},{32,... | collective-permute-start | bytes 393224 | tf_op jit(solution)/shard_map/ppermute | solution.py:27
  61.6 8.8 %collective-permute-start.10 = (bf16[256,256]{1,0:T(8,128)(2,1)S(1)}, bf16[256,256]{1,0:T(8,128)(2,1)S(1)}, u32[]{:S(2)}, u32[]{:S(2)}) collective-permute-start(bf16[256,256]{1,0:T(8,128)(2,1)S(1)} %get-tuple-element.30), channel_id=1, source_target_pairs={{0,248},{4,252},{8,0},{12,4},{16,8},{20,12},{24,16},{28,20},{32,24... | collective-permute-start | bytes 393224 | tf_op jit(solution)/shard_map/ppermute | solution.py:27
  61.8 15.2 %collective-permute-start.11 = (bf16[256,256]{1,0:T(8,128)(2,1)S(1)}, bf16[256,256]{1,0:T(8,128)(2,1)S(1)}, u32[]{:S(2)}, u32[]{:S(2)}) collective-permute-start(bf16[256,256]{1,0:T(8,128)(2,1)S(1)} %get-tuple-element.31), channel_id=1, source_target_pairs={{0,240},{4,244},{8,248},{12,252},{16,0},{20,4},{24,8},{28,12},{32,... | collective-permute-start | bytes 393224 | tf_op jit(solution)/shard_map/ppermute | solution.py:27

commit v3 on v2

v3 whole, which is shorter than its diff:
```python
import functools
import math

import jax
import jax.numpy as jnp
from jax import lax
from jax.experimental import pallas as pl
from jax.experimental.pallas import tpu as pltpu
from jax.sharding import PartitionSpec as P

HEAD_WIDTH = 128
REACH = 4
NEG = -1e30
LOG2E = 1.4426950408889634


def dot(a, b):
    return lax.dot_general(a, b, (((1,), (0,)), ((), ())), preferred_element_type=jnp.float32)


def dot_t(a, b):
    return lax.dot_general(a, b, (((1,), (1,)), ((), ())), preferred_element_type=jnp.float32)


def moved(value, to):
    count = lax.axis_size("seq")
    return lax.ppermute(value, "seq", [(source, to(source) % count) for source in range(count)])


def up(value, steps):
    return moved(value, lambda source: source + steps)


def swapped(value):
    return moved(value, lambda source: source ^ 1)


def own_forward_kernel(scale, lens, here, q_ref, k_ref, v_ref, out_ref, stat_ref, near_ref, far_ref):
    rows, width = k_ref.shape[0], HEAD_WIDTH
    base = here[0] * rows
    row = lax.broadcasted_iota(jnp.int32, (rows, width), 0)
    col = lax.broadcasted_iota(jnp.int32, (rows, width), 1)

    def one(i, carry):
        end, start = carry
        end = end + lens[i]
        return end, jnp.where(row >= end - base, end - base, start)

    _, start = lax.fori_loop(
        0, lens.shape[0], one, (jnp.int32(0), jnp.full((rows, width), -base, jnp.int32))
    )
    for t in range(REACH * rows // width):
        pos = col + (t * width - REACH * rows)
        far_ref[:, t * width : (t + 1) * width] = jnp.where(pos >= start, 0.0, NEG).astype(jnp.float32)
    for t in range(rows // width):
        pos = col + t * width
        near_ref[:, t * width : (t + 1) * width] = jnp.where(
            (pos >= start) & (pos <= row), 0.0, NEG
        ).astype(jnp.float32)
    near = near_ref[...]
    heads = q_ref.shape[1] // width
    group = heads // (k_ref.shape[1] // width)
    for h in range(heads):
        at = slice(h * width, (h + 1) * width)
        kv = slice(h // group * width, (h // group + 1) * width)
        s = dot_t(q_ref[:, at], k_ref[:, kv]) + near
        top = s.max(axis=1, keepdims=True)
        p = jnp.exp2((s - top) * (scale * LOG2E))
        stat_ref[:, h : h + 1] = top
        stat_ref[:, heads + h : heads + h + 1] = p.sum(axis=1, keepdims=True)
        out_ref[:, at] = dot(p.astype(jnp.bfloat16), v_ref[:, kv])


def far_kernel(scale, *refs):
    q_ref, g_ref, out_ref, stat_ref, bias_ref = refs[0:5]
    o_ref, dq_out, keep_ref, two_out, four_out, odd_out, k_all, v_all, dq_ref, sent = refs[-10:]
    fars = refs[5:-10]
    rows, width = q_ref.shape[0], HEAD_WIDTH
    heads = q_ref.shape[1] // width
    groups = len(fars) // 3
    factor = scale * LOG2E
    bias = bias_ref[...]
    for n in range(groups):
        two_ref, four_ref, odd_ref = fars[3 * n : 3 * n + 3]
        for b, (ref, place) in enumerate(((four_ref, 0), (odd_ref, 1), (two_ref, 0), (odd_ref, 0))):
            at = slice(b * rows, (b + 1) * rows)
            k_all[n, at, :] = ref[:, 2 * place * width : (2 * place + 1) * width]
            v_all[n, at, :] = ref[:, (2 * place + 1) * width : (2 * place + 2) * width]
        k, v = k_all[n], v_all[n]
        dk = dv = None
        for h in range(n * heads // groups, (n + 1) * heads // groups):
            at = slice(h * width, (h + 1) * width)
            q, g = q_ref[:, at], g_ref[:, at]
            top = stat_ref[:, h : h + 1]
            total = stat_ref[:, heads + h : heads + h + 1]
            s = dot_t(q, k) + bias
            most = jnp.maximum(top, s.max(axis=1, keepdims=True))
            p = jnp.exp2((s - most) * factor)
            keep = jnp.exp2((top - most) * factor)
            total = total * keep + p.sum(axis=1, keepdims=True)
            inverse = 1.0 / total
            pb = p.astype(jnp.bfloat16)
            o = (dot(pb, v) + out_ref[:, at] * keep) * inverse
            o_ref[:, at] = o.astype(jnp.bfloat16)
            gs = (g.astype(jnp.float32) * inverse).astype(jnp.bfloat16)
            delta = jnp.sum(gs.astype(jnp.float32) * o, axis=1, keepdims=True)
            keep_ref[:, h : h + 1] = most
            keep_ref[:, heads + h : heads + h + 1] = inverse
            keep_ref[:, 2 * heads + h : 2 * heads + h + 1] = delta
            ds = (p * (dot_t(gs, v) - delta)).astype(jnp.bfloat16)
            dq_ref[:, at] = dot(ds, k)
            pltpu.make_async_copy(dq_ref.at[:, at], dq_out.at[:, at], sent.at[h]).start()
            dk_part, dv_part = dot(q.T, ds), dot(gs.T, pb)
            dk, dv = (dk_part, dv_part) if dk is None else (dk + dk_part, dv + dv_part)
        for b, (ref, place) in enumerate(((four_out, 0), (odd_out, 1), (two_out, 0), (odd_out, 0))):
            at = slice(b * rows, (b + 1) * rows)
            for which, grad in enumerate((dk[:, at].T * scale, dv[:, at].T)):
                to = (2 * groups * place + 2 * n + which) * width
                ref[:, to : to + width] = grad.astype(ref.dtype)
    for h in range(heads):
        at = slice(h * width, (h + 1) * width)
        pltpu.make_async_copy(dq_ref.at[:, at], dq_out.at[:, at], sent.at[h]).wait()


def own_backward_kernel(scale, q_ref, g_ref, k_ref, v_ref, bias_ref, keep_ref, far_ref, dq_ref, own_ref):
    rows, width = q_ref.shape[0], HEAD_WIDTH
    heads = q_ref.shape[1] // width
    groups = k_ref.shape[1] // width
    bias = bias_ref[...]
    for n in range(groups):
        k, v = k_ref[:, n * width : (n + 1) * width], v_ref[:, n * width : (n + 1) * width]
        dk = dv = None
        for h in range(n * heads // groups, (n + 1) * heads // groups):
            at = slice(h * width, (h + 1) * width)
            q = q_ref[:, at]
            most = keep_ref[:, h : h + 1]
            inverse = keep_ref[:, heads + h : heads + h + 1]
            delta = keep_ref[:, 2 * heads + h : 2 * heads + h + 1]
            gs = (g_ref[:, at].astype(jnp.float32) * inverse).astype(jnp.bfloat16)
            p = jnp.exp2((dot_t(q, k) + bias - most) * (scale * LOG2E))
            ds = (p * (dot_t(gs, v) - delta)).astype(jnp.bfloat16)
            dq_ref[:, at] = ((far_ref[:, at] + dot(ds, k)) * scale).astype(jnp.bfloat16)
            dk_part, dv_part = dot(q.T, ds), dot(gs.T, p.astype(jnp.bfloat16))
            dk, dv = (dk_part, dv_part) if dk is None else (dk + dk_part, dv + dv_part)
        own_ref[:, 2 * n * width : (2 * n + 1) * width] = dk.T * scale
        own_ref[:, (2 * n + 1) * width : (2 * n + 2) * width] = dv.T


def choose_kernel(scale, place, own_ref, two_ref, four_ref, send_ref):
    even = place[0] % 2 == 0
    half = own_ref.shape[1]

    @pl.when(even)
    def _():
        send_ref[:, :half] = own_ref[...]
        send_ref[:, half:] = two_ref[...]

    @pl.when(jnp.logical_not(even))
    def _():
        send_ref[:, :half] = two_ref[...]
        send_ref[:, half:] = four_ref[...]


def join_kernel(scale, place, two_ref, four_ref, other_ref, two_out, four_out):
    even = place[0] % 2 == 0
    half = two_ref.shape[1]

    @pl.when(even)
    def _():
        three = other_ref[:, half:].astype(jnp.float32)
        two_out[...] = (two_ref[...] + three).astype(jnp.bfloat16)
        four_out[...] = four_ref[...].astype(jnp.bfloat16)

    @pl.when(jnp.logical_not(even))
    def _():
        one = other_ref[:, :half].astype(jnp.float32)
        three = other_ref[:, half:].astype(jnp.float32)
        two_out[...] = (two_ref[...] + one).astype(jnp.bfloat16)
        four_out[...] = (four_ref[...] + three).astype(jnp.bfloat16)


def total_kernel(scale, place, own_ref, other_ref, two_ref, four_ref, k_out, v_out):
    width = HEAD_WIDTH
    one = jnp.where(place[0] % 2 == 0, 1.0, 0.0)
    for n in range(k_out.shape[1] // width):
        for which, ref in enumerate((k_out, v_out)):
            at = slice((2 * n + which) * width, (2 * n + which + 1) * width)
            total = own_ref[:, at] + other_ref[:, at].astype(jnp.float32) * one
            total = total + two_ref[:, at].astype(jnp.float32) + four_ref[:, at].astype(jnp.float32)
            ref[:, n * width : (n + 1) * width] = total.astype(jnp.bfloat16)


def call(kernel, name, matmuls, outs, *args, scalars=0, scratch=(), hbm=()):
    whole = pl.BlockSpec(memory_space=pltpu.VMEM)
    return pl.pallas_call(
        functools.partial(kernel, 1.0 / math.sqrt(HEAD_WIDTH)),
        in_specs=[pl.BlockSpec(memory_space=pltpu.SMEM)] * scalars + [whole] * (len(args) - scalars),
        out_specs=[pl.BlockSpec(memory_space=pl.ANY) if i in hbm else whole for i in range(len(outs))],
        out_shape=[jax.ShapeDtypeStruct(shape, dtype) for shape, dtype in outs],
        scratch_shapes=scratch,
        compiler_params=pltpu.CompilerParams(vmem_limit_bytes=16 << 20),
        cost_estimate=pl.CostEstimate(
            flops=matmuls * 2 * 256 * 256 * 128 * 16, bytes_accessed=4 << 20, transcendentals=0
        ),
        name=name,
    )(*args)


def on_device(queries, keys, values, output_gradient, lengths):
    rows, width = queries.shape[0], HEAD_WIDTH
    groups = keys.shape[1] // width
    heads = queries.shape[1] // width
    place = lax.axis_index("seq")
    here = place.reshape(1).astype(jnp.int32)
    packs, twos, fours, fars = [], [], [], []
    for g in range(groups):
        at = slice(g * width, (g + 1) * width)
        packs.append(jnp.concatenate((keys[:, at], values[:, at]), axis=1))
    for pack in packs:
        twos.append(up(pack, 2))
        fours.append(up(pack, 4))
    parts, stats, near_bias, far_bias = call(
        own_forward_kernel,
        "own_forward",
        2,
        [
            (queries.shape, jnp.float32),
            ((rows, 2 * heads), jnp.float32),
            ((rows, rows), jnp.float32),
            ((rows, REACH * rows), jnp.float32),
        ],
        lengths,
        here,
        queries,
        keys,
        values,
        scalars=2,
    )
    packs, stats = lax.optimization_barrier((packs, stats))
    for pack, two, four in zip(packs, twos, fours):
        send = call(
            choose_kernel,
            "choose",
            0,
            [((rows, 4 * width), jnp.bfloat16)],
            here,
            pack,
            two,
            four,
            scalars=1,
        )[0]
        fars += [two, four, swapped(send)]
    wide = 2 * groups * width
    out, dq_far, keep, two, four, odd = call(
        far_kernel,
        "far",
        6 * REACH,
        [
            (queries.shape, jnp.bfloat16),
            (queries.shape, jnp.float32),
            ((rows, 3 * heads), jnp.float32),
            ((rows, wide), jnp.float32),
            ((rows, wide), jnp.float32),
            ((rows, 2 * wide), jnp.bfloat16),
        ],
        queries,
        output_gradient,
        parts,
        stats,
        far_bias,
        *fars,
        scratch=[pltpu.VMEM((groups, REACH * rows, width), jnp.bfloat16)] * 2
        + [pltpu.VMEM(queries.shape, jnp.float32), pltpu.SemaphoreType.DMA((heads,))],
        hbm=(1,),
    )
    other = swapped(odd)
    two, four = call(
        join_kernel,
        "join",
        0,
        [((rows, wide), jnp.bfloat16)] * 2,
        here,
        two,
        four,
        other,
        scalars=1,
    )
    two, four = up(two, -2), up(four, -4)
    split = lax.axis_size("head")
    got = lax.all_to_all(
        out.reshape(split, rows // split, out.shape[1]), "head", split_axis=0, concat_axis=0
    )
    d_queries, own = call(
        own_backward_kernel,
        "own_backward",
        5,
        [(queries.shape, jnp.bfloat16), ((rows, wide), jnp.float32)],
        queries,
        output_gradient,
        keys,
        values,
        near_bias,
        keep,
        dq_far,
    )
    key_gradient, value_gradient = call(
        total_kernel,
        "total",
        0,
        [(keys.shape, jnp.bfloat16)] * 2,
        here,
        own,
        other,
        two,
        four,
        scalars=1,
    )
    attn_out = jnp.transpose(got, (1, 0, 2)).reshape(got.shape[1], -1)
    return (attn_out, d_queries, key_gradient, value_gradient)


def solution(mesh):
    placed = (P("seq", "head"), P("seq", "head"), P("seq", "head"), P("seq", "head"), P())
    return jax.shard_map(
        on_device,
        mesh=mesh,
        in_specs=placed,
        out_specs=(P(("seq", "head"), None), P("seq", "head"), P("seq", "head"), P("seq", "head")),
        check_vma=False,
    )
```

time: 79.7 us -> 82.1 us (1.030)
  Pallas kernels: 23.8 us -> 36.6 us
  waiting for transfers between devices: 22.8 us -> 11.3 us
  local copies, waits for them, and re-layouts: 3.25 us -> 12.2 us
  starting transfers between devices: 25.9 us -> 20.9 us
  other arithmetic: 2.87 us -> 0.03 us
    ppermute x12 -> x9, waiting for transfers between devices: 22.8 us -> 8.46 us  [moved(): lax.ppermute(value, 'seq', [(source, to(source) % count) for source in ra...]
    pallas_call x3 -> x7, Pallas kernels: 23.8 us -> 36.6 us  [call(): pl.pallas_call(functools.partial(kernel, 1.0 / math.sqrt(HEAD_WIDTH)), in...]
    unnamed x10 -> x26, local copies, waits for them, and re-layouts: 1.23 us -> 8.81 us
    ppermute x12 -> x9, starting transfers between devices: 21.7 us -> 16.6 us  [moved(): lax.ppermute(value, 'seq', [(source, to(source) % count) for source in ra...]
    all_to_all x1, waiting for transfers between devices: 0.01 us -> 2.88 us  [on_device(): lax.all_to_all(out.reshape(split, rows // split, out.shape[1]), 'head', s...]
    concatenate x4 -> x0, other arithmetic: 1.38 us -> none  [the longest x1 0.67 us: on_device(): jnp.concatenate([s[:, width:] for s in sums], axis=1).astype(jnp.bfloat16)]
    reshape x1, local copies, waits for them, and re-layouts: 1.04 us -> 2.3 us  [on_device(): attn_out = jnp.transpose(got, (1, 0, 2)).reshape(got.shape[1], -1)]
    convert_element_type x4 -> x0, other arithmetic: 1.2 us -> none  [the longest x2 1.05 us: on_device(): other = swapped(odd).astype(jnp.float32)]
  transfers between devices with their start and end apart: 13 -> 10, of which waited for: 6 -> 6; matrix products, arithmetic and copies ran while one was open for 4% -> 3% of each run, Pallas kernels for 30% -> 10%
where the time goes in v3:
time: 82.1 us; the launch traced here: 81.7 us
  Pallas kernels  36.6 us (45%)
  starting transfers between devices  20.9 us (25%)
  local copies, waits for them, and re-layouts  12.2 us (15%)
  waiting for transfers between devices  11.3 us (14%)
    pallas_call x7, Pallas kernels, call(): pl.pallas_call(functools.partial(kernel, 1.0 / math.sqrt(HEAD_WIDTH)), in...  36.6 us
    ppermute x9, starting transfers between devices, moved(): lax.ppermute(value, 'seq', [(source, to(source) % count) for source in ra...  16.6 us
    unnamed x26, local copies, waits for them, and re-layouts  8.81 us
    ppermute x9, waiting for transfers between devices, moved(): lax.ppermute(value, 'seq', [(source, to(source) % count) for source in ra...  8.46 us
    all_to_all x1, starting transfers between devices, on_device(): lax.all_to_all(out.reshape(split, rows // split, out.shape[1]), 'head', s...  4.24 us
    all_to_all x1, waiting for transfers between devices, on_device(): lax.all_to_all(out.reshape(split, rows // split, out.shape[1]), 'head', s...  2.88 us
    reshape x1, local copies, waits for them, and re-layouts, on_device(): attn_out = jnp.transpose(got, (1, 0, 2)).reshape(got.shape[1], -1)  2.3 us
  transfers between devices with their start and end apart: 10, of which 6 were waited for; matrix products, arithmetic and copies ran while one was open for 3% of the time, Pallas kernels for 10%

profile of v3, /device:TPU:1, one launch (start us, length us, event | category | flops | bytes accessed | tf_op | source)
XLA Modules:
  0.0 81.7 jit_solution(12298691067062305253)
XLA Ops:
  0.6 1.0 %fusion = (bf16[256,128]{1,0:T(8,128)(2,1)S(1)}, bf16[256,128]{1,0:T(8,128)(2,1)S(1)}, bf16[256,128]{1,0:T(8,128)(2,1)S(1)}, bf16[256,128]{1,0:T(8,128)(2,1)S(1)}) fusion(bf16[256,256]{1,0:T(8,128)(2,1)} %k_ref.3, bf16[256,256]{1,0:T(8,128)(2,1)} %v_ref.3), kind=kLoop, calls=%fused_computation.2 | loop fusion | bytes 524288 | tf_op jit(solution)/shard_map/slice | solution.py:218
  1.7 3.9 %collective-permute-start.4 = (bf16[256,256]{1,0:T(8,128)(2,1)S(1)}, bf16[256,256]{1,0:T(8,128)(2,1)S(1)}, u32[]{:S(2)}, u32[]{:S(2)}) collective-permute-start(bf16[256,256]{1,0:T(8,128)(2,1)S(1)} %pad_maximum_fusion.1.own_ref), channel_id=1, source_target_pairs={{0,16},{4,20},{8,24},{12,28},{16,32},{20,36},{24,40},{28,44},{32,4... | collective-permute-start | bytes 393224 | tf_op jit(solution)/shard_map/ppermute | solution.py:27
  5.6 1.6 %collective-permute-start.3 = (bf16[256,256]{1,0:T(8,128)(2,1)S(1)}, bf16[256,256]{1,0:T(8,128)(2,1)S(1)}, u32[]{:S(2)}, u32[]{:S(2)}) collective-permute-start(bf16[256,256]{1,0:T(8,128)(2,1)S(1)} %pad_maximum_fusion.1.own_ref), channel_id=1, source_target_pairs={{0,8},{4,12},{8,16},{12,20},{16,24},{20,28},{24,32},{28,36},{32,40... | collective-permute-start | bytes 393224 | tf_op jit(solution)/shard_map/ppermute | solution.py:27
  7.3 3.4 %collective-permute-start.1 = (bf16[256,256]{1,0:T(8,128)(2,1)S(1)}, bf16[256,256]{1,0:T(8,128)(2,1)S(1)}, u32[]{:S(2)}, u32[]{:S(2)}) collective-permute-start(bf16[256,256]{1,0:T(8,128)(2,1)S(1)} %pad_maximum_fusion.own_ref), channel_id=1, source_target_pairs={{0,16},{4,20},{8,24},{12,28},{16,32},{20,36},{24,40},{28,44},{32,4... | collective-permute-start | bytes 393224 | tf_op jit(solution)/shard_map/ppermute | solution.py:27
  11.4 0.9 %copy-done = bf16[256,256]{1,0:T(8,128)(2,1)S(1)} copy-done((bf16[256,256]{1,0:T(8,128)(2,1)S(1)}, bf16[256,256]{1,0:T(8,128)(2,1)}, u32[]{:S(2)}) %copy-start) | copy-done | bytes 131096
  12.3 0.9 %copy-done.2 = bf16[256,256]{1,0:T(8,128)(2,1)S(1)} copy-done((bf16[256,256]{1,0:T(8,128)(2,1)S(1)}, bf16[256,256]{1,0:T(8,128)(2,1)}, u32[]{:S(2)}) %copy-start.2) | copy-done | bytes 131096
  13.2 1.2 %copy-done.4 = bf16[256,2048]{1,0:T(8,128)(2,1)S(1)} copy-done((bf16[256,2048]{1,0:T(8,128)(2,1)S(1)}, bf16[256,2048]{1,0:T(8,128)(2,1)}, u32[]{:S(2)}) %copy-start.4) | copy-done | bytes 1048600
  15.1 3.5 %own_forward.1 = (f32[256,2048]{1,0:T(8,128)S(1)}, f32[256,32]{1,0:T(8,128)S(1)}, f32[256,256]{1,0:T(8,128)S(1)}, f32[256,1024]{1,0:T(8,128)S(1)}) custom-call(s32[32]{0:T(128)S(1)} %copy-done.8, s32[1]{0:T(128)} %bitcast.here.place, bf16[256,2048]{1,0:T(8,128)(2,1)S(1)} %copy-done.4, bf16[256,256]{1,0:T(8,128)(2,1)S(1)} %copy-done, ...), custom_call_target="tpu_custom_call" | custom-call | flops 536870912 | bytes 4194304 | tf_op jit(solution)/shard_map/own_forward/pallas_call | solution.py:195
  18.6 1.0 %collective-permute-done.3.two_ref.refs_8_ = bf16[256,256]{1,0:T(8,128)(2,1)S(1)} collective-permute-done((bf16[256,256]{1,0:T(8,128)(2,1)S(1)}, bf16[256,256]{1,0:T(8,128)(2,1)S(1)}, u32[]{:S(2)}, u32[]{:S(2)}) %collective-permute-start.3) | collective-permute-done | bytes 131104 | tf_op jit(solution)/shard_map/ppermute | solution.py:27
  19.6 2.4 %collective-permute-start.5 = (bf16[256,512]{1,0:T(8,128)(2,1)S(1)}, bf16[256,512]{1,0:T(8,128)(2,1)S(1)}, u32[]{:S(2)}, u32[]{:S(2)}) collective-permute-start(bf16[256,512]{1,0:T(8,128)(2,1)S(1)} %choose.3), channel_id=1, source_target_pairs={{0,4},{4,0},{8,12},{12,8},{16,20},{20,16},{24,28},{28,24},{32,36},... | collective-permute-start | bytes 786440 | tf_op jit(solution)/shard_map/ppermute | solution.py:27
  21.9 0.9 %collective-permute-done.1.four_ref.refs_6_ = bf16[256,256]{1,0:T(8,128)(2,1)S(1)} collective-permute-done((bf16[256,256]{1,0:T(8,128)(2,1)S(1)}, bf16[256,256]{1,0:T(8,128)(2,1)S(1)}, u32[]{:S(2)}, u32[]{:S(2)}) %collective-permute-start.1) | collective-permute-done | bytes 131104 | tf_op jit(solution)/shard_map/ppermute | solution.py:27
  22.8 5.2 %collective-permute-done.two_ref.refs_5_ = bf16[256,256]{1,0:T(8,128)(2,1)S(1)} collective-permute-done((bf16[256,256]{1,0:T(8,128)(2,1)S(1)}, bf16[256,256]{1,0:T(8,128)(2,1)S(1)}, u32[]{:S(2)}, u32[]{:S(2)}) %collective-permute-start) | collective-permute-done | bytes 131104 | tf_op jit(solution)/shard_map/ppermute | solution.py:27
  28.0 1.0 %collective-permute-start.2 = (bf16[256,512]{1,0:T(8,128)(2,1)S(1)}, bf16[256,512]{1,0:T(8,128)(2,1)S(1)}, u32[]{:S(2)}, u32[]{:S(2)}) collective-permute-start(bf16[256,512]{1,0:T(8,128)(2,1)S(1)} %choose.2), channel_id=1, source_target_pairs={{0,4},{4,0},{8,12},{12,8},{16,20},{20,16},{24,28},{28,24},{32,36},... | collective-permute-start | bytes 786440 | tf_op jit(solution)/shard_map/ppermute | solution.py:27
  29.0 1.2 %collective-permute-done.2.refs_7_ = bf16[256,512]{1,0:T(8,128)(2,1)S(1)} collective-permute-done((bf16[256,512]{1,0:T(8,128)(2,1)S(1)}, bf16[256,512]{1,0:T(8,128)(2,1)S(1)}, u32[]{:S(2)}, u32[]{:S(2)}) %collective-permute-start.2) | collective-permute-done | bytes 262176 | tf_op jit(solution)/shard_map/ppermute | solution.py:27
  30.2 27.3 %far.1 = (bf16[256,2048]{1,0:T(8,128)(2,1)}, f32[256,2048]{1,0:T(8,128)S(1)}, f32[256,48]{1,0:T(8,128)S(1)}, f32[256,512]{1,0:T(8,128)S(1)}, f32[256,512]{1,0:T(8,128)S(1)}, /*index=5*/bf16[256,1024]{1,0:T(8,128)(2,1)S(1)}) custom-call(bf16[256,2048]{1,0:T(8,128)(2,1)S(1)} %copy-done.5, bf16[256,2048]{1,0:T(8,128)(2,1)S(1)} %copy-done.6, ...), custom_call_target="tpu_custom_call" | custom-call | flops 6442450944 | bytes 4194304 | tf_op jit(solution)/shard_map/far/pallas_call | solution.py:195
  57.5 1.3 %copy-done.9 = f32[256,2048]{1,0:T(8,128)} copy-done((f32[256,2048]{1,0:T(8,128)}, f32[256,2048]{1,0:T(8,128)S(1)}, u32[]{:S(2)}) %copy-start.9) | copy-done | bytes 2097176
  59.2 4.2 %all-to-all-start = ((bf16[4,64,2048]{2,1,0:T(8,128)(2,1)}), bf16[4,64,2048]{2,1,0:T(8,128)(2,1)}, u32[]{:S(2)}, u32[]{:S(2)}) async-start(bf16[4,64,2048]{2,1,0:T(8,128)(2,1)} %bitcast.1), calls=%async_computation | async-start | bytes 2097152 | tf_op jit(solution)/shard_map/all_to_all | solution.py:290
  64.4 2.4 %collective-permute-start.8 = (bf16[256,512]{1,0:T(8,128)(2,1)S(1)}, bf16[256,512]{1,0:T(8,128)(2,1)S(1)}, u32[]{:S(2)}, u32[]{:S(2)}) collective-permute-start(bf16[256,512]{1,0:T(8,128)(2,1)S(1)} %get-tuple-element.39), channel_id=1, source_target_pairs={{0,240},{4,244},{8,248},{12,252},{16,0},{20,4},{24,8},{28,12},{32,... | collective-permute-start | bytes 786440 | tf_op jit(solution)/shard_map/ppermute | solution.py:27
  66.8 1.2 %copy-done.7 = bf16[256,2048]{1,0:T(8,128)(2,1)S(1)} copy-done((bf16[256,2048]{1,0:T(8,128)(2,1)S(1)}, bf16[256,2048]{1,0:T(8,128)(2,1)}, u32[]{:S(2)}) %copy-start.7) | copy-done | bytes 1048600
  68.0 1.6 %copy-done.10 = f32[256,2048]{1,0:T(8,128)S(1)} copy-done((f32[256,2048]{1,0:T(8,128)S(1)}, f32[256,2048]{1,0:T(8,128)}, u32[]{:S(2)}) %copy-start.10) | copy-done | bytes 2097176
  69.6 0.9 %copy-done.12 = f32[256,256]{1,0:T(8,128)S(1)} copy-done((f32[256,256]{1,0:T(8,128)S(1)}, f32[256,256]{1,0:T(8,128)}, u32[]{:S(2)}) %copy-start.12) | copy-done | bytes 262168
  70.6 4.9 %own_backward.1 = (bf16[256,2048]{1,0:T(8,128)(2,1)}, f32[256,512]{1,0:T(8,128)S(1)}) custom-call(bf16[256,2048]{1,0:T(8,128)(2,1)S(1)} %copy-done.5, bf16[256,2048]{1,0:T(8,128)(2,1)S(1)} %copy-done.7, bf16[256,256]{1,0:T(8,128)(2,1)S(1)} %copy-done.1, bf16[256,256]{1,0:T(8,128)(2,1)S(1)} %copy-done.3, f32[256,256]{1,0:T(8,128)S(1)} %copy-done.12, ...), custom_call_target="tpu_custom_call" | custom-call | flops 1342177280 | bytes 4194304 | tf_op jit(solution)/shard_map/own_backward/pallas_call | solution.py:195
  75.4 2.9 %all-to-all-done = bf16[4,64,2048]{2,1,0:T(8,128)(2,1)} async-done(((bf16[4,64,2048]{2,1,0:T(8,128)(2,1)}), bf16[4,64,2048]{2,1,0:T(8,128)(2,1)}, u32[]{:S(2)}, u32[]{:S(2)}) %all-to-all-start) | async-done | bytes 1048608 | tf_op jit(solution)/shard_map/all_to_all | solution.py:290
  78.3 2.3 %copy.10 = bf16[4,8,8,2048]{3,2,0,1:T(8,128)(2,1)} copy(bf16[4,8,8,2048]{3,2,1,0:T(8,128)(2,1)} %bitcast.3) | data formatting | bytes 2097152 | tf_op jit(solution)/shard_map/reshape | solution.py:318
  (33 shorter events, 3.9 us)
Async XLA Ops:
  0.6 29.5 %copy-start.5 = (bf16[256,2048]{1,0:T(8,128)(2,1)S(1)}, bf16[256,2048]{1,0:T(8,128)(2,1)}, u32[]{:S(2)}) copy-start(bf16[256,2048]{1,0:T(8,128)(2,1)} %q_ref.3) | copy-start | bytes 3145732
  1.7 16.8 %collective-permute-start.4 = (bf16[256,256]{1,0:T(8,128)(2,1)S(1)}, bf16[256,256]{1,0:T(8,128)(2,1)S(1)}, u32[]{:S(2)}, u32[]{:S(2)}) collective-permute-start(bf16[256,256]{1,0:T(8,128)(2,1)S(1)} %pad_maximum_fusion.1.own_ref), channel_id=1, source_target_pairs={{0,16},{4,20},{8,24},{12,28},{16,32},{20,36},{24,40},{28,44},{32,4... | collective-permute-start | bytes 393224 | tf_op jit(solution)/shard_map/ppermute | solution.py:27
  5.6 13.9 %collective-permute-start.3 = (bf16[256,256]{1,0:T(8,128)(2,1)S(1)}, bf16[256,256]{1,0:T(8,128)(2,1)S(1)}, u32[]{:S(2)}, u32[]{:S(2)}) collective-permute-start(bf16[256,256]{1,0:T(8,128)(2,1)S(1)} %pad_maximum_fusion.1.own_ref), channel_id=1, source_target_pairs={{0,8},{4,12},{8,16},{12,20},{16,24},{20,28},{24,32},{28,36},{32,40... | collective-permute-start | bytes 393224 | tf_op jit(solution)/shard_map/ppermute | solution.py:27
  7.3 15.6 %collective-permute-start.1 = (bf16[256,256]{1,0:T(8,128)(2,1)S(1)}, bf16[256,256]{1,0:T(8,128)(2,1)S(1)}, u32[]{:S(2)}, u32[]{:S(2)}) collective-permute-start(bf16[256,256]{1,0:T(8,128)(2,1)S(1)} %pad_maximum_fusion.own_ref), channel_id=1, source_target_pairs={{0,16},{4,20},{8,24},{12,28},{16,32},{20,36},{24,40},{28,44},{32,4... | collective-permute-start | bytes 393224 | tf_op jit(solution)/shard_map/ppermute | solution.py:27
  10.7 17.3 %collective-permute-start = (bf16[256,256]{1,0:T(8,128)(2,1)S(1)}, bf16[256,256]{1,0:T(8,128)(2,1)S(1)}, u32[]{:S(2)}, u32[]{:S(2)}) collective-permute-start(bf16[256,256]{1,0:T(8,128)(2,1)S(1)} %pad_maximum_fusion.own_ref), channel_id=1, source_target_pairs={{0,8},{4,12},{8,16},{12,20},{16,24},{20,28},{24,32},{28,36},{32,40... | collective-permute-start | bytes 393224 | tf_op jit(solution)/shard_map/ppermute | solution.py:27
  11.4 0.9 %copy-start = (bf16[256,256]{1,0:T(8,128)(2,1)S(1)}, bf16[256,256]{1,0:T(8,128)(2,1)}, u32[]{:S(2)}) copy-start(bf16[256,256]{1,0:T(8,128)(2,1)} %k_ref.3) | copy-start | bytes 393220
  12.3 0.9 %copy-start.2 = (bf16[256,256]{1,0:T(8,128)(2,1)S(1)}, bf16[256,256]{1,0:T(8,128)(2,1)}, u32[]{:S(2)}) copy-start(bf16[256,256]{1,0:T(8,128)(2,1)} %v_ref.3) | copy-start | bytes 393220
  13.2 1.2 %copy-start.4 = (bf16[256,2048]{1,0:T(8,128)(2,1)S(1)}, bf16[256,2048]{1,0:T(8,128)(2,1)}, u32[]{:S(2)}) copy-start(bf16[256,2048]{1,0:T(8,128)(2,1)} %q_ref.3) | copy-start | bytes 3145732
  14.4 0.7 copy-start.8
  15.1 15.1 %copy-start.6 = (bf16[256,2048]{1,0:T(8,128)(2,1)S(1)}, bf16[256,2048]{1,0:T(8,128)(2,1)}, u32[]{:S(2)}) copy-start(bf16[256,2048]{1,0:T(8,128)(2,1)} %g_ref.1) | copy-start | bytes 3145732
  18.5 11.6 %copy-start.11 = (f32[256,256]{1,0:T(8,128)}, f32[256,256]{1,0:T(8,128)S(1)}, u32[]{:S(2)}) copy-start(f32[256,256]{1,0:T(8,128)S(1)} %get-tuple-element.30.bias_ref) | copy-start | bytes 786436
  19.6 9.4 %collective-permute-start.5 = (bf16[256,512]{1,0:T(8,128)(2,1)S(1)}, bf16[256,512]{1,0:T(8,128)(2,1)S(1)}, u32[]{:S(2)}, u32[]{:S(2)}) collective-permute-start(bf16[256,512]{1,0:T(8,128)(2,1)S(1)} %choose.3), channel_id=1, source_target_pairs={{0,4},{4,0},{8,12},{12,8},{16,20},{20,16},{24,28},{28,24},{32,36},... | collective-permute-start | bytes 786440 | tf_op jit(solution)/shard_map/ppermute | solution.py:27
  28.0 2.2 %collective-permute-start.2 = (bf16[256,512]{1,0:T(8,128)(2,1)S(1)}, bf16[256,512]{1,0:T(8,128)(2,1)S(1)}, u32[]{:S(2)}, u32[]{:S(2)}) collective-permute-start(bf16[256,512]{1,0:T(8,128)(2,1)S(1)} %choose.2), channel_id=1, source_target_pairs={{0,4},{4,0},{8,12},{12,8},{16,20},{20,16},{24,28},{28,24},{32,36},... | collective-permute-start | bytes 786440 | tf_op jit(solution)/shard_map/ppermute | solution.py:27
  57.5 1.3 %copy-start.9 = (f32[256,2048]{1,0:T(8,128)}, f32[256,2048]{1,0:T(8,128)S(1)}, u32[]{:S(2)}) copy-start(f32[256,2048]{1,0:T(8,128)S(1)} %get-tuple-element.32.far_ref) | copy-start | bytes 6291460
  58.8 8.0 %copy-start.1 = (bf16[256,256]{1,0:T(8,128)(2,1)S(1)}, bf16[256,256]{1,0:T(8,128)(2,1)}, u32[]{:S(2)}) copy-start(bf16[256,256]{1,0:T(8,128)(2,1)} %k_ref.3) | copy-start | bytes 393220
  58.8 8.0 %copy-start.3 = (bf16[256,256]{1,0:T(8,128)(2,1)S(1)}, bf16[256,256]{1,0:T(8,128)(2,1)}, u32[]{:S(2)}) copy-start(bf16[256,256]{1,0:T(8,128)(2,1)} %v_ref.3) | copy-start | bytes 393220
  58.8 4.6 %collective-permute-start.6 = (bf16[256,1024]{1,0:T(8,128)(2,1)S(1)}, bf16[256,1024]{1,0:T(8,128)(2,1)S(1)}, u32[]{:S(2)}, u32[]{:S(2)}) collective-permute-start(bf16[256,1024]{1,0:T(8,128)(2,1)S(1)} %get-tuple-element.35), channel_id=1, source_target_pairs={{0,4},{4,0},{8,12},{12,8},{16,20},{20,16},{24,28},{28,24},{32,36},... | collective-permute-start | bytes 1572872 | tf_op jit(solution)/shard_map/ppermute | solution.py:27
  59.2 19.1 %all-to-all-start = ((bf16[4,64,2048]{2,1,0:T(8,128)(2,1)}), bf16[4,64,2048]{2,1,0:T(8,128)(2,1)}, u32[]{:S(2)}, u32[]{:S(2)}) async-start(bf16[4,64,2048]{2,1,0:T(8,128)(2,1)} %bitcast.1), calls=%async_computation | async-start | bytes 2097152 | tf_op jit(solution)/shard_map/all_to_all | solution.py:290
  63.6 17.0 %collective-permute-start.7 = (bf16[256,512]{1,0:T(8,128)(2,1)S(1)}, bf16[256,512]{1,0:T(8,128)(2,1)S(1)}, u32[]{:S(2)}, u32[]{:S(2)}) collective-permute-start(bf16[256,512]{1,0:T(8,128)(2,1)S(1)} %get-tuple-element.38), channel_id=1, source_target_pairs={{0,248},{4,252},{8,0},{12,4},{16,8},{20,12},{24,16},{28,20},{32,24... | collective-permute-start | bytes 786440 | tf_op jit(solution)/shard_map/ppermute | solution.py:27
  64.4 16.5 %collective-permute-start.8 = (bf16[256,512]{1,0:T(8,128)(2,1)S(1)}, bf16[256,512]{1,0:T(8,128)(2,1)S(1)}, u32[]{:S(2)}, u32[]{:S(2)}) collective-permute-start(bf16[256,512]{1,0:T(8,128)(2,1)S(1)} %get-tuple-element.39), channel_id=1, source_target_pairs={{0,240},{4,244},{8,248},{12,252},{16,0},{20,4},{24,8},{28,12},{32,... | collective-permute-start | bytes 786440 | tf_op jit(solution)/shard_map/ppermute | solution.py:27
  66.8 1.2 %copy-start.7 = (bf16[256,2048]{1,0:T(8,128)(2,1)S(1)}, bf16[256,2048]{1,0:T(8,128)(2,1)}, u32[]{:S(2)}) copy-start(bf16[256,2048]{1,0:T(8,128)(2,1)} %g_ref.1) | copy-start | bytes 3145732
  68.0 1.6 %copy-start.10 = (f32[256,2048]{1,0:T(8,128)S(1)}, f32[256,2048]{1,0:T(8,128)}, u32[]{:S(2)}) copy-start(f32[256,2048]{1,0:T(8,128)} %copy-done.9) | copy-start | bytes 6291460
  69.6 0.9 %copy-start.12 = (f32[256,256]{1,0:T(8,128)S(1)}, f32[256,256]{1,0:T(8,128)}, u32[]{:S(2)}) copy-start(f32[256,256]{1,0:T(8,128)} %copy-done.11) | copy-start | bytes 786436

commit v4 on v3

v4 whole, which is shorter than its diff:
```python
import functools
import math

import jax
import jax.numpy as jnp
from jax import lax
from jax.experimental import pallas as pl
from jax.experimental.pallas import tpu as pltpu
from jax.sharding import PartitionSpec as P

HEAD_WIDTH = 128
REACH = 4
NEG = -1e30
LOG2E = 1.4426950408889634


def dot(a, b):
    return lax.dot_general(a, b, (((1,), (0,)), ((), ())), preferred_element_type=jnp.float32)


def dot_t(a, b):
    return lax.dot_general(a, b, (((1,), (1,)), ((), ())), preferred_element_type=jnp.float32)


def moved(value, to):
    count = lax.axis_size("seq")
    return lax.ppermute(value, "seq", [(source, to(source) % count) for source in range(count)])


def up(value, steps):
    return moved(value, lambda source: source + steps)


def swapped(value):
    return moved(value, lambda source: source ^ 1)


def first_seen(lens, here, rows, width):
    base = here[0] * rows
    row = lax.broadcasted_iota(jnp.int32, (rows, width), 0)

    def one(i, carry):
        end, start = carry
        end = end + lens[i]
        return end, jnp.where(row >= end - base, end - base, start)

    first = (jnp.int32(0), jnp.full((rows, width), -base, jnp.int32))
    return lax.fori_loop(0, lens.shape[0], one, first)[1]


def mask(start, distance):
    row = lax.broadcasted_iota(jnp.int32, start.shape, 0)
    pos = lax.broadcasted_iota(jnp.int32, start.shape, 1) - distance
    seen = pos >= start if distance >= start.shape[0] else (pos >= start) & (pos <= row)
    return jnp.where(seen, 0.0, NEG).astype(jnp.float32)


def near_mask(start, rows):
    width = start.shape[1]
    return jnp.concatenate([mask(start, -at) for at in range(0, rows, width)], axis=1)


def own_forward_kernel(scale, lens, here, q_ref, *refs):
    out_ref, top_ref, sum_ref, far_ref = refs[-4:]
    rows, width = q_ref.shape[0], HEAD_WIDTH
    start = first_seen(lens, here, rows, width)
    for at in range(0, REACH * rows, width):
        far_ref[:, at : at + width] = mask(start, REACH * rows - at)
    near = near_mask(start, rows)
    groups = len(refs) - 4
    heads = q_ref.shape[1] // width
    for h in range(heads):
        at = slice(h * width, (h + 1) * width)
        pack = refs[h * groups // heads]
        s = dot_t(q_ref[:, at], pack[:, :width]) + near
        top = s.max(axis=1, keepdims=True)
        p = jnp.exp2((s - top) * (scale * LOG2E))
        top_ref[:, at] = jnp.broadcast_to(top, (rows, width))
        sum_ref[:, at] = jnp.broadcast_to(p.sum(axis=1, keepdims=True), (rows, width))
        out_ref[:, at] = dot(p.astype(jnp.bfloat16), pack[:, width:])


def far_kernel(scale, *refs):
    q_ref, g_ref, out_ref, top_ref, sum_ref, bias_ref = refs[0:6]
    (o_out, dq_out, keep_out, two_out, four_out, odd_out) = refs[-12:-6]
    k_all, v_all, o_ref, dq_ref, keep_ref, sent = refs[-6:]
    fars = refs[6:-12]
    rows, width = q_ref.shape[0], HEAD_WIDTH
    groups = len(fars) // 3
    heads = q_ref.shape[1] // width
    share = heads // groups
    factor = scale * LOG2E
    bias = bias_ref[...]
    for n in range(groups):
        two_ref, four_ref, odd_ref = fars[3 * n : 3 * n + 3]
        for b, (ref, place) in enumerate(((four_ref, 0), (odd_ref, 1), (two_ref, 0), (odd_ref, 0))):
            at = slice(b * rows, (b + 1) * rows)
            k_all[n, at, :] = ref[:, 2 * place * width : (2 * place + 1) * width]
            v_all[n, at, :] = ref[:, (2 * place + 1) * width : (2 * place + 2) * width]

    def weigh(h):
        at = slice(h * width, (h + 1) * width)
        q, top = q_ref[:, at], top_ref[:, at]
        s = dot_t(q, k_all[h // share]) + bias
        most = jnp.maximum(top, s.max(axis=1, keepdims=True))
        p = jnp.exp2((s - jnp.tile(most, (1, s.shape[1] // width))) * factor)
        keep = jnp.exp2((top - most) * factor)
        total = sum_ref[:, at] * keep + p.sum(axis=1, keepdims=True)
        return at, q, p, most, keep, total

    def send(n):
        to = slice(n * share * width, (n + 1) * share * width)
        pairs = [(o_ref.at[:, to], o_out.at[:, to]), (dq_ref.at[:, to], dq_out.at[:, to])]
        if n == groups - 1:
            pairs.append((keep_ref, keep_out))
        return [pltpu.make_async_copy(*pair, sent.at[2 * n + i]) for i, pair in enumerate(pairs)]

    ahead = weigh(0)
    for h in range(heads):
        n = h // share
        at, q, p, most, keep, total = ahead
        ahead = weigh(h + 1) if h + 1 < heads else None
        k, v = k_all[n], v_all[n]
        inverse = 1.0 / total
        pb = p.astype(jnp.bfloat16)
        o = (dot(pb, v) + out_ref[:, at] * keep) * inverse
        o_ref[:, at] = o.astype(jnp.bfloat16)
        gs = (g_ref[:, at].astype(jnp.float32) * inverse).astype(jnp.bfloat16)
        delta = jnp.sum(gs.astype(jnp.float32) * o, axis=1, keepdims=True)
        keep_ref[:, h : h + 1] = most[:, :1] * factor + jnp.log2(total[:, :1])
        keep_ref[:, heads + h : heads + h + 1] = delta * total[:, :1]
        ds = (p * (dot_t(gs, v) - delta)).astype(jnp.bfloat16)
        dq_ref[:, at] = dot(ds, k).astype(jnp.bfloat16)
        dk_part, dv_part = dot(q.T, ds), dot(gs.T, pb)
        dk, dv = (dk_part, dv_part) if h % share == 0 else (dk + dk_part, dv + dv_part)
        if h % share == share - 1:
            for copy in send(n):
                copy.start()
            outs = ((four_out, 0), (odd_out, 1), (two_out, 0), (odd_out, 0))
            for b, (ref, place) in enumerate(outs):
                at = slice(b * rows, (b + 1) * rows)
                for which, grad in enumerate((dk[:, at].T * scale, dv[:, at].T)):
                    to = (2 * groups * place + 2 * n + which) * width
                    ref[:, to : to + width] = grad.astype(ref.dtype)
    for n in range(groups):
        for copy in send(n):
            copy.wait()


def own_backward_kernel(scale, lens, here, q_ref, g_ref, far_ref, keep_ref, *refs):
    dq_ref, own_ref = refs[-2:]
    rows, width = q_ref.shape[0], HEAD_WIDTH
    groups = len(refs) - 2
    heads = q_ref.shape[1] // width
    share = heads // groups
    factor = scale * LOG2E
    bias = near_mask(first_seen(lens, here, rows, width), rows)
    for h in range(heads):
        n = h // share
        k, v = refs[n][:, :width], refs[n][:, width:]
        at = slice(h * width, (h + 1) * width)
        q, g = q_ref[:, at], g_ref[:, at]
        p = jnp.exp2((dot_t(q, k) + bias) * factor - keep_ref[:, h : h + 1])
        ds = (p * (dot_t(g, v) - keep_ref[:, heads + h : heads + h + 1])).astype(jnp.bfloat16)
        dq = far_ref[:, at].astype(jnp.float32) + dot(ds, k)
        dq_ref[:, at] = (dq * scale).astype(jnp.bfloat16)
        dk_part, dv_part = dot(q.T, ds), dot(g.T, p.astype(jnp.bfloat16))
        dk, dv = (dk_part, dv_part) if h % share == 0 else (dk + dk_part, dv + dv_part)
        if h % share == share - 1:
            own_ref[:, 2 * n * width : (2 * n + 1) * width] = dk.T * scale
            own_ref[:, (2 * n + 1) * width : (2 * n + 2) * width] = dv.T


def choose_kernel(scale, place, own_ref, two_ref, four_ref, send_ref):
    even = place[0] % 2 == 0
    half = own_ref.shape[1]

    @pl.when(even)
    def _():
        send_ref[:, :half] = own_ref[...]
        send_ref[:, half:] = two_ref[...]

    @pl.when(jnp.logical_not(even))
    def _():
        send_ref[:, :half] = two_ref[...]
        send_ref[:, half:] = four_ref[...]


def join_kernel(scale, place, two_ref, four_ref, other_ref, two_out, four_out):
    even = place[0] % 2 == 0
    half = two_ref.shape[1]

    @pl.when(even)
    def _():
        three = other_ref[:, half:].astype(jnp.float32)
        two_out[...] = (two_ref[...] + three).astype(jnp.bfloat16)
        four_out[...] = four_ref[...].astype(jnp.bfloat16)

    @pl.when(jnp.logical_not(even))
    def _():
        one = other_ref[:, :half].astype(jnp.float32)
        three = other_ref[:, half:].astype(jnp.float32)
        two_out[...] = (two_ref[...] + one).astype(jnp.bfloat16)
        four_out[...] = (four_ref[...] + three).astype(jnp.bfloat16)


def total_kernel(scale, place, own_ref, other_ref, two_ref, four_ref, k_out, v_out):
    width = HEAD_WIDTH
    one = jnp.where(place[0] % 2 == 0, 1.0, 0.0)
    for n in range(k_out.shape[1] // width):
        for which, ref in enumerate((k_out, v_out)):
            at = slice((2 * n + which) * width, (2 * n + which + 1) * width)
            total = own_ref[:, at] + other_ref[:, at].astype(jnp.float32) * one
            total = total + two_ref[:, at].astype(jnp.float32) + four_ref[:, at].astype(jnp.float32)
            ref[:, n * width : (n + 1) * width] = total.astype(jnp.bfloat16)


def call(kernel, name, cost, outs, *args, scalars=0, scratch=(), hbm=()):
    whole = pl.BlockSpec(memory_space=pltpu.VMEM)
    left = pl.BlockSpec(memory_space=pltpu.HBM)
    return pl.pallas_call(
        functools.partial(kernel, 1.0 / math.sqrt(HEAD_WIDTH)),
        in_specs=[pl.BlockSpec(memory_space=pltpu.SMEM)] * scalars + [whole] * (len(args) - scalars),
        out_specs=[left if i in hbm else whole for i in range(len(outs))],
        out_shape=[jax.ShapeDtypeStruct(shape, dtype) for shape, dtype in outs],
        scratch_shapes=scratch,
        compiler_params=pltpu.CompilerParams(vmem_limit_bytes=20 << 20),
        cost_estimate=pl.CostEstimate(
            flops=cost << 20, bytes_accessed=1 << 20, transcendentals=0
        ),
        name=name,
    )(*args)


def on_device(queries, keys, values, output_gradient, lengths):
    rows, width = queries.shape[0], HEAD_WIDTH
    groups = keys.shape[1] // width
    heads = queries.shape[1] // width
    wide = 2 * groups * width
    place = lax.axis_index("seq")
    here = place.reshape(1).astype(jnp.int32)
    packs, twos, fours, fars = [], [], [], []
    for n in range(groups):
        at = slice(n * width, (n + 1) * width)
        packs.append(jnp.concatenate((keys[:, at], values[:, at]), axis=1))
    for pack in packs:
        twos.append(up(pack, 2))
        fours.append(up(pack, 4))
    parts, top, total, bias = call(
        own_forward_kernel,
        "own_forward",
        512,
        [(queries.shape, jnp.float32)] * 3 + [((rows, REACH * rows), jnp.float32)],
        lengths,
        here,
        queries,
        *packs,
        scalars=2,
    )
    packs, bias = lax.optimization_barrier((packs, bias))
    for pack, two, four in zip(packs, twos, fours):
        send = call(
            choose_kernel,
            "choose",
            0,
            [((rows, 4 * width), jnp.bfloat16)],
            here,
            pack,
            two,
            four,
            scalars=1,
        )[0]
        fars += [two, four, swapped(send)]
    out, dq_far, keep, two, four, odd = call(
        far_kernel,
        "far",
        6 * 1024,
        [
            (queries.shape, jnp.bfloat16),
            (queries.shape, jnp.bfloat16),
            ((rows, width), jnp.float32),
            ((rows, wide), jnp.float32),
            ((rows, wide), jnp.float32),
            ((rows, 2 * wide), jnp.bfloat16),
        ],
        queries,
        output_gradient,
        parts,
        top,
        total,
        bias,
        *fars,
        scratch=[pltpu.VMEM((groups, REACH * rows, width), jnp.bfloat16)] * 2
        + [pltpu.VMEM(queries.shape, jnp.bfloat16)] * 2
        + [pltpu.VMEM((rows, width), jnp.float32), pltpu.SemaphoreType.DMA((2 * groups + 1,))],
        hbm=(0, 1, 2),
    )
    other = swapped(odd)
    two, four = call(
        join_kernel,
        "join",
        0,
        [((rows, wide), jnp.bfloat16)] * 2,
        here,
        two,
        four,
        other,
        scalars=1,
    )
    two_back, four_back = up(two, -2), up(four, -4)
    split = lax.axis_size("head")
    got = lax.all_to_all(
        out.reshape(split, rows // split, out.shape[1]), "head", split_axis=0, concat_axis=0
    )
    keep, two = lax.optimization_barrier((keep, two))
    d_queries, own = call(
        own_backward_kernel,
        "own_backward",
        1024,
        [(queries.shape, jnp.bfloat16), ((rows, wide), jnp.float32)],
        lengths,
        here,
        queries,
        output_gradient,
        dq_far,
        keep,
        *packs,
        scalars=2,
    )
    key_gradient, value_gradient = call(
        total_kernel,
        "total",
        0,
        [(keys.shape, jnp.bfloat16)] * 2,
        here,
        own,
        other,
        two_back,
        four_back,
        scalars=1,
    )
    attn_out = jnp.transpose(got, (1, 0, 2)).reshape(got.shape[1], -1)
    return (attn_out, d_queries, key_gradient, value_gradient)


def solution(mesh):
    placed = (P("seq", "head"), P("seq", "head"), P("seq", "head"), P("seq", "head"), P())
    return jax.shard_map(
        on_device,
        mesh=mesh,
        in_specs=placed,
        out_specs=(P(("seq", "head"), None), P("seq", "head"), P("seq", "head"), P("seq", "head")),
        check_vma=False,
    )
```

time: 82.1 us -> 73.5 us (0.90)
  Pallas kernels: 36.6 us -> 27.5 us
  waiting for transfers between devices: 11.3 us -> 15.2 us
  local copies, waits for them, and re-layouts: 12.2 us -> 8.65 us
    pallas_call x7, Pallas kernels: 36.6 us -> 27.5 us  [call(): pl.pallas_call(functools.partial(kernel, 1.0 / math.sqrt(HEAD_WIDTH)), in...]
    ppermute x9, waiting for transfers between devices: 8.46 us -> 12.8 us  [moved(): lax.ppermute(value, 'seq', [(source, to(source) % count) for source in ra...]
    unnamed x26 -> x16, local copies, waits for them, and re-layouts: 8.81 us -> 5.31 us
  transfers between devices with their start and end apart: 10 -> 10, of which waited for: 6 -> 6; matrix products, arithmetic and copies ran while one was open for 3% -> 3% of each run, Pallas kernels for 10% -> 14%
where the time goes in v4:
time: 73.5 us; the launch traced here: 73.2 us
  Pallas kernels  27.5 us (37%)
  starting transfers between devices  21 us (29%)
  waiting for transfers between devices  15.2 us (21%)
  local copies, waits for them, and re-layouts  8.65 us (12%)
    pallas_call x7, Pallas kernels, call(): pl.pallas_call(functools.partial(kernel, 1.0 / math.sqrt(HEAD_WIDTH)), in...  27.5 us
    ppermute x9, starting transfers between devices, moved(): lax.ppermute(value, 'seq', [(source, to(source) % count) for source in ra...  16.8 us
    ppermute x9, waiting for transfers between devices, moved(): lax.ppermute(value, 'seq', [(source, to(source) % count) for source in ra...  12.8 us
    unnamed x16, local copies, waits for them, and re-layouts  5.31 us
    all_to_all x1, starting transfers between devices, on_device(): lax.all_to_all(out.reshape(split, rows // split, out.shape[1]), 'head', s...  4.26 us
    all_to_all x1, waiting for transfers between devices, on_device(): lax.all_to_all(out.reshape(split, rows // split, out.shape[1]), 'head', s...  2.41 us
    reshape x1, local copies, waits for them, and re-layouts, on_device(): attn_out = jnp.transpose(got, (1, 0, 2)).reshape(got.shape[1], -1)  2.3 us
  transfers between devices with their start and end apart: 10, of which 6 were waited for; matrix products, arithmetic and copies ran while one was open for 3% of the time, Pallas kernels for 14%

profile of v4, /device:TPU:1, one launch (start us, length us, event | category | flops | bytes accessed | tf_op | source)
XLA Modules:
  0.0 73.2 jit_solution(12798513112970438821)
XLA Ops:
  0.6 1.0 %fusion = (bf16[256,128]{1,0:T(8,128)(2,1)S(1)}, bf16[256,128]{1,0:T(8,128)(2,1)S(1)}, bf16[256,128]{1,0:T(8,128)(2,1)S(1)}, bf16[256,128]{1,0:T(8,128)(2,1)S(1)}) fusion(bf16[256,256]{1,0:T(8,128)(2,1)} %param.6, bf16[256,256]{1,0:T(8,128)(2,1)} %param.7), kind=kLoop, calls=%fused_computation.2 | loop fusion | bytes 524288 | tf_op jit(solution)/shard_map/slice | solution.py:245
  1.7 3.9 %collective-permute-start.4 = (bf16[256,256]{1,0:T(8,128)(2,1)S(1)}, bf16[256,256]{1,0:T(8,128)(2,1)S(1)}, u32[]{:S(2)}, u32[]{:S(2)}) collective-permute-start(bf16[256,256]{1,0:T(8,128)(2,1)S(1)} %pad_maximum_fusion.1.refs_1_.own_ref), channel_id=1, source_target_pairs={{0,16},{4,20},{8,24},{12,28},{16,32},{20,36},{24,40},{28,44},{32,4... | collective-permute-start | bytes 393224 | tf_op jit(solution)/shard_map/ppermute | solution.py:27
  5.6 1.6 %collective-permute-start.3 = (bf16[256,256]{1,0:T(8,128)(2,1)S(1)}, bf16[256,256]{1,0:T(8,128)(2,1)S(1)}, u32[]{:S(2)}, u32[]{:S(2)}) collective-permute-start(bf16[256,256]{1,0:T(8,128)(2,1)S(1)} %pad_maximum_fusion.1.refs_1_.own_ref), channel_id=1, source_target_pairs={{0,8},{4,12},{8,16},{12,20},{16,24},{20,28},{24,32},{28,36},{32,40... | collective-permute-start | bytes 393224 | tf_op jit(solution)/shard_map/ppermute | solution.py:27
  7.3 3.4 %collective-permute-start.1 = (bf16[256,256]{1,0:T(8,128)(2,1)S(1)}, bf16[256,256]{1,0:T(8,128)(2,1)S(1)}, u32[]{:S(2)}, u32[]{:S(2)}) collective-permute-start(bf16[256,256]{1,0:T(8,128)(2,1)S(1)} %pad_maximum_fusion.refs_0_.own_ref), channel_id=1, source_target_pairs={{0,16},{4,20},{8,24},{12,28},{16,32},{20,36},{24,40},{28,44},{32,4... | collective-permute-start | bytes 393224 | tf_op jit(solution)/shard_map/ppermute | solution.py:27
  11.4 1.2 %copy-done = bf16[256,2048]{1,0:T(8,128)(2,1)S(1)} copy-done((bf16[256,2048]{1,0:T(8,128)(2,1)S(1)}, bf16[256,2048]{1,0:T(8,128)(2,1)}, u32[]{:S(2)}) %copy-start) | copy-done | bytes 1048600
  13.3 3.3 %own_forward.1 = (f32[256,2048]{1,0:T(8,128)S(1)}, f32[256,2048]{1,0:T(8,128)S(1)}, f32[256,2048]{1,0:T(8,128)S(1)}, f32[256,1024]{1,0:T(8,128)S(1)}) custom-call(s32[32]{0:T(128)S(1)} %copy-done.4, s32[1]{0:T(128)} %bitcast.here.place, bf16[256,2048]{1,0:T(8,128)(2,1)S(1)} %copy-done, bf16[256,256]{1,0:T(8,128)(2,1)S(1)} %pad_maximum_fusion.refs_0_.own_ref, ...), custom_call_target="tpu_custom_call" | custom-call | flops 536870912 | bytes 1048576 | tf_op jit(solution)/shard_map/own_forward/pallas_call | solution.py:221
  16.6 2.9 %collective-permute-done.3.two_ref.refs_9_ = bf16[256,256]{1,0:T(8,128)(2,1)S(1)} collective-permute-done((bf16[256,256]{1,0:T(8,128)(2,1)S(1)}, bf16[256,256]{1,0:T(8,128)(2,1)S(1)}, u32[]{:S(2)}, u32[]{:S(2)}) %collective-permute-start.3) | collective-permute-done | bytes 131104 | tf_op jit(solution)/shard_map/ppermute | solution.py:27
  19.6 2.4 %collective-permute-start.5 = (bf16[256,512]{1,0:T(8,128)(2,1)S(1)}, bf16[256,512]{1,0:T(8,128)(2,1)S(1)}, u32[]{:S(2)}, u32[]{:S(2)}) collective-permute-start(bf16[256,512]{1,0:T(8,128)(2,1)S(1)} %choose.3), channel_id=1, source_target_pairs={{0,4},{4,0},{8,12},{12,8},{16,20},{20,16},{24,28},{28,24},{32,36},... | collective-permute-start | bytes 786440 | tf_op jit(solution)/shard_map/ppermute | solution.py:27
  21.9 0.9 %collective-permute-done.1.four_ref.refs_7_ = bf16[256,256]{1,0:T(8,128)(2,1)S(1)} collective-permute-done((bf16[256,256]{1,0:T(8,128)(2,1)S(1)}, bf16[256,256]{1,0:T(8,128)(2,1)S(1)}, u32[]{:S(2)}, u32[]{:S(2)}) %collective-permute-start.1) | collective-permute-done | bytes 131104 | tf_op jit(solution)/shard_map/ppermute | solution.py:27
  22.8 5.2 %collective-permute-done.two_ref.refs_6_ = bf16[256,256]{1,0:T(8,128)(2,1)S(1)} collective-permute-done((bf16[256,256]{1,0:T(8,128)(2,1)S(1)}, bf16[256,256]{1,0:T(8,128)(2,1)S(1)}, u32[]{:S(2)}, u32[]{:S(2)}) %collective-permute-start) | collective-permute-done | bytes 131104 | tf_op jit(solution)/shard_map/ppermute | solution.py:27
  28.0 1.2 %collective-permute-start.2 = (bf16[256,512]{1,0:T(8,128)(2,1)S(1)}, bf16[256,512]{1,0:T(8,128)(2,1)S(1)}, u32[]{:S(2)}, u32[]{:S(2)}) collective-permute-start(bf16[256,512]{1,0:T(8,128)(2,1)S(1)} %choose.2), channel_id=1, source_target_pairs={{0,4},{4,0},{8,12},{12,8},{16,20},{20,16},{24,28},{28,24},{32,36},... | collective-permute-start | bytes 786440 | tf_op jit(solution)/shard_map/ppermute | solution.py:27
  29.2 1.2 %collective-permute-done.2.refs_8_ = bf16[256,512]{1,0:T(8,128)(2,1)S(1)} collective-permute-done((bf16[256,512]{1,0:T(8,128)(2,1)S(1)}, bf16[256,512]{1,0:T(8,128)(2,1)S(1)}, u32[]{:S(2)}, u32[]{:S(2)}) %collective-permute-start.2) | collective-permute-done | bytes 262176 | tf_op jit(solution)/shard_map/ppermute | solution.py:27
  30.4 16.6 %far.1 = (bf16[256,2048]{1,0:T(8,128)(2,1)}, bf16[256,2048]{1,0:T(8,128)(2,1)S(1)}, f32[256,128]{1,0:T(8,128)S(1)}, f32[256,512]{1,0:T(8,128)S(1)}, f32[256,512]...) custom-call(bf16[256,2048]{1,0:T(8,128)(2,1)S(1)} %copy-done.1, bf16[256,2048]{1,0:T(8,128)(2,1)S(1)} %copy-done.2, ...), custom_call_target="tpu_custom_call" | custom-call | flops 6442450944 | bytes 1048576 | tf_op jit(solution)/shard_map/far/pallas_call | solution.py:221
  47.0 1.0 %copy-done.6 = bf16[256,2048]{1,0:T(8,128)(2,1)} copy-done((bf16[256,2048]{1,0:T(8,128)(2,1)}, bf16[256,2048]{1,0:T(8,128)(2,1)S(1)}, u32[]{:S(2)}) %copy-start.6) | copy-done | bytes 1048600
  48.3 4.3 %all-to-all-start = ((bf16[4,64,2048]{2,1,0:T(8,128)(2,1)}), bf16[4,64,2048]{2,1,0:T(8,128)(2,1)}, u32[]{:S(2)}, u32[]{:S(2)}) async-start(bf16[4,64,2048]{2,1,0:T(8,128)(2,1)} %bitcast.1), calls=%async_computation | async-start | bytes 2097152 | tf_op jit(solution)/shard_map/all_to_all | solution.py:312
  52.7 2.4 %collective-permute-start.8 = (bf16[256,512]{1,0:T(8,128)(2,1)S(1)}, bf16[256,512]{1,0:T(8,128)(2,1)S(1)}, u32[]{:S(2)}, u32[]{:S(2)}) collective-permute-start(bf16[256,512]{1,0:T(8,128)(2,1)S(1)} %get-tuple-element.41), channel_id=1, source_target_pairs={{0,240},{4,244},{8,248},{12,252},{16,0},{20,4},{24,8},{28,12},{32,... | collective-permute-start | bytes 786440 | tf_op jit(solution)/shard_map/ppermute | solution.py:27
  55.1 0.8 %collective-permute-start.7 = (bf16[256,512]{1,0:T(8,128)(2,1)S(1)}, bf16[256,512]{1,0:T(8,128)(2,1)S(1)}, u32[]{:S(2)}, u32[]{:S(2)}) collective-permute-start(bf16[256,512]{1,0:T(8,128)(2,1)S(1)} %get-tuple-element.37), channel_id=1, source_target_pairs={{0,248},{4,252},{8,0},{12,4},{16,8},{20,12},{24,16},{28,20},{32,24... | collective-permute-start | bytes 786440 | tf_op jit(solution)/shard_map/ppermute | solution.py:27
  55.9 1.2 %copy-done.3 = bf16[256,2048]{1,0:T(8,128)(2,1)S(1)} copy-done((bf16[256,2048]{1,0:T(8,128)(2,1)S(1)}, bf16[256,2048]{1,0:T(8,128)(2,1)}, u32[]{:S(2)}) %copy-start.3) | copy-done | bytes 1048600
  57.1 1.2 %copy-done.7 = bf16[256,2048]{1,0:T(8,128)(2,1)S(1)} copy-done((bf16[256,2048]{1,0:T(8,128)(2,1)S(1)}, bf16[256,2048]{1,0:T(8,128)(2,1)}, u32[]{:S(2)}) %copy-start.7) | copy-done | bytes 1048600
  58.4 6.7 %own_backward.1 = (bf16[256,2048]{1,0:T(8,128)(2,1)}, f32[256,512]{1,0:T(8,128)S(1)}) custom-call(s32[32]{0:T(128)S(1)} %copy-done.5, s32[1]{0:T(128)} %bitcast.here.place, bf16[256,2048]{1,0:T(8,128)(2,1)S(1)} %copy-done.1, bf16[256,2048]{1,0:T(8,128)(2,1)S(1)} %copy-done.3, bf16[256,2048]{1,0:T(8,128)(2,1)S(1)} %copy-done.7, ...), custom_call_target="tpu_custom_call" | custom-call | flops 1073741824 | bytes 1048576 | tf_op jit(solution)/shard_map/own_backward/pallas_call | solution.py:221
  65.0 2.4 %all-to-all-done = bf16[4,64,2048]{2,1,0:T(8,128)(2,1)} async-done(((bf16[4,64,2048]{2,1,0:T(8,128)(2,1)}), bf16[4,64,2048]{2,1,0:T(8,128)(2,1)}, u32[]{:S(2)}, u32[]{:S(2)}) %all-to-all-start) | async-done | bytes 1048608 | tf_op jit(solution)/shard_map/all_to_all | solution.py:312
  67.4 2.3 %copy.10 = bf16[4,8,8,2048]{3,2,0,1:T(8,128)(2,1)} copy(bf16[4,8,8,2048]{3,2,1,0:T(8,128)(2,1)} %bitcast.3) | data formatting | bytes 2097152 | tf_op jit(solution)/shard_map/reshape | solution.py:342
  69.7 2.6 %collective-permute-done.7.two_ref = bf16[256,512]{1,0:T(8,128)(2,1)S(1)} collective-permute-done((bf16[256,512]{1,0:T(8,128)(2,1)S(1)}, bf16[256,512]{1,0:T(8,128)(2,1)S(1)}, u32[]{:S(2)}, u32[]{:S(2)}) %collective-permute-start.7) | collective-permute-done | bytes 262176 | tf_op jit(solution)/shard_map/ppermute | solution.py:27
  72.4 0.8 %total.1 = (bf16[256,256]{1,0:T(8,128)(2,1)}, bf16[256,256]{1,0:T(8,128)(2,1)}) custom-call(s32[1]{0:T(128)} %bitcast.here.place, f32[256,512]{1,0:T(8,128)S(1)} %get-tuple-element.40.own_ref, bf16[256,1024]{1,0:T(8,128)(2,1)S(1)} %collective-permute-done.6.other_ref, bf16[256,512]{1,0:T(8,128)(2,1)S(1)} %collective-permute-done.7.two_ref, ...), custom_call_target="tpu_custom_call" | custom-call | bytes 1048576 | tf_op jit(solution)/shard_map/total/pallas_call | solution.py:221
  (23 shorter events, 2.0 us)
Async XLA Ops:
  0.6 29.7 %copy-start.1 = (bf16[256,2048]{1,0:T(8,128)(2,1)S(1)}, bf16[256,2048]{1,0:T(8,128)(2,1)}, u32[]{:S(2)}) copy-start(bf16[256,2048]{1,0:T(8,128)(2,1)} %q_ref.3) | copy-start | bytes 3145732
  1.7 14.9 %collective-permute-start.4 = (bf16[256,256]{1,0:T(8,128)(2,1)S(1)}, bf16[256,256]{1,0:T(8,128)(2,1)S(1)}, u32[]{:S(2)}, u32[]{:S(2)}) collective-permute-start(bf16[256,256]{1,0:T(8,128)(2,1)S(1)} %pad_maximum_fusion.1.refs_1_.own_ref), channel_id=1, source_target_pairs={{0,16},{4,20},{8,24},{12,28},{16,32},{20,36},{24,40},{28,44},{32,4... | collective-permute-start | bytes 393224 | tf_op jit(solution)/shard_map/ppermute | solution.py:27
  5.6 13.9 %collective-permute-start.3 = (bf16[256,256]{1,0:T(8,128)(2,1)S(1)}, bf16[256,256]{1,0:T(8,128)(2,1)S(1)}, u32[]{:S(2)}, u32[]{:S(2)}) collective-permute-start(bf16[256,256]{1,0:T(8,128)(2,1)S(1)} %pad_maximum_fusion.1.refs_1_.own_ref), channel_id=1, source_target_pairs={{0,8},{4,12},{8,16},{12,20},{16,24},{20,28},{24,32},{28,36},{32,40... | collective-permute-start | bytes 393224 | tf_op jit(solution)/shard_map/ppermute | solution.py:27
  7.3 15.6 %collective-permute-start.1 = (bf16[256,256]{1,0:T(8,128)(2,1)S(1)}, bf16[256,256]{1,0:T(8,128)(2,1)S(1)}, u32[]{:S(2)}, u32[]{:S(2)}) collective-permute-start(bf16[256,256]{1,0:T(8,128)(2,1)S(1)} %pad_maximum_fusion.refs_0_.own_ref), channel_id=1, source_target_pairs={{0,16},{4,20},{8,24},{12,28},{16,32},{20,36},{24,40},{28,44},{32,4... | collective-permute-start | bytes 393224 | tf_op jit(solution)/shard_map/ppermute | solution.py:27
  10.6 17.3 %collective-permute-start = (bf16[256,256]{1,0:T(8,128)(2,1)S(1)}, bf16[256,256]{1,0:T(8,128)(2,1)S(1)}, u32[]{:S(2)}, u32[]{:S(2)}) collective-permute-start(bf16[256,256]{1,0:T(8,128)(2,1)S(1)} %pad_maximum_fusion.refs_0_.own_ref), channel_id=1, source_target_pairs={{0,8},{4,12},{8,16},{12,20},{16,24},{20,28},{24,32},{28,36},{32,40... | collective-permute-start | bytes 393224 | tf_op jit(solution)/shard_map/ppermute | solution.py:27
  11.4 1.2 %copy-start = (bf16[256,2048]{1,0:T(8,128)(2,1)S(1)}, bf16[256,2048]{1,0:T(8,128)(2,1)}, u32[]{:S(2)}) copy-start(bf16[256,2048]{1,0:T(8,128)(2,1)} %q_ref.3) | copy-start | bytes 3145732
  12.6 0.7 copy-start.4
  13.3 17.1 %copy-start.2 = (bf16[256,2048]{1,0:T(8,128)(2,1)S(1)}, bf16[256,2048]{1,0:T(8,128)(2,1)}, u32[]{:S(2)}) copy-start(bf16[256,2048]{1,0:T(8,128)(2,1)} %g_ref.1) | copy-start | bytes 3145732
  19.6 9.6 %collective-permute-start.5 = (bf16[256,512]{1,0:T(8,128)(2,1)S(1)}, bf16[256,512]{1,0:T(8,128)(2,1)S(1)}, u32[]{:S(2)}, u32[]{:S(2)}) collective-permute-start(bf16[256,512]{1,0:T(8,128)(2,1)S(1)} %choose.3), channel_id=1, source_target_pairs={{0,4},{4,0},{8,12},{12,8},{16,20},{20,16},{24,28},{28,24},{32,36},... | collective-permute-start | bytes 786440 | tf_op jit(solution)/shard_map/ppermute | solution.py:27
  28.0 2.4 %collective-permute-start.2 = (bf16[256,512]{1,0:T(8,128)(2,1)S(1)}, bf16[256,512]{1,0:T(8,128)(2,1)S(1)}, u32[]{:S(2)}, u32[]{:S(2)}) collective-permute-start(bf16[256,512]{1,0:T(8,128)(2,1)S(1)} %choose.2), channel_id=1, source_target_pairs={{0,4},{4,0},{8,12},{12,8},{16,20},{20,16},{24,28},{28,24},{32,36},... | collective-permute-start | bytes 786440 | tf_op jit(solution)/shard_map/ppermute | solution.py:27
  47.0 1.0 %copy-start.6 = (bf16[256,2048]{1,0:T(8,128)(2,1)}, bf16[256,2048]{1,0:T(8,128)(2,1)S(1)}, u32[]{:S(2)}) copy-start(bf16[256,2048]{1,0:T(8,128)(2,1)S(1)} %get-tuple-element.32.far_ref) | copy-start | bytes 3145732
  47.9 8.0 %copy-start.5 = (s32[32]{0:T(128)S(1)}, s32[32]{0:T(128)}, u32[]{:S(2)}) copy-start(s32[32]{0:T(128)} %lens.3) | copy-start | bytes 388
  47.9 4.6 %collective-permute-start.6 = (bf16[256,1024]{1,0:T(8,128)(2,1)S(1)}, bf16[256,1024]{1,0:T(8,128)(2,1)S(1)}, u32[]{:S(2)}, u32[]{:S(2)}) collective-permute-start(bf16[256,1024]{1,0:T(8,128)(2,1)S(1)} %get-tuple-element.36), channel_id=1, source_target_pairs={{0,4},{4,0},{8,12},{12,8},{16,20},{20,16},{24,28},{28,24},{32,36},... | collective-permute-start | bytes 1572872 | tf_op jit(solution)/shard_map/ppermute | solution.py:27
  48.3 19.1 %all-to-all-start = ((bf16[4,64,2048]{2,1,0:T(8,128)(2,1)}), bf16[4,64,2048]{2,1,0:T(8,128)(2,1)}, u32[]{:S(2)}, u32[]{:S(2)}) async-start(bf16[4,64,2048]{2,1,0:T(8,128)(2,1)} %bitcast.1), calls=%async_computation | async-start | bytes 2097152 | tf_op jit(solution)/shard_map/all_to_all | solution.py:312
  52.7 17.1 %collective-permute-start.8 = (bf16[256,512]{1,0:T(8,128)(2,1)S(1)}, bf16[256,512]{1,0:T(8,128)(2,1)S(1)}, u32[]{:S(2)}, u32[]{:S(2)}) collective-permute-start(bf16[256,512]{1,0:T(8,128)(2,1)S(1)} %get-tuple-element.41), channel_id=1, source_target_pairs={{0,240},{4,244},{8,248},{12,252},{16,0},{20,4},{24,8},{28,12},{32,... | collective-permute-start | bytes 786440 | tf_op jit(solution)/shard_map/ppermute | solution.py:27
  55.1 17.2 %collective-permute-start.7 = (bf16[256,512]{1,0:T(8,128)(2,1)S(1)}, bf16[256,512]{1,0:T(8,128)(2,1)S(1)}, u32[]{:S(2)}, u32[]{:S(2)}) collective-permute-start(bf16[256,512]{1,0:T(8,128)(2,1)S(1)} %get-tuple-element.37), channel_id=1, source_target_pairs={{0,248},{4,252},{8,0},{12,4},{16,8},{20,12},{24,16},{28,20},{32,24... | collective-permute-start | bytes 786440 | tf_op jit(solution)/shard_map/ppermute | solution.py:27
  55.9 1.2 %copy-start.3 = (bf16[256,2048]{1,0:T(8,128)(2,1)S(1)}, bf16[256,2048]{1,0:T(8,128)(2,1)}, u32[]{:S(2)}) copy-start(bf16[256,2048]{1,0:T(8,128)(2,1)} %g_ref.1) | copy-start | bytes 3145732
  57.1 1.2 %copy-start.7 = (bf16[256,2048]{1,0:T(8,128)(2,1)S(1)}, bf16[256,2048]{1,0:T(8,128)(2,1)}, u32[]{:S(2)}) copy-start(bf16[256,2048]{1,0:T(8,128)(2,1)} %copy-done.6) | copy-start | bytes 3145732

commit v5 on v4

--- a/solution.py
+++ b/solution.py
@@ -60,24 +60,25 @@
     return jnp.concatenate([mask(start, -at) for at in range(0, rows, width)], axis=1)
 
 
-def own_forward_kernel(scale, lens, here, q_ref, *refs):
-    out_ref, top_ref, sum_ref, far_ref = refs[-4:]
+def own_forward_kernel(
+    scale, lens, here, q_ref, k_ref, v_ref, out_ref, top_ref, sum_ref, far_ref
+):
     rows, width = q_ref.shape[0], HEAD_WIDTH
     start = first_seen(lens, here, rows, width)
     for at in range(0, REACH * rows, width):
         far_ref[:, at : at + width] = mask(start, REACH * rows - at)
     near = near_mask(start, rows)
-    groups = len(refs) - 4
     heads = q_ref.shape[1] // width
+    share = q_ref.shape[1] // k_ref.shape[1]
     for h in range(heads):
         at = slice(h * width, (h + 1) * width)
-        pack = refs[h * groups // heads]
-        s = dot_t(q_ref[:, at], pack[:, :width]) + near
+        kv = slice(h // share * width, (h // share + 1) * width)
+        s = dot_t(q_ref[:, at], k_ref[:, kv]) + near
         top = s.max(axis=1, keepdims=True)
         p = jnp.exp2((s - top) * (scale * LOG2E))
         top_ref[:, at] = jnp.broadcast_to(top, (rows, width))
         sum_ref[:, at] = jnp.broadcast_to(p.sum(axis=1, keepdims=True), (rows, width))
-        out_ref[:, at] = dot(p.astype(jnp.bfloat16), pack[:, width:])
+        out_ref[:, at] = dot(p.astype(jnp.bfloat16), v_ref[:, kv])
 
 
 def far_kernel(scale, *refs):
@@ -86,17 +87,17 @@
     k_all, v_all, o_ref, dq_ref, keep_ref, sent = refs[-6:]
     fars = refs[6:-12]
     rows, width = q_ref.shape[0], HEAD_WIDTH
-    groups = len(fars) // 3
+    groups = k_all.shape[0]
     heads = q_ref.shape[1] // width
     share = heads // groups
     factor = scale * LOG2E
     bias = bias_ref[...]
-    for n in range(groups):
-        two_ref, four_ref, odd_ref = fars[3 * n : 3 * n + 3]
+    for which, to in enumerate((k_all, v_all)):
+        two_ref, four_ref, odd_ref = fars[3 * which : 3 * which + 3]
         for b, (ref, place) in enumerate(((four_ref, 0), (odd_ref, 1), (two_ref, 0), (odd_ref, 0))):
-            at = slice(b * rows, (b + 1) * rows)
-            k_all[n, at, :] = ref[:, 2 * place * width : (2 * place + 1) * width]
-            v_all[n, at, :] = ref[:, (2 * place + 1) * width : (2 * place + 2) * width]
+            for n in range(groups):
+                column = (groups * place + n) * width
+                to[n, b * rows : (b + 1) * rows, :] = ref[:, column : column + width]
 
     def weigh(h):
         at = slice(h * width, (h + 1) * width)
@@ -147,18 +148,19 @@
             copy.wait()
 
 
-def own_backward_kernel(scale, lens, here, q_ref, g_ref, far_ref, keep_ref, *refs):
-    dq_ref, own_ref = refs[-2:]
+def own_backward_kernel(
+    scale, lens, here, q_ref, g_ref, far_ref, keep_ref, k_ref, v_ref, dq_ref, own_ref
+):
     rows, width = q_ref.shape[0], HEAD_WIDTH
-    groups = len(refs) - 2
     heads = q_ref.shape[1] // width
-    share = heads // groups
+    share = q_ref.shape[1] // k_ref.shape[1]
     factor = scale * LOG2E
     bias = near_mask(first_seen(lens, here, rows, width), rows)
     for h in range(heads):
         n = h // share
-        k, v = refs[n][:, :width], refs[n][:, width:]
         at = slice(h * width, (h + 1) * width)
+        kv = slice(n * width, (n + 1) * width)
+        k, v = k_ref[:, kv], v_ref[:, kv]
         q, g = q_ref[:, at], g_ref[:, at]
         p = jnp.exp2((dot_t(q, k) + bias) * factor - keep_ref[:, h : h + 1])
         ds = (p * (dot_t(g, v) - keep_ref[:, heads + h : heads + h + 1])).astype(jnp.bfloat16)
@@ -222,7 +224,10 @@
         functools.partial(kernel, 1.0 / math.sqrt(HEAD_WIDTH)),
         in_specs=[pl.BlockSpec(memory_space=pltpu.SMEM)] * scalars + [whole] * (len(args) - scalars),
         out_specs=[left if i in hbm else whole for i in range(len(outs))],
-        out_shape=[jax.ShapeDtypeStruct(shape, dtype) for shape, dtype in outs],
+        out_shape=[
+            pltpu.HBM(shape, dtype) if i in hbm else jax.ShapeDtypeStruct(shape, dtype)
+            for i, (shape, dtype) in enumerate(outs)
+        ],
         scratch_shapes=scratch,
         compiler_params=pltpu.CompilerParams(vmem_limit_bytes=20 << 20),
         cost_estimate=pl.CostEstimate(
@@ -239,13 +244,10 @@
     wide = 2 * groups * width
     place = lax.axis_index("seq")
     here = place.reshape(1).astype(jnp.int32)
-    packs, twos, fours, fars = [], [], [], []
-    for n in range(groups):
-        at = slice(n * width, (n + 1) * width)
-        packs.append(jnp.concatenate((keys[:, at], values[:, at]), axis=1))
-    for pack in packs:
-        twos.append(up(pack, 2))
-        fours.append(up(pack, 4))
+    twos, fours, fars = [], [], []
+    for own in (keys, values):
+        twos.append(up(own, 2))
+        fours.append(up(own, 4))
     parts, top, total, bias = call(
         own_forward_kernel,
         "own_forward",
@@ -254,18 +256,19 @@
         lengths,
         here,
         queries,
-        *packs,
+        keys,
+        values,
         scalars=2,
     )
-    packs, bias = lax.optimization_barrier((packs, bias))
-    for pack, two, four in zip(packs, twos, fours):
+    near_keys, near_values, bias = lax.optimization_barrier((keys, values, bias))
+    for own, two, four in zip((near_keys, near_values), twos, fours):
         send = call(
             choose_kernel,
             "choose",
             0,
-            [((rows, 4 * width), jnp.bfloat16)],
+            [((rows, wide), jnp.bfloat16)],
             here,
-            pack,
+            own,
             two,
             four,
             scalars=1,
@@ -324,7 +327,8 @@
         output_gradient,
         dq_far,
         keep,
-        *packs,
+        keys,
+        values,
         scalars=2,
     )
     key_gradient, value_gradient = call(

time: 73.5 us -> 72 us (0.980)
  waiting for transfers between devices: 15.2 us -> 9.31 us
  starting transfers between devices: 21 us -> 25.5 us
    ppermute x9, starting transfers between devices: 16.8 us -> 21.3 us  [moved(): lax.ppermute(value, 'seq', [(source, to(source) % count) for source in ra...]
    ppermute x9, waiting for transfers between devices: 12.8 us -> 8.55 us  [moved(): lax.ppermute(value, 'seq', [(source, to(source) % count) for source in ra...]
    all_to_all x1, waiting for transfers between devices: 2.41 us -> 0.77 us  [on_device(): lax.all_to_all(out.reshape(split, rows // split, out.shape[1]), 'head', s...]
    slice x1 -> x0, local copies, waits for them, and re-layouts: 1.04 us -> none  [on_device(): packs.append(jnp.concatenate((keys[:, at], values[:, at]), axis=1))]
    unnamed x16 -> x24, local copies, waits for them, and re-layouts: 5.31 us -> 6.2 us
  transfers between devices with their start and end apart: 10 -> 10, of which waited for: 6 -> 4; matrix products, arithmetic and copies ran while one was open for 3% -> 3% of each run, Pallas kernels for 14% -> 14%
where the time goes in v5:
time: 72 us; the launch traced here: 71.6 us
  Pallas kernels  27.6 us (38%)
  starting transfers between devices  25.5 us (35%)
  waiting for transfers between devices  9.31 us (13%)
  local copies, waits for them, and re-layouts  8.5 us (12%)
  between operations  0.76 us (1%)
    pallas_call x7, Pallas kernels, call(): pl.pallas_call(functools.partial(kernel, 1.0 / math.sqrt(HEAD_WIDTH)), in...  27.6 us
    ppermute x9, starting transfers between devices, moved(): lax.ppermute(value, 'seq', [(source, to(source) % count) for source in ra...  21.3 us
    ppermute x9, waiting for transfers between devices, moved(): lax.ppermute(value, 'seq', [(source, to(source) % count) for source in ra...  8.55 us
    unnamed x24, local copies, waits for them, and re-layouts  6.2 us
    all_to_all x1, starting transfers between devices, on_device(): lax.all_to_all(out.reshape(split, rows // split, out.shape[1]), 'head', s...  4.24 us
    reshape x1, local copies, waits for them, and re-layouts, on_device(): attn_out = jnp.transpose(got, (1, 0, 2)).reshape(got.shape[1], -1)  2.3 us
  transfers between devices with their start and end apart: 10, of which 4 were waited for; matrix products, arithmetic and copies ran while one was open for 3% of the time, Pallas kernels for 14%

profile of v5, /device:TPU:1, one launch (start us, length us, event | category | flops | bytes accessed | tf_op | source)
XLA Modules:
  0.0 71.6 jit_solution(2089190071842622001)
XLA Ops:
  0.6 2.5 %collective-permute-start.3 = (bf16[256,256]{1,0:T(8,128)(2,1)}, bf16[256,256]{1,0:T(8,128)(2,1)S(1)}, u32[]{:S(2)}, u32[]{:S(2)}) collective-permute-start(bf16[256,256]{1,0:T(8,128)(2,1)} %v_ref.3), channel_id=1, source_target_pairs={{0,8},{4,12},{8,16},{12,20},{16,24},{20,28},{24,32},{28,36},{32,40... | collective-permute-start | bytes 393224 | tf_op jit(solution)/shard_map/ppermute | solution.py:27
  3.2 3.0 %collective-permute-start.4 = (bf16[256,256]{1,0:T(8,128)(2,1)}, bf16[256,256]{1,0:T(8,128)(2,1)S(1)}, u32[]{:S(2)}, u32[]{:S(2)}) collective-permute-start(bf16[256,256]{1,0:T(8,128)(2,1)} %v_ref.3), channel_id=1, source_target_pairs={{0,16},{4,20},{8,24},{12,28},{16,32},{20,36},{24,40},{28,44},{32,4... | collective-permute-start | bytes 393224 | tf_op jit(solution)/shard_map/ppermute | solution.py:27
  6.2 2.8 %collective-permute-start = (bf16[256,256]{1,0:T(8,128)(2,1)}, bf16[256,256]{1,0:T(8,128)(2,1)S(1)}, u32[]{:S(2)}, u32[]{:S(2)}) collective-permute-start(bf16[256,256]{1,0:T(8,128)(2,1)} %k_ref.3), channel_id=1, source_target_pairs={{0,8},{4,12},{8,16},{12,20},{16,24},{20,28},{24,32},{28,36},{32,40... | collective-permute-start | bytes 393224 | tf_op jit(solution)/shard_map/ppermute | solution.py:27
  9.0 1.2 %collective-permute-start.1 = (bf16[256,256]{1,0:T(8,128)(2,1)}, bf16[256,256]{1,0:T(8,128)(2,1)S(1)}, u32[]{:S(2)}, u32[]{:S(2)}) collective-permute-start(bf16[256,256]{1,0:T(8,128)(2,1)} %k_ref.3), channel_id=1, source_target_pairs={{0,16},{4,20},{8,24},{12,28},{16,32},{20,36},{24,40},{28,44},{32,4... | collective-permute-start | bytes 393224 | tf_op jit(solution)/shard_map/ppermute | solution.py:27
  10.2 0.9 %copy-done = bf16[256,256]{1,0:T(8,128)(2,1)S(1)} copy-done((bf16[256,256]{1,0:T(8,128)(2,1)S(1)}, bf16[256,256]{1,0:T(8,128)(2,1)}, u32[]{:S(2)}) %copy-start) | copy-done | bytes 131096
  11.1 0.9 %copy-done.2 = bf16[256,256]{1,0:T(8,128)(2,1)S(1)} copy-done((bf16[256,256]{1,0:T(8,128)(2,1)S(1)}, bf16[256,256]{1,0:T(8,128)(2,1)}, u32[]{:S(2)}) %copy-start.2) | copy-done | bytes 131096
  12.1 1.2 %copy-done.4 = bf16[256,2048]{1,0:T(8,128)(2,1)S(1)} copy-done((bf16[256,2048]{1,0:T(8,128)(2,1)S(1)}, bf16[256,2048]{1,0:T(8,128)(2,1)}, u32[]{:S(2)}) %copy-start.4) | copy-done | bytes 1048600
  13.3 0.7 copy-done.8
  13.9 3.5 %own_forward.1 = (f32[256,2048]{1,0:T(8,128)S(1)}, f32[256,2048]{1,0:T(8,128)S(1)}, f32[256,2048]{1,0:T(8,128)S(1)}, f32[256,1024]{1,0:T(8,128)S(1)}) custom-call(s32[32]{0:T(128)S(1)} %copy-done.8, s32[1]{0:T(128)} %bitcast.here.place, bf16[256,2048]{1,0:T(8,128)(2,1)S(1)} %copy-done.4, bf16[256,256]{1,0:T(8,128)(2,1)S(1)} %copy-done, ...), custom_call_target="tpu_custom_call" | custom-call | flops 536870912 | bytes 1048576 | tf_op jit(solution)/shard_map/own_forward/pallas_call | solution.py:223
  17.5 4.3 %collective-permute-start.5 = (bf16[256,512]{1,0:T(8,128)(2,1)S(1)}, bf16[256,512]{1,0:T(8,128)(2,1)S(1)}, u32[]{:S(2)}, u32[]{:S(2)}) collective-permute-start(bf16[256,512]{1,0:T(8,128)(2,1)S(1)} %choose.3), channel_id=1, source_target_pairs={{0,4},{4,0},{8,12},{12,8},{16,20},{20,16},{24,28},{28,24},{32,36},... | collective-permute-start | bytes 786440 | tf_op jit(solution)/shard_map/ppermute | solution.py:27
  21.7 4.0 %collective-permute-done.1.four_ref.refs_7_ = bf16[256,256]{1,0:T(8,128)(2,1)S(1)} collective-permute-done((bf16[256,256]{1,0:T(8,128)(2,1)}, bf16[256,256]{1,0:T(8,128)(2,1)S(1)}, u32[]{:S(2)}, u32[]{:S(2)}) %collective-permute-start.1) | collective-permute-done | bytes 131104 | tf_op jit(solution)/shard_map/ppermute | solution.py:27
  25.7 1.9 %collective-permute-start.2 = (bf16[256,512]{1,0:T(8,128)(2,1)S(1)}, bf16[256,512]{1,0:T(8,128)(2,1)S(1)}, u32[]{:S(2)}, u32[]{:S(2)}) collective-permute-start(bf16[256,512]{1,0:T(8,128)(2,1)S(1)} %choose.2), channel_id=1, source_target_pairs={{0,4},{4,0},{8,12},{12,8},{16,20},{20,16},{24,28},{28,24},{32,36},... | collective-permute-start | bytes 786440 | tf_op jit(solution)/shard_map/ppermute | solution.py:27
  27.6 1.2 %collective-permute-done.2.refs_8_ = bf16[256,512]{1,0:T(8,128)(2,1)S(1)} collective-permute-done((bf16[256,512]{1,0:T(8,128)(2,1)S(1)}, bf16[256,512]{1,0:T(8,128)(2,1)S(1)}, u32[]{:S(2)}, u32[]{:S(2)}) %collective-permute-start.2) | collective-permute-done | bytes 262176 | tf_op jit(solution)/shard_map/ppermute | solution.py:27
  28.7 16.7 %far.1 = (bf16[256,2048]{1,0:T(8,128)(2,1)}, bf16[256,2048]{1,0:T(8,128)(2,1)}, f32[256,128]{1,0:T(8,128)}, f32[256,512]{1,0:T(8,128)S(1)}, f32[256,512]{1,0:T(8,128)S(1)}, /*index=5*/bf16[256,1024]{1,0:T(8,128)(2,1)S(1)}) custom-call(bf16[256,2048]{1,0:T(8,128)(2,1)S(1)} %copy-done.5, bf16[256,2048]{1,0:T(8,128)(2,1)S(1)} %copy-done.6, ...), custom_call_target="tpu_custom_call" | custom-call | flops 6442450944 | bytes 1048576 | tf_op jit(solution)/shard_map/far/pallas_call | solution.py:223
  46.0 4.2 %all-to-all-start = ((bf16[4,64,2048]{2,1,0:T(8,128)(2,1)}), bf16[4,64,2048]{2,1,0:T(8,128)(2,1)}, u32[]{:S(2)}, u32[]{:S(2)}) async-start(bf16[4,64,2048]{2,1,0:T(8,128)(2,1)} %bitcast.5), calls=%async_computation | async-start | bytes 2097152 | tf_op jit(solution)/shard_map/all_to_all | solution.py:315
  50.4 1.0 %collective-permute-start.8 = (bf16[256,512]{1,0:T(8,128)(2,1)S(1)}, bf16[256,512]{1,0:T(8,128)(2,1)S(1)}, u32[]{:S(2)}, u32[]{:S(2)}) collective-permute-start(bf16[256,512]{1,0:T(8,128)(2,1)S(1)} %get-tuple-element.41), channel_id=1, source_target_pairs={{0,240},{4,244},{8,248},{12,252},{16,0},{20,4},{24,8},{28,12},{32,... | collective-permute-start | bytes 786440 | tf_op jit(solution)/shard_map/ppermute | solution.py:27
  51.4 4.1 %collective-permute-start.7 = (bf16[256,512]{1,0:T(8,128)(2,1)S(1)}, bf16[256,512]{1,0:T(8,128)(2,1)S(1)}, u32[]{:S(2)}, u32[]{:S(2)}) collective-permute-start(bf16[256,512]{1,0:T(8,128)(2,1)S(1)} %get-tuple-element.37), channel_id=1, source_target_pairs={{0,248},{4,252},{8,0},{12,4},{16,8},{20,12},{24,16},{28,20},{32,24... | collective-permute-start | bytes 786440 | tf_op jit(solution)/shard_map/ppermute | solution.py:27
  55.5 1.2 %copy-done.7 = bf16[256,2048]{1,0:T(8,128)(2,1)S(1)} copy-done((bf16[256,2048]{1,0:T(8,128)(2,1)S(1)}, bf16[256,2048]{1,0:T(8,128)(2,1)}, u32[]{:S(2)}) %copy-start.7) | copy-done | bytes 1048600
  56.7 1.2 %copy-done.10 = bf16[256,2048]{1,0:T(8,128)(2,1)S(1)} copy-done((bf16[256,2048]{1,0:T(8,128)(2,1)S(1)}, bf16[256,2048]{1,0:T(8,128)(2,1)}, u32[]{:S(2)}) %copy-start.10) | copy-done | bytes 1048600
  57.9 6.4 %own_backward.1 = (bf16[256,2048]{1,0:T(8,128)(2,1)}, f32[256,512]{1,0:T(8,128)S(1)}) custom-call(s32[32]{0:T(128)S(1)} %copy-done.9, s32[1]{0:T(128)} %bitcast.here.place, bf16[256,2048]{1,0:T(8,128)(2,1)S(1)} %copy-done.5, bf16[256,2048]{1,0:T(8,128)(2,1)S(1)} %copy-done.7, bf16[256,2048]{1,0:T(8,128)(2,1)S(1)} %copy-done.10, f32[256,128]{1,0:T(8,128)S(1)} %copy-done.11, ...), custom_call_target="tpu_custom_call" | custom-call | flops 1073741824 | bytes 1048576 | tf_op jit(solution)/shard_map/own_backward/pallas_call | solution.py:223
  64.3 0.8 %all-to-all-done = bf16[4,64,2048]{2,1,0:T(8,128)(2,1)} async-done(((bf16[4,64,2048]{2,1,0:T(8,128)(2,1)}), bf16[4,64,2048]{2,1,0:T(8,128)(2,1)}, u32[]{:S(2)}, u32[]{:S(2)}) %all-to-all-start) | async-done | bytes 1048608 | tf_op jit(solution)/shard_map/all_to_all | solution.py:315
  65.1 2.3 %copy.10 = bf16[4,8,8,2048]{3,2,0,1:T(8,128)(2,1)} copy(bf16[4,8,8,2048]{3,2,1,0:T(8,128)(2,1)} %bitcast.3) | data formatting | bytes 2097152 | tf_op jit(solution)/shard_map/reshape | solution.py:346
  67.4 3.4 %collective-permute-done.7.two_ref = bf16[256,512]{1,0:T(8,128)(2,1)S(1)} collective-permute-done((bf16[256,512]{1,0:T(8,128)(2,1)S(1)}, bf16[256,512]{1,0:T(8,128)(2,1)S(1)}, u32[]{:S(2)}, u32[]{:S(2)}) %collective-permute-start.7) | collective-permute-done | bytes 262176 | tf_op jit(solution)/shard_map/ppermute | solution.py:27
  70.8 0.8 %total.1 = (bf16[256,256]{1,0:T(8,128)(2,1)}, bf16[256,256]{1,0:T(8,128)(2,1)}) custom-call(s32[1]{0:T(128)} %bitcast.here.place, f32[256,512]{1,0:T(8,128)S(1)} %get-tuple-element.40.own_ref, bf16[256,1024]{1,0:T(8,128)(2,1)S(1)} %collective-permute-done.6.other_ref, bf16[256,512]{1,0:T(8,128)(2,1)S(1)} %collective-permute-done.7.two_ref, ...), custom_call_target="tpu_custom_call" | custom-call | bytes 1048576 | tf_op jit(solution)/shard_map/total/pallas_call | solution.py:223
  (28 shorter events, 0.7 us)
Async XLA Ops:
  0.6 16.8 %collective-permute-start.3 = (bf16[256,256]{1,0:T(8,128)(2,1)}, bf16[256,256]{1,0:T(8,128)(2,1)S(1)}, u32[]{:S(2)}, u32[]{:S(2)}) collective-permute-start(bf16[256,256]{1,0:T(8,128)(2,1)} %v_ref.3), channel_id=1, source_target_pairs={{0,8},{4,12},{8,16},{12,20},{16,24},{20,28},{24,32},{28,36},{32,40... | collective-permute-start | bytes 393224 | tf_op jit(solution)/shard_map/ppermute | solution.py:27
  3.2 14.2 %collective-permute-start.4 = (bf16[256,256]{1,0:T(8,128)(2,1)}, bf16[256,256]{1,0:T(8,128)(2,1)S(1)}, u32[]{:S(2)}, u32[]{:S(2)}) collective-permute-start(bf16[256,256]{1,0:T(8,128)(2,1)} %v_ref.3), channel_id=1, source_target_pairs={{0,16},{4,20},{8,24},{12,28},{16,32},{20,36},{24,40},{28,44},{32,4... | collective-permute-start | bytes 393224 | tf_op jit(solution)/shard_map/ppermute | solution.py:27
  6.2 15.6 %collective-permute-start = (bf16[256,256]{1,0:T(8,128)(2,1)}, bf16[256,256]{1,0:T(8,128)(2,1)S(1)}, u32[]{:S(2)}, u32[]{:S(2)}) collective-permute-start(bf16[256,256]{1,0:T(8,128)(2,1)} %k_ref.3), channel_id=1, source_target_pairs={{0,8},{4,12},{8,16},{12,20},{16,24},{20,28},{24,32},{28,36},{32,40... | collective-permute-start | bytes 393224 | tf_op jit(solution)/shard_map/ppermute | solution.py:27
  9.0 16.7 %collective-permute-start.1 = (bf16[256,256]{1,0:T(8,128)(2,1)}, bf16[256,256]{1,0:T(8,128)(2,1)S(1)}, u32[]{:S(2)}, u32[]{:S(2)}) collective-permute-start(bf16[256,256]{1,0:T(8,128)(2,1)} %k_ref.3), channel_id=1, source_target_pairs={{0,16},{4,20},{8,24},{12,28},{16,32},{20,36},{24,40},{28,44},{32,4... | collective-permute-start | bytes 393224 | tf_op jit(solution)/shard_map/ppermute | solution.py:27
  10.2 0.9 %copy-start = (bf16[256,256]{1,0:T(8,128)(2,1)S(1)}, bf16[256,256]{1,0:T(8,128)(2,1)}, u32[]{:S(2)}) copy-start(bf16[256,256]{1,0:T(8,128)(2,1)} %k_ref.3) | copy-start | bytes 393220
  11.1 0.9 %copy-start.2 = (bf16[256,256]{1,0:T(8,128)(2,1)S(1)}, bf16[256,256]{1,0:T(8,128)(2,1)}, u32[]{:S(2)}) copy-start(bf16[256,256]{1,0:T(8,128)(2,1)} %v_ref.3) | copy-start | bytes 393220
  12.1 1.2 %copy-start.4 = (bf16[256,2048]{1,0:T(8,128)(2,1)S(1)}, bf16[256,2048]{1,0:T(8,128)(2,1)}, u32[]{:S(2)}) copy-start(bf16[256,2048]{1,0:T(8,128)(2,1)} %q_ref.3) | copy-start | bytes 3145732
  13.3 0.7 copy-start.8
  13.9 14.8 %copy-start.5 = (bf16[256,2048]{1,0:T(8,128)(2,1)S(1)}, bf16[256,2048]{1,0:T(8,128)(2,1)}, u32[]{:S(2)}) copy-start(bf16[256,2048]{1,0:T(8,128)(2,1)} %q_ref.3) | copy-start | bytes 3145732
  13.9 14.8 %copy-start.6 = (bf16[256,2048]{1,0:T(8,128)(2,1)S(1)}, bf16[256,2048]{1,0:T(8,128)(2,1)}, u32[]{:S(2)}) copy-start(bf16[256,2048]{1,0:T(8,128)(2,1)} %g_ref.1) | copy-start | bytes 3145732
  17.5 10.1 %collective-permute-start.5 = (bf16[256,512]{1,0:T(8,128)(2,1)S(1)}, bf16[256,512]{1,0:T(8,128)(2,1)S(1)}, u32[]{:S(2)}, u32[]{:S(2)}) collective-permute-start(bf16[256,512]{1,0:T(8,128)(2,1)S(1)} %choose.3), channel_id=1, source_target_pairs={{0,4},{4,0},{8,12},{12,8},{16,20},{20,16},{24,28},{28,24},{32,36},... | collective-permute-start | bytes 786440 | tf_op jit(solution)/shard_map/ppermute | solution.py:27
  25.7 3.0 %collective-permute-start.2 = (bf16[256,512]{1,0:T(8,128)(2,1)S(1)}, bf16[256,512]{1,0:T(8,128)(2,1)S(1)}, u32[]{:S(2)}, u32[]{:S(2)}) collective-permute-start(bf16[256,512]{1,0:T(8,128)(2,1)S(1)} %choose.2), channel_id=1, source_target_pairs={{0,4},{4,0},{8,12},{12,8},{16,20},{20,16},{24,28},{28,24},{32,36},... | collective-permute-start | bytes 786440 | tf_op jit(solution)/shard_map/ppermute | solution.py:27
  45.5 10.0 %copy-start.1 = (bf16[256,256]{1,0:T(8,128)(2,1)S(1)}, bf16[256,256]{1,0:T(8,128)(2,1)}, u32[]{:S(2)}) copy-start(bf16[256,256]{1,0:T(8,128)(2,1)} %k_ref.3) | copy-start | bytes 393220
  45.5 10.0 %copy-start.3 = (bf16[256,256]{1,0:T(8,128)(2,1)S(1)}, bf16[256,256]{1,0:T(8,128)(2,1)}, u32[]{:S(2)}) copy-start(bf16[256,256]{1,0:T(8,128)(2,1)} %v_ref.3) | copy-start | bytes 393220
  45.5 10.0 %copy-start.9 = (s32[32]{0:T(128)S(1)}, s32[32]{0:T(128)}, u32[]{:S(2)}) copy-start(s32[32]{0:T(128)} %lens.3) | copy-start | bytes 388
  45.5 9.9 %copy-start.11 = (f32[256,128]{1,0:T(8,128)S(1)}, f32[256,128]{1,0:T(8,128)}, u32[]{:S(2)}) copy-start(f32[256,128]{1,0:T(8,128)} %get-tuple-element.38.keep_ref) | copy-start | bytes 393220
  45.5 4.7 %collective-permute-start.6 = (bf16[256,1024]{1,0:T(8,128)(2,1)S(1)}, bf16[256,1024]{1,0:T(8,128)(2,1)S(1)}, u32[]{:S(2)}, u32[]{:S(2)}) collective-permute-start(bf16[256,1024]{1,0:T(8,128)(2,1)S(1)} %get-tuple-element.36), channel_id=1, source_target_pairs={{0,4},{4,0},{8,12},{12,8},{16,20},{20,16},{24,28},{28,24},{32,36},... | collective-permute-start | bytes 1572872 | tf_op jit(solution)/shard_map/ppermute | solution.py:27
  46.0 19.1 %all-to-all-start = ((bf16[4,64,2048]{2,1,0:T(8,128)(2,1)}), bf16[4,64,2048]{2,1,0:T(8,128)(2,1)}, u32[]{:S(2)}, u32[]{:S(2)}) async-start(bf16[4,64,2048]{2,1,0:T(8,128)(2,1)} %bitcast.5), calls=%async_computation | async-start | bytes 2097152 | tf_op jit(solution)/shard_map/all_to_all | solution.py:315
  50.4 17.1 %collective-permute-start.8 = (bf16[256,512]{1,0:T(8,128)(2,1)S(1)}, bf16[256,512]{1,0:T(8,128)(2,1)S(1)}, u32[]{:S(2)}, u32[]{:S(2)}) collective-permute-start(bf16[256,512]{1,0:T(8,128)(2,1)S(1)} %get-tuple-element.41), channel_id=1, source_target_pairs={{0,240},{4,244},{8,248},{12,252},{16,0},{20,4},{24,8},{28,12},{32,... | collective-permute-start | bytes 786440 | tf_op jit(solution)/shard_map/ppermute | solution.py:27
  51.4 19.4 %collective-permute-start.7 = (bf16[256,512]{1,0:T(8,128)(2,1)S(1)}, bf16[256,512]{1,0:T(8,128)(2,1)S(1)}, u32[]{:S(2)}, u32[]{:S(2)}) collective-permute-start(bf16[256,512]{1,0:T(8,128)(2,1)S(1)} %get-tuple-element.37), channel_id=1, source_target_pairs={{0,248},{4,252},{8,0},{12,4},{16,8},{20,12},{24,16},{28,20},{32,24... | collective-permute-start | bytes 786440 | tf_op jit(solution)/shard_map/ppermute | solution.py:27
  55.5 1.2 %copy-start.7 = (bf16[256,2048]{1,0:T(8,128)(2,1)S(1)}, bf16[256,2048]{1,0:T(8,128)(2,1)}, u32[]{:S(2)}) copy-start(bf16[256,2048]{1,0:T(8,128)(2,1)} %g_ref.1) | copy-start | bytes 3145732
  56.7 1.2 %copy-start.10 = (bf16[256,2048]{1,0:T(8,128)(2,1)S(1)}, bf16[256,2048]{1,0:T(8,128)(2,1)}, u32[]{:S(2)}) copy-start(bf16[256,2048]{1,0:T(8,128)(2,1)} %get-tuple-element.32.far_ref) | copy-start | bytes 3145732

commit v6 on v5

--- a/solution.py
+++ b/solution.py
@@ -12,6 +12,7 @@
 REACH = 4
 NEG = -1e30
 LOG2E = 1.4426950408889634
+PAIR = 2
 
 
 def dot(a, b):
@@ -116,33 +117,47 @@
             pairs.append((keep_ref, keep_out))
         return [pltpu.make_async_copy(*pair, sent.at[2 * n + i]) for i, pair in enumerate(pairs)]
 
-    ahead = weigh(0)
-    for h in range(heads):
-        n = h // share
-        at, q, p, most, keep, total = ahead
-        ahead = weigh(h + 1) if h + 1 < heads else None
-        k, v = k_all[n], v_all[n]
+    def settle(h, at, q, p, most, keep, total):
         inverse = 1.0 / total
         pb = p.astype(jnp.bfloat16)
-        o = (dot(pb, v) + out_ref[:, at] * keep) * inverse
+        o = (dot(pb, v_all[h // share]) + out_ref[:, at] * keep) * inverse
         o_ref[:, at] = o.astype(jnp.bfloat16)
         gs = (g_ref[:, at].astype(jnp.float32) * inverse).astype(jnp.bfloat16)
         delta = jnp.sum(gs.astype(jnp.float32) * o, axis=1, keepdims=True)
         keep_ref[:, h : h + 1] = most[:, :1] * factor + jnp.log2(total[:, :1])
         keep_ref[:, heads + h : heads + h + 1] = delta * total[:, :1]
-        ds = (p * (dot_t(gs, v) - delta)).astype(jnp.bfloat16)
-        dq_ref[:, at] = dot(ds, k).astype(jnp.bfloat16)
-        dk_part, dv_part = dot(q.T, ds), dot(gs.T, pb)
-        dk, dv = (dk_part, dv_part) if h % share == 0 else (dk + dk_part, dv + dv_part)
-        if h % share == share - 1:
-            for copy in send(n):
-                copy.start()
-            outs = ((four_out, 0), (odd_out, 1), (two_out, 0), (odd_out, 0))
-            for b, (ref, place) in enumerate(outs):
-                at = slice(b * rows, (b + 1) * rows)
-                for which, grad in enumerate((dk[:, at].T * scale, dv[:, at].T)):
-                    to = (2 * groups * place + 2 * n + which) * width
-                    ref[:, to : to + width] = grad.astype(ref.dtype)
+        return h, at, q, p, pb, gs, delta
+
+    def differ(h, at, q, p, pb, gs, delta):
+        ds = (p * (dot_t(gs, v_all[h // share]) - delta)).astype(jnp.bfloat16)
+        dq_ref[:, at] = dot(ds, k_all[h // share]).astype(jnp.bfloat16)
+        return q, gs, ds, pb
+
+    weighed, settled, held = weigh(0), None, []
+    for h in range(heads + 1):
+        ahead = weigh(h + 1) if h + 1 < heads else None
+        done = settle(h, *weighed) if h < heads else None
+        if settled is not None:
+            held.append(differ(*settled))
+            if len(held) == PAIR:
+                q, gs, ds, pb = (jnp.concatenate(x, axis=0) for x in zip(*held))
+                held = []
+                dk_part, dv_part = dot(q.T, ds), dot(gs.T, pb)
+                if h % share == PAIR:
+                    dk, dv = dk_part, dv_part
+                else:
+                    dk, dv = dk + dk_part, dv + dv_part
+            if h % share == 0:
+                n = h // share - 1
+                for copy in send(n):
+                    copy.start()
+                outs = ((four_out, 0), (odd_out, 1), (two_out, 0), (odd_out, 0))
+                for b, (ref, place) in enumerate(outs):
+                    at = slice(b * rows, (b + 1) * rows)
+                    for which, grad in enumerate((dk[:, at].T * scale, dv[:, at].T)):
+                        to = (2 * groups * place + 2 * n + which) * width
+                        ref[:, to : to + width] = grad.astype(ref.dtype)
+        weighed, settled = ahead, done
     for n in range(groups):
         for copy in send(n):
             copy.wait()

time: 72 us -> 70 us (0.972)
  Pallas kernels: 27.6 us -> 25.5 us
    pallas_call x7, Pallas kernels: 27.6 us -> 25.5 us  [call(): pl.pallas_call(functools.partial(kernel, 1.0 / math.sqrt(HEAD_WIDTH)), in...]
where the time goes in v6:
time: 70 us; the launch traced here: 69.6 us
  starting transfers between devices  25.5 us (36%)
  Pallas kernels  25.5 us (36%)
  waiting for transfers between devices  9.33 us (13%)
  local copies, waits for them, and re-layouts  8.5 us (12%)
  between operations  0.76 us (1%)
    pallas_call x7, Pallas kernels, call(): pl.pallas_call(functools.partial(kernel, 1.0 / math.sqrt(HEAD_WIDTH)), in...  25.5 us
    ppermute x9, starting transfers between devices, moved(): lax.ppermute(value, 'seq', [(source, to(source) % count) for source in ra...  21.3 us
    ppermute x9, waiting for transfers between devices, moved(): lax.ppermute(value, 'seq', [(source, to(source) % count) for source in ra...  8.55 us
    unnamed x24, local copies, waits for them, and re-layouts  6.2 us
    all_to_all x1, starting transfers between devices, on_device(): lax.all_to_all(out.reshape(split, rows // split, out.shape[1]), 'head', s...  4.24 us
    reshape x1, local copies, waits for them, and re-layouts, on_device(): attn_out = jnp.transpose(got, (1, 0, 2)).reshape(got.shape[1], -1)  2.3 us
  transfers between devices with their start and end apart: 10, of which 4 were waited for; matrix products, arithmetic and copies ran while one was open for 3% of the time, Pallas kernels for 14%

profile of v6, /device:TPU:1, one launch (start us, length us, event | category | flops | bytes accessed | tf_op | source)
XLA Modules:
  0.0 69.6 jit_solution(3528636492896745664)
XLA Ops:
  0.6 2.5 %collective-permute-start.3 = (bf16[256,256]{1,0:T(8,128)(2,1)}, bf16[256,256]{1,0:T(8,128)(2,1)S(1)}, u32[]{:S(2)}, u32[]{:S(2)}) collective-permute-start(bf16[256,256]{1,0:T(8,128)(2,1)} %v_ref.3), channel_id=1, source_target_pairs={{0,8},{4,12},{8,16},{12,20},{16,24},{20,28},{24,32},{28,36},{32,40... | collective-permute-start | bytes 393224 | tf_op jit(solution)/shard_map/ppermute | solution.py:28
  3.2 3.0 %collective-permute-start.4 = (bf16[256,256]{1,0:T(8,128)(2,1)}, bf16[256,256]{1,0:T(8,128)(2,1)S(1)}, u32[]{:S(2)}, u32[]{:S(2)}) collective-permute-start(bf16[256,256]{1,0:T(8,128)(2,1)} %v_ref.3), channel_id=1, source_target_pairs={{0,16},{4,20},{8,24},{12,28},{16,32},{20,36},{24,40},{28,44},{32,4... | collective-permute-start | bytes 393224 | tf_op jit(solution)/shard_map/ppermute | solution.py:28
  6.2 2.8 %collective-permute-start = (bf16[256,256]{1,0:T(8,128)(2,1)}, bf16[256,256]{1,0:T(8,128)(2,1)S(1)}, u32[]{:S(2)}, u32[]{:S(2)}) collective-permute-start(bf16[256,256]{1,0:T(8,128)(2,1)} %k_ref.3), channel_id=1, source_target_pairs={{0,8},{4,12},{8,16},{12,20},{16,24},{20,28},{24,32},{28,36},{32,40... | collective-permute-start | bytes 393224 | tf_op jit(solution)/shard_map/ppermute | solution.py:28
  9.0 1.2 %collective-permute-start.1 = (bf16[256,256]{1,0:T(8,128)(2,1)}, bf16[256,256]{1,0:T(8,128)(2,1)S(1)}, u32[]{:S(2)}, u32[]{:S(2)}) collective-permute-start(bf16[256,256]{1,0:T(8,128)(2,1)} %k_ref.3), channel_id=1, source_target_pairs={{0,16},{4,20},{8,24},{12,28},{16,32},{20,36},{24,40},{28,44},{32,4... | collective-permute-start | bytes 393224 | tf_op jit(solution)/shard_map/ppermute | solution.py:28
  10.2 0.9 %copy-done = bf16[256,256]{1,0:T(8,128)(2,1)S(1)} copy-done((bf16[256,256]{1,0:T(8,128)(2,1)S(1)}, bf16[256,256]{1,0:T(8,128)(2,1)}, u32[]{:S(2)}) %copy-start) | copy-done | bytes 131096
  11.1 0.9 %copy-done.2 = bf16[256,256]{1,0:T(8,128)(2,1)S(1)} copy-done((bf16[256,256]{1,0:T(8,128)(2,1)S(1)}, bf16[256,256]{1,0:T(8,128)(2,1)}, u32[]{:S(2)}) %copy-start.2) | copy-done | bytes 131096
  12.1 1.2 %copy-done.4 = bf16[256,2048]{1,0:T(8,128)(2,1)S(1)} copy-done((bf16[256,2048]{1,0:T(8,128)(2,1)S(1)}, bf16[256,2048]{1,0:T(8,128)(2,1)}, u32[]{:S(2)}) %copy-start.4) | copy-done | bytes 1048600
  13.3 0.7 copy-done.8
  13.9 3.5 %own_forward.1 = (f32[256,2048]{1,0:T(8,128)S(1)}, f32[256,2048]{1,0:T(8,128)S(1)}, f32[256,2048]{1,0:T(8,128)S(1)}, f32[256,1024]{1,0:T(8,128)S(1)}) custom-call(s32[32]{0:T(128)S(1)} %copy-done.8, s32[1]{0:T(128)} %bitcast.here.place, bf16[256,2048]{1,0:T(8,128)(2,1)S(1)} %copy-done.4, bf16[256,256]{1,0:T(8,128)(2,1)S(1)} %copy-done, ...), custom_call_target="tpu_custom_call" | custom-call | flops 536870912 | bytes 1048576 | tf_op jit(solution)/shard_map/own_forward/pallas_call | solution.py:238
  17.5 4.3 %collective-permute-start.5 = (bf16[256,512]{1,0:T(8,128)(2,1)S(1)}, bf16[256,512]{1,0:T(8,128)(2,1)S(1)}, u32[]{:S(2)}, u32[]{:S(2)}) collective-permute-start(bf16[256,512]{1,0:T(8,128)(2,1)S(1)} %choose.3), channel_id=1, source_target_pairs={{0,4},{4,0},{8,12},{12,8},{16,20},{20,16},{24,28},{28,24},{32,36},... | collective-permute-start | bytes 786440 | tf_op jit(solution)/shard_map/ppermute | solution.py:28
  21.7 4.0 %collective-permute-done.1.four_ref.refs_7_ = bf16[256,256]{1,0:T(8,128)(2,1)S(1)} collective-permute-done((bf16[256,256]{1,0:T(8,128)(2,1)}, bf16[256,256]{1,0:T(8,128)(2,1)S(1)}, u32[]{:S(2)}, u32[]{:S(2)}) %collective-permute-start.1) | collective-permute-done | bytes 131104 | tf_op jit(solution)/shard_map/ppermute | solution.py:28
  25.7 1.9 %collective-permute-start.2 = (bf16[256,512]{1,0:T(8,128)(2,1)S(1)}, bf16[256,512]{1,0:T(8,128)(2,1)S(1)}, u32[]{:S(2)}, u32[]{:S(2)}) collective-permute-start(bf16[256,512]{1,0:T(8,128)(2,1)S(1)} %choose.2), channel_id=1, source_target_pairs={{0,4},{4,0},{8,12},{12,8},{16,20},{20,16},{24,28},{28,24},{32,36},... | collective-permute-start | bytes 786440 | tf_op jit(solution)/shard_map/ppermute | solution.py:28
  27.6 1.2 %collective-permute-done.2.refs_8_ = bf16[256,512]{1,0:T(8,128)(2,1)S(1)} collective-permute-done((bf16[256,512]{1,0:T(8,128)(2,1)S(1)}, bf16[256,512]{1,0:T(8,128)(2,1)S(1)}, u32[]{:S(2)}, u32[]{:S(2)}) %collective-permute-start.2) | collective-permute-done | bytes 262176 | tf_op jit(solution)/shard_map/ppermute | solution.py:28
  28.7 14.7 %far.1 = (bf16[256,2048]{1,0:T(8,128)(2,1)}, bf16[256,2048]{1,0:T(8,128)(2,1)}, f32[256,128]{1,0:T(8,128)}, f32[256,512]{1,0:T(8,128)S(1)}, f32[256,512]{1,0:T(8,128)S(1)}, /*index=5*/bf16[256,1024]{1,0:T(8,128)(2,1)S(1)}) custom-call(bf16[256,2048]{1,0:T(8,128)(2,1)S(1)} %copy-done.5, bf16[256,2048]{1,0:T(8,128)(2,1)S(1)} %copy-done.6, ...), custom_call_target="tpu_custom_call" | custom-call | flops 6442450944 | bytes 1048576 | tf_op jit(solution)/shard_map/far/pallas_call | solution.py:238
  44.0 4.2 %all-to-all-start = ((bf16[4,64,2048]{2,1,0:T(8,128)(2,1)}), bf16[4,64,2048]{2,1,0:T(8,128)(2,1)}, u32[]{:S(2)}, u32[]{:S(2)}) async-start(bf16[4,64,2048]{2,1,0:T(8,128)(2,1)} %bitcast.5), calls=%async_computation | async-start | bytes 2097152 | tf_op jit(solution)/shard_map/all_to_all | solution.py:330
  48.3 1.0 %collective-permute-start.8 = (bf16[256,512]{1,0:T(8,128)(2,1)S(1)}, bf16[256,512]{1,0:T(8,128)(2,1)S(1)}, u32[]{:S(2)}, u32[]{:S(2)}) collective-permute-start(bf16[256,512]{1,0:T(8,128)(2,1)S(1)} %get-tuple-element.41), channel_id=1, source_target_pairs={{0,240},{4,244},{8,248},{12,252},{16,0},{20,4},{24,8},{28,12},{32,... | collective-permute-start | bytes 786440 | tf_op jit(solution)/shard_map/ppermute | solution.py:28
  49.4 4.0 %collective-permute-start.7 = (bf16[256,512]{1,0:T(8,128)(2,1)S(1)}, bf16[256,512]{1,0:T(8,128)(2,1)S(1)}, u32[]{:S(2)}, u32[]{:S(2)}) collective-permute-start(bf16[256,512]{1,0:T(8,128)(2,1)S(1)} %get-tuple-element.37), channel_id=1, source_target_pairs={{0,248},{4,252},{8,0},{12,4},{16,8},{20,12},{24,16},{28,20},{32,24... | collective-permute-start | bytes 786440 | tf_op jit(solution)/shard_map/ppermute | solution.py:28
  53.4 1.2 %copy-done.7 = bf16[256,2048]{1,0:T(8,128)(2,1)S(1)} copy-done((bf16[256,2048]{1,0:T(8,128)(2,1)S(1)}, bf16[256,2048]{1,0:T(8,128)(2,1)}, u32[]{:S(2)}) %copy-start.7) | copy-done | bytes 1048600
  54.7 1.2 %copy-done.10 = bf16[256,2048]{1,0:T(8,128)(2,1)S(1)} copy-done((bf16[256,2048]{1,0:T(8,128)(2,1)S(1)}, bf16[256,2048]{1,0:T(8,128)(2,1)}, u32[]{:S(2)}) %copy-start.10) | copy-done | bytes 1048600
  55.9 6.4 %own_backward.1 = (bf16[256,2048]{1,0:T(8,128)(2,1)}, f32[256,512]{1,0:T(8,128)S(1)}) custom-call(s32[32]{0:T(128)S(1)} %copy-done.9, s32[1]{0:T(128)} %bitcast.here.place, bf16[256,2048]{1,0:T(8,128)(2,1)S(1)} %copy-done.5, bf16[256,2048]{1,0:T(8,128)(2,1)S(1)} %copy-done.7, bf16[256,2048]{1,0:T(8,128)(2,1)S(1)} %copy-done.10, f32[256,128]{1,0:T(8,128)S(1)} %copy-done.11, ...), custom_call_target="tpu_custom_call" | custom-call | flops 1073741824 | bytes 1048576 | tf_op jit(solution)/shard_map/own_backward/pallas_call | solution.py:238
  62.3 0.8 %all-to-all-done = bf16[4,64,2048]{2,1,0:T(8,128)(2,1)} async-done(((bf16[4,64,2048]{2,1,0:T(8,128)(2,1)}), bf16[4,64,2048]{2,1,0:T(8,128)(2,1)}, u32[]{:S(2)}, u32[]{:S(2)}) %all-to-all-start) | async-done | bytes 1048608 | tf_op jit(solution)/shard_map/all_to_all | solution.py:330
  63.1 2.3 %copy.10 = bf16[4,8,8,2048]{3,2,0,1:T(8,128)(2,1)} copy(bf16[4,8,8,2048]{3,2,1,0:T(8,128)(2,1)} %bitcast.3) | data formatting | bytes 2097152 | tf_op jit(solution)/shard_map/reshape | solution.py:361
  65.4 3.4 %collective-permute-done.7.two_ref = bf16[256,512]{1,0:T(8,128)(2,1)S(1)} collective-permute-done((bf16[256,512]{1,0:T(8,128)(2,1)S(1)}, bf16[256,512]{1,0:T(8,128)(2,1)S(1)}, u32[]{:S(2)}, u32[]{:S(2)}) %collective-permute-start.7) | collective-permute-done | bytes 262176 | tf_op jit(solution)/shard_map/ppermute | solution.py:28
  68.8 0.8 %total.1 = (bf16[256,256]{1,0:T(8,128)(2,1)}, bf16[256,256]{1,0:T(8,128)(2,1)}) custom-call(s32[1]{0:T(128)} %bitcast.here.place, f32[256,512]{1,0:T(8,128)S(1)} %get-tuple-element.40.own_ref, bf16[256,1024]{1,0:T(8,128)(2,1)S(1)} %collective-permute-done.6.other_ref, bf16[256,512]{1,0:T(8,128)(2,1)S(1)} %collective-permute-done.7.two_ref, ...), custom_call_target="tpu_custom_call" | custom-call | bytes 1048576 | tf_op jit(solution)/shard_map/total/pallas_call | solution.py:238
  (28 shorter events, 0.7 us)
Async XLA Ops:
  0.6 16.8 %collective-permute-start.3 = (bf16[256,256]{1,0:T(8,128)(2,1)}, bf16[256,256]{1,0:T(8,128)(2,1)S(1)}, u32[]{:S(2)}, u32[]{:S(2)}) collective-permute-start(bf16[256,256]{1,0:T(8,128)(2,1)} %v_ref.3), channel_id=1, source_target_pairs={{0,8},{4,12},{8,16},{12,20},{16,24},{20,28},{24,32},{28,36},{32,40... | collective-permute-start | bytes 393224 | tf_op jit(solution)/shard_map/ppermute | solution.py:28
  3.2 14.2 %collective-permute-start.4 = (bf16[256,256]{1,0:T(8,128)(2,1)}, bf16[256,256]{1,0:T(8,128)(2,1)S(1)}, u32[]{:S(2)}, u32[]{:S(2)}) collective-permute-start(bf16[256,256]{1,0:T(8,128)(2,1)} %v_ref.3), channel_id=1, source_target_pairs={{0,16},{4,20},{8,24},{12,28},{16,32},{20,36},{24,40},{28,44},{32,4... | collective-permute-start | bytes 393224 | tf_op jit(solution)/shard_map/ppermute | solution.py:28
  6.2 15.6 %collective-permute-start = (bf16[256,256]{1,0:T(8,128)(2,1)}, bf16[256,256]{1,0:T(8,128)(2,1)S(1)}, u32[]{:S(2)}, u32[]{:S(2)}) collective-permute-start(bf16[256,256]{1,0:T(8,128)(2,1)} %k_ref.3), channel_id=1, source_target_pairs={{0,8},{4,12},{8,16},{12,20},{16,24},{20,28},{24,32},{28,36},{32,40... | collective-permute-start | bytes 393224 | tf_op jit(solution)/shard_map/ppermute | solution.py:28
  9.0 16.7 %collective-permute-start.1 = (bf16[256,256]{1,0:T(8,128)(2,1)}, bf16[256,256]{1,0:T(8,128)(2,1)S(1)}, u32[]{:S(2)}, u32[]{:S(2)}) collective-permute-start(bf16[256,256]{1,0:T(8,128)(2,1)} %k_ref.3), channel_id=1, source_target_pairs={{0,16},{4,20},{8,24},{12,28},{16,32},{20,36},{24,40},{28,44},{32,4... | collective-permute-start | bytes 393224 | tf_op jit(solution)/shard_map/ppermute | solution.py:28
  10.2 0.9 %copy-start = (bf16[256,256]{1,0:T(8,128)(2,1)S(1)}, bf16[256,256]{1,0:T(8,128)(2,1)}, u32[]{:S(2)}) copy-start(bf16[256,256]{1,0:T(8,128)(2,1)} %k_ref.3) | copy-start | bytes 393220
  11.1 0.9 %copy-start.2 = (bf16[256,256]{1,0:T(8,128)(2,1)S(1)}, bf16[256,256]{1,0:T(8,128)(2,1)}, u32[]{:S(2)}) copy-start(bf16[256,256]{1,0:T(8,128)(2,1)} %v_ref.3) | copy-start | bytes 393220
  12.1 1.2 %copy-start.4 = (bf16[256,2048]{1,0:T(8,128)(2,1)S(1)}, bf16[256,2048]{1,0:T(8,128)(2,1)}, u32[]{:S(2)}) copy-start(bf16[256,2048]{1,0:T(8,128)(2,1)} %q_ref.3) | copy-start | bytes 3145732
  13.3 0.7 copy-start.8
  13.9 14.8 %copy-start.5 = (bf16[256,2048]{1,0:T(8,128)(2,1)S(1)}, bf16[256,2048]{1,0:T(8,128)(2,1)}, u32[]{:S(2)}) copy-start(bf16[256,2048]{1,0:T(8,128)(2,1)} %q_ref.3) | copy-start | bytes 3145732
  13.9 14.8 %copy-start.6 = (bf16[256,2048]{1,0:T(8,128)(2,1)S(1)}, bf16[256,2048]{1,0:T(8,128)(2,1)}, u32[]{:S(2)}) copy-start(bf16[256,2048]{1,0:T(8,128)(2,1)} %g_ref.1) | copy-start | bytes 3145732
  17.5 10.1 %collective-permute-start.5 = (bf16[256,512]{1,0:T(8,128)(2,1)S(1)}, bf16[256,512]{1,0:T(8,128)(2,1)S(1)}, u32[]{:S(2)}, u32[]{:S(2)}) collective-permute-start(bf16[256,512]{1,0:T(8,128)(2,1)S(1)} %choose.3), channel_id=1, source_target_pairs={{0,4},{4,0},{8,12},{12,8},{16,20},{20,16},{24,28},{28,24},{32,36},... | collective-permute-start | bytes 786440 | tf_op jit(solution)/shard_map/ppermute | solution.py:28
  25.7 3.0 %collective-permute-start.2 = (bf16[256,512]{1,0:T(8,128)(2,1)S(1)}, bf16[256,512]{1,0:T(8,128)(2,1)S(1)}, u32[]{:S(2)}, u32[]{:S(2)}) collective-permute-start(bf16[256,512]{1,0:T(8,128)(2,1)S(1)} %choose.2), channel_id=1, source_target_pairs={{0,4},{4,0},{8,12},{12,8},{16,20},{20,16},{24,28},{28,24},{32,36},... | collective-permute-start | bytes 786440 | tf_op jit(solution)/shard_map/ppermute | solution.py:28
  43.4 10.0 %copy-start.1 = (bf16[256,256]{1,0:T(8,128)(2,1)S(1)}, bf16[256,256]{1,0:T(8,128)(2,1)}, u32[]{:S(2)}) copy-start(bf16[256,256]{1,0:T(8,128)(2,1)} %k_ref.3) | copy-start | bytes 393220
  43.5 10.0 %copy-start.3 = (bf16[256,256]{1,0:T(8,128)(2,1)S(1)}, bf16[256,256]{1,0:T(8,128)(2,1)}, u32[]{:S(2)}) copy-start(bf16[256,256]{1,0:T(8,128)(2,1)} %v_ref.3) | copy-start | bytes 393220
  43.5 10.0 %copy-start.9 = (s32[32]{0:T(128)S(1)}, s32[32]{0:T(128)}, u32[]{:S(2)}) copy-start(s32[32]{0:T(128)} %lens.3) | copy-start | bytes 388
  43.5 9.9 %copy-start.11 = (f32[256,128]{1,0:T(8,128)S(1)}, f32[256,128]{1,0:T(8,128)}, u32[]{:S(2)}) copy-start(f32[256,128]{1,0:T(8,128)} %get-tuple-element.38.keep_ref) | copy-start | bytes 393220
  43.5 4.7 %collective-permute-start.6 = (bf16[256,1024]{1,0:T(8,128)(2,1)S(1)}, bf16[256,1024]{1,0:T(8,128)(2,1)S(1)}, u32[]{:S(2)}, u32[]{:S(2)}) collective-permute-start(bf16[256,1024]{1,0:T(8,128)(2,1)S(1)} %get-tuple-element.36), channel_id=1, source_target_pairs={{0,4},{4,0},{8,12},{12,8},{16,20},{20,16},{24,28},{28,24},{32,36},... | collective-permute-start | bytes 1572872 | tf_op jit(solution)/shard_map/ppermute | solution.py:28
  44.0 19.1 %all-to-all-start = ((bf16[4,64,2048]{2,1,0:T(8,128)(2,1)}), bf16[4,64,2048]{2,1,0:T(8,128)(2,1)}, u32[]{:S(2)}, u32[]{:S(2)}) async-start(bf16[4,64,2048]{2,1,0:T(8,128)(2,1)} %bitcast.5), calls=%async_computation | async-start | bytes 2097152 | tf_op jit(solution)/shard_map/all_to_all | solution.py:330
  48.3 17.0 %collective-permute-start.8 = (bf16[256,512]{1,0:T(8,128)(2,1)S(1)}, bf16[256,512]{1,0:T(8,128)(2,1)S(1)}, u32[]{:S(2)}, u32[]{:S(2)}) collective-permute-start(bf16[256,512]{1,0:T(8,128)(2,1)S(1)} %get-tuple-element.41), channel_id=1, source_target_pairs={{0,240},{4,244},{8,248},{12,252},{16,0},{20,4},{24,8},{28,12},{32,... | collective-permute-start | bytes 786440 | tf_op jit(solution)/shard_map/ppermute | solution.py:28
  49.4 19.4 %collective-permute-start.7 = (bf16[256,512]{1,0:T(8,128)(2,1)S(1)}, bf16[256,512]{1,0:T(8,128)(2,1)S(1)}, u32[]{:S(2)}, u32[]{:S(2)}) collective-permute-start(bf16[256,512]{1,0:T(8,128)(2,1)S(1)} %get-tuple-element.37), channel_id=1, source_target_pairs={{0,248},{4,252},{8,0},{12,4},{16,8},{20,12},{24,16},{28,20},{32,24... | collective-permute-start | bytes 786440 | tf_op jit(solution)/shard_map/ppermute | solution.py:28
  53.4 1.2 %copy-start.7 = (bf16[256,2048]{1,0:T(8,128)(2,1)S(1)}, bf16[256,2048]{1,0:T(8,128)(2,1)}, u32[]{:S(2)}) copy-start(bf16[256,2048]{1,0:T(8,128)(2,1)} %g_ref.1) | copy-start | bytes 3145732
  54.7 1.2 %copy-start.10 = (bf16[256,2048]{1,0:T(8,128)(2,1)S(1)}, bf16[256,2048]{1,0:T(8,128)(2,1)}, u32[]{:S(2)}) copy-start(bf16[256,2048]{1,0:T(8,128)(2,1)} %get-tuple-element.32.far_ref) | copy-start | bytes 3145732

commit v7 on v6

--- a/solution.py
+++ b/solution.py
@@ -82,11 +82,12 @@
         out_ref[:, at] = dot(p.astype(jnp.bfloat16), v_ref[:, kv])
 
 
-def far_kernel(scale, *refs):
+def far_kernel(split, scale, turn, *refs):
     q_ref, g_ref, out_ref, top_ref, sum_ref, bias_ref = refs[0:6]
-    (o_out, dq_out, keep_out, two_out, four_out, odd_out) = refs[-12:-6]
+    o_outs = refs[-11 - split : -11]
+    dq_out, keep_out, two_out, four_out, odd_out = refs[-11:-6]
     k_all, v_all, o_ref, dq_ref, keep_ref, sent = refs[-6:]
-    fars = refs[6:-12]
+    fars = refs[6 : -11 - split]
     rows, width = q_ref.shape[0], HEAD_WIDTH
     groups = k_all.shape[0]
     heads = q_ref.shape[1] // width
@@ -112,10 +113,15 @@
 
     def send(n):
         to = slice(n * share * width, (n + 1) * share * width)
-        pairs = [(o_ref.at[:, to], o_out.at[:, to]), (dq_ref.at[:, to], dq_out.at[:, to])]
+        piece = rows // split
+        pairs = [(dq_ref.at[:, to], dq_out.at[:, to])]
+        for ahead, o_out in enumerate(o_outs):
+            first = pl.multiple_of(lax.rem(turn[0] + ahead, split) * piece, piece)
+            pairs.append((o_ref.at[pl.ds(first, piece), to], o_out.at[:, to]))
         if n == groups - 1:
             pairs.append((keep_ref, keep_out))
-        return [pltpu.make_async_copy(*pair, sent.at[2 * n + i]) for i, pair in enumerate(pairs)]
+        first = n * (split + 1)
+        return [pltpu.make_async_copy(*pair, sent.at[first + i]) for i, pair in enumerate(pairs)]
 
     def settle(h, at, q, p, most, keep, total):
         inverse = 1.0 / total
@@ -221,6 +227,18 @@
         four_out[...] = (four_ref[...] + three).astype(jnp.bfloat16)
 
 
+def spread_kernel(scale, turn, *refs):
+    pieces, out_ref, sent = refs[:-2], refs[-2], refs[-1]
+    split, cols = len(pieces), pieces[0].shape[1]
+    copies = []
+    for ahead, piece in enumerate(pieces):
+        first = pl.multiple_of(lax.rem(turn[0] + split - ahead, split) * cols, cols)
+        copies.append(pltpu.make_async_copy(piece, out_ref.at[:, pl.ds(first, cols)], sent.at[ahead]))
+        copies[-1].start()
+    for copy in copies:
+        copy.wait()
+
+
 def total_kernel(scale, place, own_ref, other_ref, two_ref, four_ref, k_out, v_out):
     width = HEAD_WIDTH
     one = jnp.where(place[0] % 2 == 0, 1.0, 0.0)
@@ -232,12 +250,14 @@
             ref[:, n * width : (n + 1) * width] = total.astype(jnp.bfloat16)
 
 
-def call(kernel, name, cost, outs, *args, scalars=0, scratch=(), hbm=()):
+def call(kernel, name, cost, outs, *args, scalars=0, scratch=(), hbm=(), stay=0):
     whole = pl.BlockSpec(memory_space=pltpu.VMEM)
     left = pl.BlockSpec(memory_space=pltpu.HBM)
     return pl.pallas_call(
         functools.partial(kernel, 1.0 / math.sqrt(HEAD_WIDTH)),
-        in_specs=[pl.BlockSpec(memory_space=pltpu.SMEM)] * scalars + [whole] * (len(args) - scalars),
+        in_specs=[pl.BlockSpec(memory_space=pltpu.SMEM)] * scalars
+        + [whole] * (len(args) - scalars - stay)
+        + [pl.BlockSpec(memory_space=pl.ANY)] * stay,
         out_specs=[left if i in hbm else whole for i in range(len(outs))],
         out_shape=[
             pltpu.HBM(shape, dtype) if i in hbm else jax.ShapeDtypeStruct(shape, dtype)
@@ -259,6 +279,8 @@
     wide = 2 * groups * width
     place = lax.axis_index("seq")
     here = place.reshape(1).astype(jnp.int32)
+    turn = lax.axis_index("head").reshape(1).astype(jnp.int32)
+    split = lax.axis_size("head")
     twos, fours, fars = [], [], []
     for own in (keys, values):
         twos.append(up(own, 2))
@@ -289,18 +311,19 @@
             scalars=1,
         )[0]
         fars += [two, four, swapped(send)]
-    out, dq_far, keep, two, four, odd = call(
-        far_kernel,
+    *pieces, dq_far, keep, two, four, odd = call(
+        functools.partial(far_kernel, split),
         "far",
         6 * 1024,
-        [
-            (queries.shape, jnp.bfloat16),
+        [((rows // split, queries.shape[1]), jnp.bfloat16)] * split
+        + [
             (queries.shape, jnp.bfloat16),
             ((rows, width), jnp.float32),
             ((rows, wide), jnp.float32),
             ((rows, wide), jnp.float32),
             ((rows, 2 * wide), jnp.bfloat16),
         ],
+        turn,
         queries,
         output_gradient,
         parts,
@@ -310,8 +333,9 @@
         *fars,
         scratch=[pltpu.VMEM((groups, REACH * rows, width), jnp.bfloat16)] * 2
         + [pltpu.VMEM(queries.shape, jnp.bfloat16)] * 2
-        + [pltpu.VMEM((rows, width), jnp.float32), pltpu.SemaphoreType.DMA((2 * groups + 1,))],
-        hbm=(0, 1, 2),
+        + [pltpu.VMEM((rows, width), jnp.float32), pltpu.SemaphoreType.DMA((groups * (split + 1) + 1,))],
+        scalars=1,
+        hbm=range(split + 2),
     )
     other = swapped(odd)
     two, four = call(
@@ -326,10 +350,14 @@
         scalars=1,
     )
     two_back, four_back = up(two, -2), up(four, -4)
-    split = lax.axis_size("head")
-    got = lax.all_to_all(
-        out.reshape(split, rows // split, out.shape[1]), "head", split_axis=0, concat_axis=0
-    )
+
+    def around(piece, ahead):
+        return lax.ppermute(
+            piece, "head", [(source, (source + ahead) % split) for source in range(split)]
+        )
+
+    late, two = lax.optimization_barrier((pieces, two))
+    got = [around(pieces[n] if n == split // 2 else late[n], n) for n in range(1, split)]
     keep, two = lax.optimization_barrier((keep, two))
     d_queries, own = call(
         own_backward_kernel,
@@ -358,7 +386,20 @@
         four_back,
         scalars=1,
     )
-    attn_out = jnp.transpose(got, (1, 0, 2)).reshape(got.shape[1], -1)
+    got, key_gradient = lax.optimization_barrier((got, key_gradient))
+    attn_out = call(
+        spread_kernel,
+        "spread",
+        0,
+        [((rows // split, split * queries.shape[1]), jnp.bfloat16)],
+        turn,
+        pieces[0],
+        *got,
+        scalars=1,
+        scratch=[pltpu.SemaphoreType.DMA((split,))],
+        hbm=(0,),
+        stay=split,
+    )[0]
     return (attn_out, d_queries, key_gradient, value_gradient)
 
 

time: 70 us -> 77.1 us (1.10)
  local copies, waits for them, and re-layouts: 8.5 us -> 15.9 us
  Pallas kernels: 25.5 us -> 27.7 us
  waiting for transfers between devices: 9.33 us -> 7.72 us
  starting transfers between devices: 25.5 us -> 24.5 us
    unnamed x24 -> x40, local copies, waits for them, and re-layouts: 6.2 us -> 15.9 us
    ppermute x0 -> x3, starting transfers between devices: none -> 5.58 us  [around(): lax.ppermute(piece, 'head', [(source, (source + ahead) % split) for sourc...]
    all_to_all x1 -> x0, starting transfers between devices: 4.24 us -> none  [on_device(): lax.all_to_all(out.reshape(split, rows // split, out.shape[1]), 'head', s...]
    ppermute x9, starting transfers between devices: 21.3 us -> 18.9 us  [moved(): lax.ppermute(value, 'seq', [(source, to(source) % count) for source in ra...]
    reshape x1 -> x0, local copies, waits for them, and re-layouts: 2.3 us -> none  [on_device(): attn_out = jnp.transpose(got, (1, 0, 2)).reshape(got.shape[1], -1)]
    pallas_call x7 -> x8, Pallas kernels: 25.5 us -> 27.7 us  [call(): pl.pallas_call(functools.partial(kernel, 1.0 / math.sqrt(HEAD_WIDTH)), in...]
    ppermute x9, waiting for transfers between devices: 8.55 us -> 7.71 us  [moved(): lax.ppermute(value, 'seq', [(source, to(source) % count) for source in ra...]
    all_to_all x1 -> x0, waiting for transfers between devices: 0.78 us -> none  [on_device(): lax.all_to_all(out.reshape(split, rows // split, out.shape[1]), 'head', s...]
  transfers between devices with their start and end apart: 10 -> 12, of which waited for: 4 -> 3; matrix products, arithmetic and copies ran while one was open for 3% -> 0% of each run, Pallas kernels for 14% -> 14%
where the time goes in v7:
time: 77.1 us; the launch traced here: 76.7 us
  Pallas kernels  27.7 us (36%)
  starting transfers between devices  24.5 us (32%)
  local copies, waits for them, and re-layouts  15.9 us (21%)
  waiting for transfers between devices  7.72 us (10%)
  between operations  0.91 us (1%)
    pallas_call x8, Pallas kernels, call(): pl.pallas_call(functools.partial(kernel, 1.0 / math.sqrt(HEAD_WIDTH)), in...  27.7 us
    ppermute x9, starting transfers between devices, moved(): lax.ppermute(value, 'seq', [(source, to(source) % count) for source in ra...  18.9 us
    unnamed x40, local copies, waits for them, and re-layouts  15.9 us
    ppermute x9, waiting for transfers between devices, moved(): lax.ppermute(value, 'seq', [(source, to(source) % count) for source in ra...  7.71 us
    ppermute x3, starting transfers between devices, around(): lax.ppermute(piece, 'head', [(source, (source + ahead) % split) for sourc...  5.58 us
  transfers between devices with their start and end apart: 12, of which 3 were waited for; matrix products, arithmetic and copies ran while one was open for 0% of the time, Pallas kernels for 14%

profile of v7, /device:TPU:1, one launch (start us, length us, event | category | flops | bytes accessed | tf_op | source)
XLA Modules:
  0.0 76.7 jit_solution(16651989239475987676)
XLA Ops:
  0.6 2.5 %collective-permute-start.3 = (bf16[256,256]{1,0:T(8,128)(2,1)}, bf16[256,256]{1,0:T(8,128)(2,1)S(1)}, u32[]{:S(2)}, u32[]{:S(2)}) collective-permute-start(bf16[256,256]{1,0:T(8,128)(2,1)} %v_ref.3), channel_id=1, source_target_pairs={{0,8},{4,12},{8,16},{12,20},{16,24},{20,28},{24,32},{28,36},{32,40... | collective-permute-start | bytes 393224 | tf_op jit(solution)/shard_map/ppermute | solution.py:28
  3.2 3.0 %collective-permute-start.4 = (bf16[256,256]{1,0:T(8,128)(2,1)}, bf16[256,256]{1,0:T(8,128)(2,1)S(1)}, u32[]{:S(2)}, u32[]{:S(2)}) collective-permute-start(bf16[256,256]{1,0:T(8,128)(2,1)} %v_ref.3), channel_id=1, source_target_pairs={{0,16},{4,20},{8,24},{12,28},{16,32},{20,36},{24,40},{28,44},{32,4... | collective-permute-start | bytes 393224 | tf_op jit(solution)/shard_map/ppermute | solution.py:28
  6.2 2.8 %collective-permute-start = (bf16[256,256]{1,0:T(8,128)(2,1)}, bf16[256,256]{1,0:T(8,128)(2,1)S(1)}, u32[]{:S(2)}, u32[]{:S(2)}) collective-permute-start(bf16[256,256]{1,0:T(8,128)(2,1)} %k_ref.3), channel_id=1, source_target_pairs={{0,8},{4,12},{8,16},{12,20},{16,24},{20,28},{24,32},{28,36},{32,40... | collective-permute-start | bytes 393224 | tf_op jit(solution)/shard_map/ppermute | solution.py:28
  9.0 1.2 %collective-permute-start.1 = (bf16[256,256]{1,0:T(8,128)(2,1)}, bf16[256,256]{1,0:T(8,128)(2,1)S(1)}, u32[]{:S(2)}, u32[]{:S(2)}) collective-permute-start(bf16[256,256]{1,0:T(8,128)(2,1)} %k_ref.3), channel_id=1, source_target_pairs={{0,16},{4,20},{8,24},{12,28},{16,32},{20,36},{24,40},{28,44},{32,4... | collective-permute-start | bytes 393224 | tf_op jit(solution)/shard_map/ppermute | solution.py:28
  12.1 1.2 %copy-done.5 = bf16[256,2048]{1,0:T(8,128)(2,1)S(1)} copy-done((bf16[256,2048]{1,0:T(8,128)(2,1)S(1)}, bf16[256,2048]{1,0:T(8,128)(2,1)}, u32[]{:S(2)}) %copy-start.5) | copy-done | bytes 1048600
  13.9 3.4 %own_forward.1 = (f32[256,2048]{1,0:T(8,128)S(1)}, f32[256,2048]{1,0:T(8,128)S(1)}, f32[256,2048]{1,0:T(8,128)S(1)}, f32[256,1024]{1,0:T(8,128)S(1)}) custom-call(s32[32]{0:T(128)S(1)} %copy-done.8, s32[1]{0:T(128)} %bitcast.1.here.place, bf16[256,2048]{1,0:T(8,128)(2,1)S(1)} %copy-done.5, bf16[256,256]{1,0:T(8,128)(2,1)S(1)} %copy-done.1, ...), custom_call_target="tpu_custom_call" | custom-call | flops 536870912 | bytes 1048576 | tf_op jit(solution)/shard_map/own_forward/pallas_call | solution.py:256
  17.4 1.3 %copy-done.11 = f32[256,2048]{1,0:T(8,128)} copy-done((f32[256,2048]{1,0:T(8,128)}, f32[256,2048]{1,0:T(8,128)S(1)}, u32[]{:S(2)}) %copy-start.11) | copy-done | bytes 2097176
  18.7 1.3 %copy-done.13 = f32[256,2048]{1,0:T(8,128)} copy-done((f32[256,2048]{1,0:T(8,128)}, f32[256,2048]{1,0:T(8,128)S(1)}, u32[]{:S(2)}) %copy-start.13) | copy-done | bytes 2097176
  20.0 1.4 %copy-done.15 = f32[256,2048]{1,0:T(8,128)} copy-done((f32[256,2048]{1,0:T(8,128)}, f32[256,2048]{1,0:T(8,128)S(1)}, u32[]{:S(2)}) %copy-start.15) | copy-done | bytes 2097176
  21.5 1.9 %collective-permute-start.5 = (bf16[256,512]{1,0:T(8,128)(2,1)S(1)}, bf16[256,512]{1,0:T(8,128)(2,1)S(1)}, u32[]{:S(2)}, u32[]{:S(2)}) collective-permute-start(bf16[256,512]{1,0:T(8,128)(2,1)S(1)} %choose.3), channel_id=1, source_target_pairs={{0,4},{4,0},{8,12},{12,8},{16,20},{20,16},{24,28},{28,24},{32,36},... | collective-permute-start | bytes 786440 | tf_op jit(solution)/shard_map/ppermute | solution.py:28
  23.4 2.3 %collective-permute-done.1.four_ref.refs_7_ = bf16[256,256]{1,0:T(8,128)(2,1)S(1)} collective-permute-done((bf16[256,256]{1,0:T(8,128)(2,1)}, bf16[256,256]{1,0:T(8,128)(2,1)S(1)}, u32[]{:S(2)}, u32[]{:S(2)}) %collective-permute-start.1) | collective-permute-done | bytes 131104 | tf_op jit(solution)/shard_map/ppermute | solution.py:28
  25.7 1.9 %collective-permute-start.2 = (bf16[256,512]{1,0:T(8,128)(2,1)S(1)}, bf16[256,512]{1,0:T(8,128)(2,1)}, u32[]{:S(2)}, u32[]{:S(2)}) collective-permute-start(bf16[256,512]{1,0:T(8,128)(2,1)S(1)} %choose.2), channel_id=1, source_target_pairs={{0,4},{4,0},{8,12},{12,8},{16,20},{20,16},{24,28},{28,24},{32,36},... | collective-permute-start | bytes 786440 | tf_op jit(solution)/shard_map/ppermute | solution.py:28
  27.6 1.3 %collective-permute-done.2.refs_8_ = bf16[256,512]{1,0:T(8,128)(2,1)} collective-permute-done((bf16[256,512]{1,0:T(8,128)(2,1)S(1)}, bf16[256,512]{1,0:T(8,128)(2,1)}, u32[]{:S(2)}, u32[]{:S(2)}) %collective-permute-start.2) | collective-permute-done | bytes 262176 | tf_op jit(solution)/shard_map/ppermute | solution.py:28
  28.9 1.6 %copy-done.12 = f32[256,2048]{1,0:T(8,128)S(1)} copy-done((f32[256,2048]{1,0:T(8,128)S(1)}, f32[256,2048]{1,0:T(8,128)}, u32[]{:S(2)}) %copy-start.12) | copy-done | bytes 2097176
  30.5 1.6 %copy-done.14 = f32[256,2048]{1,0:T(8,128)S(1)} copy-done((f32[256,2048]{1,0:T(8,128)S(1)}, f32[256,2048]{1,0:T(8,128)}, u32[]{:S(2)}) %copy-start.14) | copy-done | bytes 2097176
  32.1 1.6 %copy-done.16 = f32[256,2048]{1,0:T(8,128)S(1)} copy-done((f32[256,2048]{1,0:T(8,128)S(1)}, f32[256,2048]{1,0:T(8,128)}, u32[]{:S(2)}) %copy-start.16) | copy-done | bytes 2097176
  33.7 1.2 %copy-done.18 = f32[256,1024]{1,0:T(8,128)S(1)} copy-done((f32[256,1024]{1,0:T(8,128)S(1)}, f32[256,1024]{1,0:T(8,128)}, u32[]{:S(2)}) %copy-start.18) | copy-done | bytes 1048600
  34.9 15.8 %far.1 = (bf16[64,2048]{1,0:T(8,128)(2,1)}, bf16[64,2048]{1,0:T(8,128)(2,1)}, bf16[64,2048]{1,0:T(8,128)(2,1)}, bf16[64,2048]{1,0:T(8,128)(2,1)}, bf16[256,2048]...) custom-call(s32[1]{0:T(128)} %bitcast.turn, ...), custom_call_target="tpu_custom_call" | custom-call | flops 6442450944 | bytes 1048576 | tf_op jit(solution)/shard_map/far/pallas_call | solution.py:256
  51.2 2.9 %collective-permute-start.8 = (bf16[64,2048]{1,0:T(8,128)(2,1)}, bf16[64,2048]{1,0:T(8,128)(2,1)S(1)}, u32[]{:S(2)}, u32[]{:S(2)}) collective-permute-start(bf16[64,2048]{1,0:T(8,128)(2,1)} %get-tuple-element.41), channel_id=1, source_target_pairs={{0,2},{1,3},{2,0},{3,1},{4,6},{5,7},{6,4},{7,5},{8,10},{9,11},{10,... | collective-permute-start | bytes 786440 | tf_op jit(solution)/shard_map/ppermute | solution.py:355
  55.4 4.0 %collective-permute-start.10 = (bf16[256,512]{1,0:T(8,128)(2,1)S(1)}, bf16[256,512]{1,0:T(8,128)(2,1)S(1)}, u32[]{:S(2)}, u32[]{:S(2)}) collective-permute-start(bf16[256,512]{1,0:T(8,128)(2,1)S(1)} %get-tuple-element.46), channel_id=1, source_target_pairs={{0,248},{4,252},{8,0},{12,4},{16,8},{20,12},{24,16},{28,20},{32,24... | collective-permute-start | bytes 786440 | tf_op jit(solution)/shard_map/ppermute | solution.py:28
  59.8 2.3 %collective-permute-start.9 = (bf16[64,2048]{1,0:T(8,128)(2,1)}, bf16[64,2048]{1,0:T(8,128)(2,1)S(1)}, u32[]{:S(2)}, u32[]{:S(2)}) collective-permute-start(bf16[64,2048]{1,0:T(8,128)(2,1)} %get-tuple-element.48), channel_id=1, source_target_pairs={{0,3},{1,0},{2,1},{3,2},{4,7},{5,4},{6,5},{7,6},{8,11},{9,8},{10,9... | collective-permute-start | bytes 786440 | tf_op jit(solution)/shard_map/ppermute | solution.py:355
  62.1 1.2 %copy-done.10 = bf16[256,2048]{1,0:T(8,128)(2,1)S(1)} copy-done((bf16[256,2048]{1,0:T(8,128)(2,1)S(1)}, bf16[256,2048]{1,0:T(8,128)(2,1)}, u32[]{:S(2)}) %copy-start.10) | copy-done | bytes 1048600
  64.2 6.4 %own_backward.1 = (bf16[256,2048]{1,0:T(8,128)(2,1)}, f32[256,512]{1,0:T(8,128)S(1)}) custom-call(s32[32]{0:T(128)S(1)} %copy-done.9, s32[1]{0:T(128)} %bitcast.1.here.place, bf16[256,2048]{1,0:T(8,128)(2,1)S(1)} %copy-done.6, bf16[256,2048]{1,0:T(8,128)(2,1)S(1)} %copy-done.7, bf16[256,2048]{1,0:T(8,128)(2,1)S(1)} %copy-done.10, f32[256,128]{1,0:T(8,128)S(1)} %copy-done.19, ...), custom_call_target="tpu_custom_call" | custom-call | flops 1073741824 | bytes 1048576 | tf_op jit(solution)/shard_map/own_backward/pallas_call | solution.py:256
  70.6 4.1 %collective-permute-done.10.two_ref = bf16[256,512]{1,0:T(8,128)(2,1)S(1)} collective-permute-done((bf16[256,512]{1,0:T(8,128)(2,1)S(1)}, bf16[256,512]{1,0:T(8,128)(2,1)S(1)}, u32[]{:S(2)}, u32[]{:S(2)}) %collective-permute-start.10) | collective-permute-done | bytes 262176 | tf_op jit(solution)/shard_map/ppermute | solution.py:28
  (48 shorter events, 7.5 us)
Async XLA Ops:
  0.6 20.8 %collective-permute-start.3 = (bf16[256,256]{1,0:T(8,128)(2,1)}, bf16[256,256]{1,0:T(8,128)(2,1)S(1)}, u32[]{:S(2)}, u32[]{:S(2)}) collective-permute-start(bf16[256,256]{1,0:T(8,128)(2,1)} %v_ref.3), channel_id=1, source_target_pairs={{0,8},{4,12},{8,16},{12,20},{16,24},{20,28},{24,32},{28,36},{32,40... | collective-permute-start | bytes 393224 | tf_op jit(solution)/shard_map/ppermute | solution.py:28
  3.2 18.3 %collective-permute-start.4 = (bf16[256,256]{1,0:T(8,128)(2,1)}, bf16[256,256]{1,0:T(8,128)(2,1)S(1)}, u32[]{:S(2)}, u32[]{:S(2)}) collective-permute-start(bf16[256,256]{1,0:T(8,128)(2,1)} %v_ref.3), channel_id=1, source_target_pairs={{0,16},{4,20},{8,24},{12,28},{16,32},{20,36},{24,40},{28,44},{32,4... | collective-permute-start | bytes 393224 | tf_op jit(solution)/shard_map/ppermute | solution.py:28
  6.2 17.2 %collective-permute-start = (bf16[256,256]{1,0:T(8,128)(2,1)}, bf16[256,256]{1,0:T(8,128)(2,1)S(1)}, u32[]{:S(2)}, u32[]{:S(2)}) collective-permute-start(bf16[256,256]{1,0:T(8,128)(2,1)} %k_ref.3), channel_id=1, source_target_pairs={{0,8},{4,12},{8,16},{12,20},{16,24},{20,28},{24,32},{28,36},{32,40... | collective-permute-start | bytes 393224 | tf_op jit(solution)/shard_map/ppermute | solution.py:28
  9.0 16.7 %collective-permute-start.1 = (bf16[256,256]{1,0:T(8,128)(2,1)}, bf16[256,256]{1,0:T(8,128)(2,1)S(1)}, u32[]{:S(2)}, u32[]{:S(2)}) collective-permute-start(bf16[256,256]{1,0:T(8,128)(2,1)} %k_ref.3), channel_id=1, source_target_pairs={{0,16},{4,20},{8,24},{12,28},{16,32},{20,36},{24,40},{28,44},{32,4... | collective-permute-start | bytes 393224 | tf_op jit(solution)/shard_map/ppermute | solution.py:28
  13.9 15.0 %copy-start.6 = (bf16[256,2048]{1,0:T(8,128)(2,1)S(1)}, bf16[256,2048]{1,0:T(8,128)(2,1)}, u32[]{:S(2)}) copy-start(bf16[256,2048]{1,0:T(8,128)(2,1)} %q_ref.3) | copy-start | bytes 3145732
  13.9 15.0 %copy-start.7 = (bf16[256,2048]{1,0:T(8,128)(2,1)S(1)}, bf16[256,2048]{1,0:T(8,128)(2,1)}, u32[]{:S(2)}) copy-start(bf16[256,2048]{1,0:T(8,128)(2,1)} %g_ref.1) | copy-start | bytes 3145732
  17.4 1.3 %copy-start.11 = (f32[256,2048]{1,0:T(8,128)}, f32[256,2048]{1,0:T(8,128)S(1)}, u32[]{:S(2)}) copy-start(f32[256,2048]{1,0:T(8,128)S(1)} %get-tuple-element.32.refs_2_) | copy-start | bytes 6291460
  20.0 1.4 %copy-start.15 = (f32[256,2048]{1,0:T(8,128)}, f32[256,2048]{1,0:T(8,128)S(1)}, u32[]{:S(2)}) copy-start(f32[256,2048]{1,0:T(8,128)S(1)} %get-tuple-element.34.refs_4_) | copy-start | bytes 6291460
  21.4 4.3 %copy-start.17 = (f32[256,1024]{1,0:T(8,128)}, f32[256,1024]{1,0:T(8,128)S(1)}, u32[]{:S(2)}) copy-start(f32[256,1024]{1,0:T(8,128)S(1)} %get-tuple-element.36.refs_5_) | copy-start | bytes 3145732
  21.5 6.1 %collective-permute-start.5 = (bf16[256,512]{1,0:T(8,128)(2,1)S(1)}, bf16[256,512]{1,0:T(8,128)(2,1)S(1)}, u32[]{:S(2)}, u32[]{:S(2)}) collective-permute-start(bf16[256,512]{1,0:T(8,128)(2,1)S(1)} %choose.3), channel_id=1, source_target_pairs={{0,4},{4,0},{8,12},{12,8},{16,20},{20,16},{24,28},{28,24},{32,36},... | collective-permute-start | bytes 786440 | tf_op jit(solution)/shard_map/ppermute | solution.py:28
  25.7 3.2 %collective-permute-start.2 = (bf16[256,512]{1,0:T(8,128)(2,1)S(1)}, bf16[256,512]{1,0:T(8,128)(2,1)}, u32[]{:S(2)}, u32[]{:S(2)}) collective-permute-start(bf16[256,512]{1,0:T(8,128)(2,1)S(1)} %choose.2), channel_id=1, source_target_pairs={{0,4},{4,0},{8,12},{12,8},{16,20},{20,16},{24,28},{28,24},{32,36},... | collective-permute-start | bytes 786440 | tf_op jit(solution)/shard_map/ppermute | solution.py:28
  28.9 1.6 %copy-start.12 = (f32[256,2048]{1,0:T(8,128)S(1)}, f32[256,2048]{1,0:T(8,128)}, u32[]{:S(2)}) copy-start(f32[256,2048]{1,0:T(8,128)} %copy-done.11) | copy-start | bytes 6291460
  30.5 1.6 %copy-start.14 = (f32[256,2048]{1,0:T(8,128)S(1)}, f32[256,2048]{1,0:T(8,128)}, u32[]{:S(2)}) copy-start(f32[256,2048]{1,0:T(8,128)} %copy-done.13) | copy-start | bytes 6291460
  32.1 1.6 %copy-start.16 = (f32[256,2048]{1,0:T(8,128)S(1)}, f32[256,2048]{1,0:T(8,128)}, u32[]{:S(2)}) copy-start(f32[256,2048]{1,0:T(8,128)} %copy-done.15) | copy-start | bytes 6291460
  34.9 27.2 %copy-start.2 = (bf16[256,256]{1,0:T(8,128)(2,1)S(1)}, bf16[256,256]{1,0:T(8,128)(2,1)}, u32[]{:S(2)}) copy-start(bf16[256,256]{1,0:T(8,128)(2,1)} %k_ref.3) | copy-start | bytes 393220
  34.9 27.2 %copy-start.4 = (bf16[256,256]{1,0:T(8,128)(2,1)S(1)}, bf16[256,256]{1,0:T(8,128)(2,1)}, u32[]{:S(2)}) copy-start(bf16[256,256]{1,0:T(8,128)(2,1)} %v_ref.3) | copy-start | bytes 393220
  34.9 27.2 %copy-start.9 = (s32[32]{0:T(128)S(1)}, s32[32]{0:T(128)}, u32[]{:S(2)}) copy-start(s32[32]{0:T(128)} %lens.3) | copy-start | bytes 388
  50.8 3.4 %collective-permute-start.6 = (bf16[256,1024]{1,0:T(8,128)(2,1)S(1)}, bf16[256,1024]{1,0:T(8,128)(2,1)S(1)}, u32[]{:S(2)}, u32[]{:S(2)}) collective-permute-start(bf16[256,1024]{1,0:T(8,128)(2,1)S(1)} %get-tuple-element.45), channel_id=1, source_target_pairs={{0,4},{4,0},{8,12},{12,8},{16,20},{20,16},{24,28},{28,24},{32,36},... | collective-permute-start | bytes 1572872 | tf_op jit(solution)/shard_map/ppermute | solution.py:28
  51.2 24.3 %collective-permute-start.8 = (bf16[64,2048]{1,0:T(8,128)(2,1)}, bf16[64,2048]{1,0:T(8,128)(2,1)S(1)}, u32[]{:S(2)}, u32[]{:S(2)}) collective-permute-start(bf16[64,2048]{1,0:T(8,128)(2,1)} %get-tuple-element.41), channel_id=1, source_target_pairs={{0,2},{1,3},{2,0},{3,1},{4,6},{5,7},{6,4},{7,5},{8,10},{9,11},{10,... | collective-permute-start | bytes 786440 | tf_op jit(solution)/shard_map/ppermute | solution.py:355
  54.3 16.4 %collective-permute-start.11 = (bf16[256,512]{1,0:T(8,128)(2,1)S(1)}, bf16[256,512]{1,0:T(8,128)(2,1)S(1)}, u32[]{:S(2)}, u32[]{:S(2)}) collective-permute-start(bf16[256,512]{1,0:T(8,128)(2,1)S(1)} %get-tuple-element.52), channel_id=1, source_target_pairs={{0,240},{4,244},{8,248},{12,252},{16,0},{20,4},{24,8},{28,12},{32,... | collective-permute-start | bytes 786440 | tf_op jit(solution)/shard_map/ppermute | solution.py:28
  55.4 19.3 %collective-permute-start.10 = (bf16[256,512]{1,0:T(8,128)(2,1)S(1)}, bf16[256,512]{1,0:T(8,128)(2,1)S(1)}, u32[]{:S(2)}, u32[]{:S(2)}) collective-permute-start(bf16[256,512]{1,0:T(8,128)(2,1)S(1)} %get-tuple-element.46), channel_id=1, source_target_pairs={{0,248},{4,252},{8,0},{12,4},{16,8},{20,12},{24,16},{28,20},{32,24... | collective-permute-start | bytes 786440 | tf_op jit(solution)/shard_map/ppermute | solution.py:28
  59.4 16.1 %collective-permute-start.7 = (bf16[64,2048]{1,0:T(8,128)(2,1)}, bf16[64,2048]{1,0:T(8,128)(2,1)S(1)}, u32[]{:S(2)}, u32[]{:S(2)}) collective-permute-start(bf16[64,2048]{1,0:T(8,128)(2,1)} %get-tuple-element.47), channel_id=1, source_target_pairs={{0,1},{1,2},{2,3},{3,0},{4,5},{5,6},{6,7},{7,4},{8,9},{9,10},{10,1... | collective-permute-start | bytes 786440 | tf_op jit(solution)/shard_map/ppermute | solution.py:355
  59.8 15.7 %collective-permute-start.9 = (bf16[64,2048]{1,0:T(8,128)(2,1)}, bf16[64,2048]{1,0:T(8,128)(2,1)S(1)}, u32[]{:S(2)}, u32[]{:S(2)}) collective-permute-start(bf16[64,2048]{1,0:T(8,128)(2,1)} %get-tuple-element.48), channel_id=1, source_target_pairs={{0,3},{1,0},{2,1},{3,2},{4,7},{5,4},{6,5},{7,6},{8,11},{9,8},{10,9... | collective-permute-start | bytes 786440 | tf_op jit(solution)/shard_map/ppermute | solution.py:355
  64.2 11.3 %copy-start = (bf16[64,2048]{1,0:T(8,128)(2,1)S(1)}, bf16[64,2048]{1,0:T(8,128)(2,1)}, u32[]{:S(2)}) copy-start(bf16[64,2048]{1,0:T(8,128)(2,1)} %get-tuple-element.39.refs_0_) | copy-start | bytes 786436
  (8 other events, 8.4 us)

commit v8 on v6

--- a/solution.py
+++ b/solution.py
@@ -12,7 +12,7 @@
 REACH = 4
 NEG = -1e30
 LOG2E = 1.4426950408889634
-PAIR = 2
+PAIR = 4
 
 
 def dot(a, b):
@@ -94,7 +94,7 @@
     factor = scale * LOG2E
     bias = bias_ref[...]
     for which, to in enumerate((k_all, v_all)):
-        two_ref, four_ref, odd_ref = fars[3 * which : 3 * which + 3]
+        four_ref, two_ref, odd_ref = fars[3 * which : 3 * which + 3]
         for b, (ref, place) in enumerate(((four_ref, 0), (odd_ref, 1), (two_ref, 0), (odd_ref, 0))):
             for n in range(groups):
                 column = (groups * place + n) * width
@@ -188,7 +188,7 @@
             own_ref[:, (2 * n + 1) * width : (2 * n + 2) * width] = dv.T
 
 
-def choose_kernel(scale, place, own_ref, two_ref, four_ref, send_ref):
+def choose_kernel(scale, place, own_ref, four_ref, two_ref, send_ref):
     even = place[0] % 2 == 0
     half = own_ref.shape[1]
 
@@ -261,8 +261,9 @@
     here = place.reshape(1).astype(jnp.int32)
     twos, fours, fars = [], [], []
     for own in (keys, values):
+        fours.append(up(own, 4))
+    for own in (keys, values):
         twos.append(up(own, 2))
-        fours.append(up(own, 4))
     parts, top, total, bias = call(
         own_forward_kernel,
         "own_forward",
@@ -284,11 +285,11 @@
             [((rows, wide), jnp.bfloat16)],
             here,
             own,
+            four,
             two,
-            four,
             scalars=1,
         )[0]
-        fars += [two, four, swapped(send)]
+        fars += [four, two, swapped(send)]
     out, dq_far, keep, two, four, odd = call(
         far_kernel,
         "far",

time: 70 us -> 70.1 us (level)
  starting transfers between devices: 25.5 us -> 21.1 us
  waiting for transfers between devices: 9.33 us -> 13.7 us
    ppermute x9, starting transfers between devices: 21.3 us -> 16.8 us  [moved(): lax.ppermute(value, 'seq', [(source, to(source) % count) for source in ra...]
    ppermute x9, waiting for transfers between devices: 8.55 us -> 11 us  [moved(): lax.ppermute(value, 'seq', [(source, to(source) % count) for source in ra...]
    all_to_all x1, waiting for transfers between devices: 0.78 us -> 2.68 us  [on_device(): lax.all_to_all(out.reshape(split, rows // split, out.shape[1]), 'head', s...]
  transfers between devices with their start and end apart: 10 -> 10, of which waited for: 4 -> 6; matrix products, arithmetic and copies ran while one was open for 3% -> 3% of each run, Pallas kernels for 14% -> 14%
where the time goes in v8:
time: 70.1 us; the launch traced here: 69.7 us
  Pallas kernels  25.7 us (37%)
  starting transfers between devices  21.1 us (30%)
  waiting for transfers between devices  13.7 us (20%)
  local copies, waits for them, and re-layouts  8.5 us (12%)
  between operations  0.75 us (1%)
    pallas_call x7, Pallas kernels, call(): pl.pallas_call(functools.partial(kernel, 1.0 / math.sqrt(HEAD_WIDTH)), in...  25.7 us
    ppermute x9, starting transfers between devices, moved(): lax.ppermute(value, 'seq', [(source, to(source) % count) for source in ra...  16.8 us
    ppermute x9, waiting for transfers between devices, moved(): lax.ppermute(value, 'seq', [(source, to(source) % count) for source in ra...  11 us
    unnamed x24, local copies, waits for them, and re-layouts  6.2 us
    all_to_all x1, starting transfers between devices, on_device(): lax.all_to_all(out.reshape(split, rows // split, out.shape[1]), 'head', s...  4.24 us
    all_to_all x1, waiting for transfers between devices, on_device(): lax.all_to_all(out.reshape(split, rows // split, out.shape[1]), 'head', s...  2.68 us
    reshape x1, local copies, waits for them, and re-layouts, on_device(): attn_out = jnp.transpose(got, (1, 0, 2)).reshape(got.shape[1], -1)  2.3 us
  transfers between devices with their start and end apart: 10, of which 6 were waited for; matrix products, arithmetic and copies ran while one was open for 3% of the time, Pallas kernels for 14%

profile of v8, /device:TPU:1, one launch (start us, length us, event | category | flops | bytes accessed | tf_op | source)
XLA Modules:
  0.0 69.7 jit_solution(15084327276824106293)
XLA Ops:
  0.6 3.9 %collective-permute-start.3 = (bf16[256,256]{1,0:T(8,128)(2,1)}, bf16[256,256]{1,0:T(8,128)(2,1)S(1)}, u32[]{:S(2)}, u32[]{:S(2)}) collective-permute-start(bf16[256,256]{1,0:T(8,128)(2,1)} %v_ref.3), channel_id=1, source_target_pairs={{0,16},{4,20},{8,24},{12,28},{16,32},{20,36},{24,40},{28,44},{32,4... | collective-permute-start | bytes 393224 | tf_op jit(solution)/shard_map/ppermute | solution.py:28
  4.5 1.6 %collective-permute-start.4 = (bf16[256,256]{1,0:T(8,128)(2,1)}, bf16[256,256]{1,0:T(8,128)(2,1)S(1)}, u32[]{:S(2)}, u32[]{:S(2)}) collective-permute-start(bf16[256,256]{1,0:T(8,128)(2,1)} %v_ref.3), channel_id=1, source_target_pairs={{0,8},{4,12},{8,16},{12,20},{16,24},{20,28},{24,32},{28,36},{32,40... | collective-permute-start | bytes 393224 | tf_op jit(solution)/shard_map/ppermute | solution.py:28
  6.2 3.3 %collective-permute-start = (bf16[256,256]{1,0:T(8,128)(2,1)}, bf16[256,256]{1,0:T(8,128)(2,1)S(1)}, u32[]{:S(2)}, u32[]{:S(2)}) collective-permute-start(bf16[256,256]{1,0:T(8,128)(2,1)} %k_ref.3), channel_id=1, source_target_pairs={{0,16},{4,20},{8,24},{12,28},{16,32},{20,36},{24,40},{28,44},{32,4... | collective-permute-start | bytes 393224 | tf_op jit(solution)/shard_map/ppermute | solution.py:28
  10.2 0.9 %copy-done = bf16[256,256]{1,0:T(8,128)(2,1)S(1)} copy-done((bf16[256,256]{1,0:T(8,128)(2,1)S(1)}, bf16[256,256]{1,0:T(8,128)(2,1)}, u32[]{:S(2)}) %copy-start) | copy-done | bytes 131096
  11.1 0.9 %copy-done.2 = bf16[256,256]{1,0:T(8,128)(2,1)S(1)} copy-done((bf16[256,256]{1,0:T(8,128)(2,1)S(1)}, bf16[256,256]{1,0:T(8,128)(2,1)}, u32[]{:S(2)}) %copy-start.2) | copy-done | bytes 131096
  12.1 1.2 %copy-done.4 = bf16[256,2048]{1,0:T(8,128)(2,1)S(1)} copy-done((bf16[256,2048]{1,0:T(8,128)(2,1)S(1)}, bf16[256,2048]{1,0:T(8,128)(2,1)}, u32[]{:S(2)}) %copy-start.4) | copy-done | bytes 1048600
  13.9 3.5 %own_forward.1 = (f32[256,2048]{1,0:T(8,128)S(1)}, f32[256,2048]{1,0:T(8,128)S(1)}, f32[256,2048]{1,0:T(8,128)S(1)}, f32[256,1024]{1,0:T(8,128)S(1)}) custom-call(s32[32]{0:T(128)S(1)} %copy-done.8, s32[1]{0:T(128)} %bitcast.here.place, bf16[256,2048]{1,0:T(8,128)(2,1)S(1)} %copy-done.4, bf16[256,256]{1,0:T(8,128)(2,1)S(1)} %copy-done, ...), custom_call_target="tpu_custom_call" | custom-call | flops 536870912 | bytes 1048576 | tf_op jit(solution)/shard_map/own_forward/pallas_call | solution.py:238
  17.4 1.3 %collective-permute-done.4.two_ref.refs_10_ = bf16[256,256]{1,0:T(8,128)(2,1)S(1)} collective-permute-done((bf16[256,256]{1,0:T(8,128)(2,1)}, bf16[256,256]{1,0:T(8,128)(2,1)S(1)}, u32[]{:S(2)}, u32[]{:S(2)}) %collective-permute-start.4) | collective-permute-done | bytes 131104 | tf_op jit(solution)/shard_map/ppermute | solution.py:28
  18.7 2.4 %collective-permute-start.5 = (bf16[256,512]{1,0:T(8,128)(2,1)S(1)}, bf16[256,512]{1,0:T(8,128)(2,1)S(1)}, u32[]{:S(2)}, u32[]{:S(2)}) collective-permute-start(bf16[256,512]{1,0:T(8,128)(2,1)S(1)} %choose.3), channel_id=1, source_target_pairs={{0,4},{4,0},{8,12},{12,8},{16,20},{20,16},{24,28},{28,24},{32,36},... | collective-permute-start | bytes 786440 | tf_op jit(solution)/shard_map/ppermute | solution.py:28
  21.1 0.9 %collective-permute-done.four_ref.refs_6_ = bf16[256,256]{1,0:T(8,128)(2,1)S(1)} collective-permute-done((bf16[256,256]{1,0:T(8,128)(2,1)}, bf16[256,256]{1,0:T(8,128)(2,1)S(1)}, u32[]{:S(2)}, u32[]{:S(2)}) %collective-permute-start) | collective-permute-done | bytes 131104 | tf_op jit(solution)/shard_map/ppermute | solution.py:28
  21.9 5.2 %collective-permute-done.1.two_ref.refs_7_ = bf16[256,256]{1,0:T(8,128)(2,1)S(1)} collective-permute-done((bf16[256,256]{1,0:T(8,128)(2,1)}, bf16[256,256]{1,0:T(8,128)(2,1)S(1)}, u32[]{:S(2)}, u32[]{:S(2)}) %collective-permute-start.1) | collective-permute-done | bytes 131104 | tf_op jit(solution)/shard_map/ppermute | solution.py:28
  27.1 1.2 %collective-permute-start.2 = (bf16[256,512]{1,0:T(8,128)(2,1)S(1)}, bf16[256,512]{1,0:T(8,128)(2,1)S(1)}, u32[]{:S(2)}, u32[]{:S(2)}) collective-permute-start(bf16[256,512]{1,0:T(8,128)(2,1)S(1)} %choose.2), channel_id=1, source_target_pairs={{0,4},{4,0},{8,12},{12,8},{16,20},{20,16},{24,28},{28,24},{32,36},... | collective-permute-start | bytes 786440 | tf_op jit(solution)/shard_map/ppermute | solution.py:28
  28.3 1.2 %collective-permute-done.2.refs_8_ = bf16[256,512]{1,0:T(8,128)(2,1)S(1)} collective-permute-done((bf16[256,512]{1,0:T(8,128)(2,1)S(1)}, bf16[256,512]{1,0:T(8,128)(2,1)S(1)}, u32[]{:S(2)}, u32[]{:S(2)}) %collective-permute-start.2) | collective-permute-done | bytes 262176 | tf_op jit(solution)/shard_map/ppermute | solution.py:28
  29.5 14.9 %far.1 = (bf16[256,2048]{1,0:T(8,128)(2,1)}, bf16[256,2048]{1,0:T(8,128)(2,1)}, f32[256,128]{1,0:T(8,128)}, f32[256,512]{1,0:T(8,128)S(1)}, f32[256,512]{1,0:T(8,128)S(1)}, /*index=5*/bf16[256,1024]{1,0:T(8,128)(2,1)S(1)}) custom-call(bf16[256,2048]{1,0:T(8,128)(2,1)S(1)} %copy-done.5, bf16[256,2048]{1,0:T(8,128)(2,1)S(1)} %copy-done.6, ...), custom_call_target="tpu_custom_call" | custom-call | flops 6442450944 | bytes 1048576 | tf_op jit(solution)/shard_map/far/pallas_call | solution.py:238
  44.9 4.2 %all-to-all-start = ((bf16[4,64,2048]{2,1,0:T(8,128)(2,1)}), bf16[4,64,2048]{2,1,0:T(8,128)(2,1)}, u32[]{:S(2)}, u32[]{:S(2)}) async-start(bf16[4,64,2048]{2,1,0:T(8,128)(2,1)} %bitcast.5), calls=%async_computation | async-start | bytes 2097152 | tf_op jit(solution)/shard_map/all_to_all | solution.py:331
  49.3 2.4 %collective-permute-start.8 = (bf16[256,512]{1,0:T(8,128)(2,1)S(1)}, bf16[256,512]{1,0:T(8,128)(2,1)S(1)}, u32[]{:S(2)}, u32[]{:S(2)}) collective-permute-start(bf16[256,512]{1,0:T(8,128)(2,1)S(1)} %get-tuple-element.41), channel_id=1, source_target_pairs={{0,240},{4,244},{8,248},{12,252},{16,0},{20,4},{24,8},{28,12},{32,... | collective-permute-start | bytes 786440 | tf_op jit(solution)/shard_map/ppermute | solution.py:28
  51.7 0.8 %collective-permute-start.7 = (bf16[256,512]{1,0:T(8,128)(2,1)S(1)}, bf16[256,512]{1,0:T(8,128)(2,1)S(1)}, u32[]{:S(2)}, u32[]{:S(2)}) collective-permute-start(bf16[256,512]{1,0:T(8,128)(2,1)S(1)} %get-tuple-element.37), channel_id=1, source_target_pairs={{0,248},{4,252},{8,0},{12,4},{16,8},{20,12},{24,16},{28,20},{32,24... | collective-permute-start | bytes 786440 | tf_op jit(solution)/shard_map/ppermute | solution.py:28
  52.5 1.2 %copy-done.7 = bf16[256,2048]{1,0:T(8,128)(2,1)S(1)} copy-done((bf16[256,2048]{1,0:T(8,128)(2,1)S(1)}, bf16[256,2048]{1,0:T(8,128)(2,1)}, u32[]{:S(2)}) %copy-start.7) | copy-done | bytes 1048600
  53.7 1.2 %copy-done.10 = bf16[256,2048]{1,0:T(8,128)(2,1)S(1)} copy-done((bf16[256,2048]{1,0:T(8,128)(2,1)S(1)}, bf16[256,2048]{1,0:T(8,128)(2,1)}, u32[]{:S(2)}) %copy-start.10) | copy-done | bytes 1048600
  54.9 6.4 %own_backward.1 = (bf16[256,2048]{1,0:T(8,128)(2,1)}, f32[256,512]{1,0:T(8,128)S(1)}) custom-call(s32[32]{0:T(128)S(1)} %copy-done.9, s32[1]{0:T(128)} %bitcast.here.place, bf16[256,2048]{1,0:T(8,128)(2,1)S(1)} %copy-done.5, bf16[256,2048]{1,0:T(8,128)(2,1)S(1)} %copy-done.7, bf16[256,2048]{1,0:T(8,128)(2,1)S(1)} %copy-done.10, f32[256,128]{1,0:T(8,128)S(1)} %copy-done.11, ...), custom_call_target="tpu_custom_call" | custom-call | flops 1073741824 | bytes 1048576 | tf_op jit(solution)/shard_map/own_backward/pallas_call | solution.py:238
  61.4 2.7 %all-to-all-done = bf16[4,64,2048]{2,1,0:T(8,128)(2,1)} async-done(((bf16[4,64,2048]{2,1,0:T(8,128)(2,1)}), bf16[4,64,2048]{2,1,0:T(8,128)(2,1)}, u32[]{:S(2)}, u32[]{:S(2)}) %all-to-all-start) | async-done | bytes 1048608 | tf_op jit(solution)/shard_map/all_to_all | solution.py:331
  64.0 2.3 %copy.10 = bf16[4,8,8,2048]{3,2,0,1:T(8,128)(2,1)} copy(bf16[4,8,8,2048]{3,2,1,0:T(8,128)(2,1)} %bitcast.3) | data formatting | bytes 2097152 | tf_op jit(solution)/shard_map/reshape | solution.py:362
  66.3 2.6 %collective-permute-done.7.two_ref = bf16[256,512]{1,0:T(8,128)(2,1)S(1)} collective-permute-done((bf16[256,512]{1,0:T(8,128)(2,1)S(1)}, bf16[256,512]{1,0:T(8,128)(2,1)S(1)}, u32[]{:S(2)}, u32[]{:S(2)}) %collective-permute-start.7) | collective-permute-done | bytes 262176 | tf_op jit(solution)/shard_map/ppermute | solution.py:28
  68.9 0.8 %total.1 = (bf16[256,256]{1,0:T(8,128)(2,1)}, bf16[256,256]{1,0:T(8,128)(2,1)}) custom-call(s32[1]{0:T(128)} %bitcast.here.place, f32[256,512]{1,0:T(8,128)S(1)} %get-tuple-element.40.own_ref, bf16[256,1024]{1,0:T(8,128)(2,1)S(1)} %collective-permute-done.6.other_ref, bf16[256,512]{1,0:T(8,128)(2,1)S(1)} %collective-permute-done.7.two_ref, ...), custom_call_target="tpu_custom_call" | custom-call | bytes 1048576 | tf_op jit(solution)/shard_map/total/pallas_call | solution.py:238
  (28 shorter events, 2.1 us)
Async XLA Ops:
  0.6 16.8 %collective-permute-start.3 = (bf16[256,256]{1,0:T(8,128)(2,1)}, bf16[256,256]{1,0:T(8,128)(2,1)S(1)}, u32[]{:S(2)}, u32[]{:S(2)}) collective-permute-start(bf16[256,256]{1,0:T(8,128)(2,1)} %v_ref.3), channel_id=1, source_target_pairs={{0,16},{4,20},{8,24},{12,28},{16,32},{20,36},{24,40},{28,44},{32,4... | collective-permute-start | bytes 393224 | tf_op jit(solution)/shard_map/ppermute | solution.py:28
  4.5 14.1 %collective-permute-start.4 = (bf16[256,256]{1,0:T(8,128)(2,1)}, bf16[256,256]{1,0:T(8,128)(2,1)S(1)}, u32[]{:S(2)}, u32[]{:S(2)}) collective-permute-start(bf16[256,256]{1,0:T(8,128)(2,1)} %v_ref.3), channel_id=1, source_target_pairs={{0,8},{4,12},{8,16},{12,20},{16,24},{20,28},{24,32},{28,36},{32,40... | collective-permute-start | bytes 393224 | tf_op jit(solution)/shard_map/ppermute | solution.py:28
  6.2 15.8 %collective-permute-start = (bf16[256,256]{1,0:T(8,128)(2,1)}, bf16[256,256]{1,0:T(8,128)(2,1)S(1)}, u32[]{:S(2)}, u32[]{:S(2)}) collective-permute-start(bf16[256,256]{1,0:T(8,128)(2,1)} %k_ref.3), channel_id=1, source_target_pairs={{0,16},{4,20},{8,24},{12,28},{16,32},{20,36},{24,40},{28,44},{32,4... | collective-permute-start | bytes 393224 | tf_op jit(solution)/shard_map/ppermute | solution.py:28
  9.5 17.6 %collective-permute-start.1 = (bf16[256,256]{1,0:T(8,128)(2,1)}, bf16[256,256]{1,0:T(8,128)(2,1)S(1)}, u32[]{:S(2)}, u32[]{:S(2)}) collective-permute-start(bf16[256,256]{1,0:T(8,128)(2,1)} %k_ref.3), channel_id=1, source_target_pairs={{0,8},{4,12},{8,16},{12,20},{16,24},{20,28},{24,32},{28,36},{32,40... | collective-permute-start | bytes 393224 | tf_op jit(solution)/shard_map/ppermute | solution.py:28
  10.2 0.9 %copy-start = (bf16[256,256]{1,0:T(8,128)(2,1)S(1)}, bf16[256,256]{1,0:T(8,128)(2,1)}, u32[]{:S(2)}) copy-start(bf16[256,256]{1,0:T(8,128)(2,1)} %k_ref.3) | copy-start | bytes 393220
  11.1 0.9 %copy-start.2 = (bf16[256,256]{1,0:T(8,128)(2,1)S(1)}, bf16[256,256]{1,0:T(8,128)(2,1)}, u32[]{:S(2)}) copy-start(bf16[256,256]{1,0:T(8,128)(2,1)} %v_ref.3) | copy-start | bytes 393220
  12.1 1.2 %copy-start.4 = (bf16[256,2048]{1,0:T(8,128)(2,1)S(1)}, bf16[256,2048]{1,0:T(8,128)(2,1)}, u32[]{:S(2)}) copy-start(bf16[256,2048]{1,0:T(8,128)(2,1)} %q_ref.3) | copy-start | bytes 3145732
  13.3 0.7 copy-start.8
  13.9 15.5 %copy-start.5 = (bf16[256,2048]{1,0:T(8,128)(2,1)S(1)}, bf16[256,2048]{1,0:T(8,128)(2,1)}, u32[]{:S(2)}) copy-start(bf16[256,2048]{1,0:T(8,128)(2,1)} %q_ref.3) | copy-start | bytes 3145732
  13.9 15.5 %copy-start.6 = (bf16[256,2048]{1,0:T(8,128)(2,1)S(1)}, bf16[256,2048]{1,0:T(8,128)(2,1)}, u32[]{:S(2)}) copy-start(bf16[256,2048]{1,0:T(8,128)(2,1)} %g_ref.1) | copy-start | bytes 3145732
  18.7 9.6 %collective-permute-start.5 = (bf16[256,512]{1,0:T(8,128)(2,1)S(1)}, bf16[256,512]{1,0:T(8,128)(2,1)S(1)}, u32[]{:S(2)}, u32[]{:S(2)}) collective-permute-start(bf16[256,512]{1,0:T(8,128)(2,1)S(1)} %choose.3), channel_id=1, source_target_pairs={{0,4},{4,0},{8,12},{12,8},{16,20},{20,16},{24,28},{28,24},{32,36},... | collective-permute-start | bytes 786440 | tf_op jit(solution)/shard_map/ppermute | solution.py:28
  27.1 2.4 %collective-permute-start.2 = (bf16[256,512]{1,0:T(8,128)(2,1)S(1)}, bf16[256,512]{1,0:T(8,128)(2,1)S(1)}, u32[]{:S(2)}, u32[]{:S(2)}) collective-permute-start(bf16[256,512]{1,0:T(8,128)(2,1)S(1)} %choose.2), channel_id=1, source_target_pairs={{0,4},{4,0},{8,12},{12,8},{16,20},{20,16},{24,28},{28,24},{32,36},... | collective-permute-start | bytes 786440 | tf_op jit(solution)/shard_map/ppermute | solution.py:28
  44.4 8.1 %copy-start.1 = (bf16[256,256]{1,0:T(8,128)(2,1)S(1)}, bf16[256,256]{1,0:T(8,128)(2,1)}, u32[]{:S(2)}) copy-start(bf16[256,256]{1,0:T(8,128)(2,1)} %k_ref.3) | copy-start | bytes 393220
  44.4 8.1 %copy-start.3 = (bf16[256,256]{1,0:T(8,128)(2,1)S(1)}, bf16[256,256]{1,0:T(8,128)(2,1)}, u32[]{:S(2)}) copy-start(bf16[256,256]{1,0:T(8,128)(2,1)} %v_ref.3) | copy-start | bytes 393220
  44.4 8.1 %copy-start.9 = (s32[32]{0:T(128)S(1)}, s32[32]{0:T(128)}, u32[]{:S(2)}) copy-start(s32[32]{0:T(128)} %lens.3) | copy-start | bytes 388
  44.4 8.1 %copy-start.11 = (f32[256,128]{1,0:T(8,128)S(1)}, f32[256,128]{1,0:T(8,128)}, u32[]{:S(2)}) copy-start(f32[256,128]{1,0:T(8,128)} %get-tuple-element.38.keep_ref) | copy-start | bytes 393220
  44.4 4.7 %collective-permute-start.6 = (bf16[256,1024]{1,0:T(8,128)(2,1)S(1)}, bf16[256,1024]{1,0:T(8,128)(2,1)S(1)}, u32[]{:S(2)}, u32[]{:S(2)}) collective-permute-start(bf16[256,1024]{1,0:T(8,128)(2,1)S(1)} %get-tuple-element.36), channel_id=1, source_target_pairs={{0,4},{4,0},{8,12},{12,8},{16,20},{20,16},{24,28},{28,24},{32,36},... | collective-permute-start | bytes 1572872 | tf_op jit(solution)/shard_map/ppermute | solution.py:28
  44.9 19.1 %all-to-all-start = ((bf16[4,64,2048]{2,1,0:T(8,128)(2,1)}), bf16[4,64,2048]{2,1,0:T(8,128)(2,1)}, u32[]{:S(2)}, u32[]{:S(2)}) async-start(bf16[4,64,2048]{2,1,0:T(8,128)(2,1)} %bitcast.5), calls=%async_computation | async-start | bytes 2097152 | tf_op jit(solution)/shard_map/all_to_all | solution.py:331
  49.3 17.1 %collective-permute-start.8 = (bf16[256,512]{1,0:T(8,128)(2,1)S(1)}, bf16[256,512]{1,0:T(8,128)(2,1)S(1)}, u32[]{:S(2)}, u32[]{:S(2)}) collective-permute-start(bf16[256,512]{1,0:T(8,128)(2,1)S(1)} %get-tuple-element.41), channel_id=1, source_target_pairs={{0,240},{4,244},{8,248},{12,252},{16,0},{20,4},{24,8},{28,12},{32,... | collective-permute-start | bytes 786440 | tf_op jit(solution)/shard_map/ppermute | solution.py:28
  51.7 17.2 %collective-permute-start.7 = (bf16[256,512]{1,0:T(8,128)(2,1)S(1)}, bf16[256,512]{1,0:T(8,128)(2,1)S(1)}, u32[]{:S(2)}, u32[]{:S(2)}) collective-permute-start(bf16[256,512]{1,0:T(8,128)(2,1)S(1)} %get-tuple-element.37), channel_id=1, source_target_pairs={{0,248},{4,252},{8,0},{12,4},{16,8},{20,12},{24,16},{28,20},{32,24... | collective-permute-start | bytes 786440 | tf_op jit(solution)/shard_map/ppermute | solution.py:28
  52.5 1.2 %copy-start.7 = (bf16[256,2048]{1,0:T(8,128)(2,1)S(1)}, bf16[256,2048]{1,0:T(8,128)(2,1)}, u32[]{:S(2)}) copy-start(bf16[256,2048]{1,0:T(8,128)(2,1)} %g_ref.1) | copy-start | bytes 3145732
  53.7 1.2 %copy-start.10 = (bf16[256,2048]{1,0:T(8,128)(2,1)S(1)}, bf16[256,2048]{1,0:T(8,128)(2,1)}, u32[]{:S(2)}) copy-start(bf16[256,2048]{1,0:T(8,128)(2,1)} %get-tuple-element.32.far_ref) | copy-start | bytes 3145732

commit v9 on v6

--- a/solution.py
+++ b/solution.py
@@ -164,13 +164,14 @@
 
 
 def own_backward_kernel(
-    scale, lens, here, q_ref, g_ref, far_ref, keep_ref, k_ref, v_ref, dq_ref, own_ref
+    scale, lens, here, q_ref, g_ref, far_ref, keep_ref, k_ref, v_ref, other_ref, dq_ref, own_ref
 ):
     rows, width = q_ref.shape[0], HEAD_WIDTH
     heads = q_ref.shape[1] // width
     share = q_ref.shape[1] // k_ref.shape[1]
     factor = scale * LOG2E
     bias = near_mask(first_seen(lens, here, rows, width), rows)
+    one = jnp.where(here[0] % 2 == 0, 1.0, 0.0)
     for h in range(heads):
         n = h // share
         at = slice(h * width, (h + 1) * width)
@@ -184,8 +185,9 @@
         dk_part, dv_part = dot(q.T, ds), dot(g.T, p.astype(jnp.bfloat16))
         dk, dv = (dk_part, dv_part) if h % share == 0 else (dk + dk_part, dv + dv_part)
         if h % share == share - 1:
-            own_ref[:, 2 * n * width : (2 * n + 1) * width] = dk.T * scale
-            own_ref[:, (2 * n + 1) * width : (2 * n + 2) * width] = dv.T
+            for which, grad in enumerate((dk.T * scale, dv.T)):
+                to = slice((2 * n + which) * width, (2 * n + which + 1) * width)
+                own_ref[:, to] = grad + other_ref[:, to].astype(jnp.float32) * one
 
 
 def choose_kernel(scale, place, own_ref, two_ref, four_ref, send_ref):
@@ -221,14 +223,12 @@
         four_out[...] = (four_ref[...] + three).astype(jnp.bfloat16)
 
 
-def total_kernel(scale, place, own_ref, other_ref, two_ref, four_ref, k_out, v_out):
+def total_kernel(scale, own_ref, two_ref, four_ref, k_out, v_out):
     width = HEAD_WIDTH
-    one = jnp.where(place[0] % 2 == 0, 1.0, 0.0)
     for n in range(k_out.shape[1] // width):
         for which, ref in enumerate((k_out, v_out)):
             at = slice((2 * n + which) * width, (2 * n + which + 1) * width)
-            total = own_ref[:, at] + other_ref[:, at].astype(jnp.float32) * one
-            total = total + two_ref[:, at].astype(jnp.float32) + four_ref[:, at].astype(jnp.float32)
+            total = own_ref[:, at] + two_ref[:, at].astype(jnp.float32) + four_ref[:, at].astype(jnp.float32)
             ref[:, n * width : (n + 1) * width] = total.astype(jnp.bfloat16)
 
 
@@ -344,6 +344,7 @@
         keep,
         keys,
         values,
+        other,
         scalars=2,
     )
     key_gradient, value_gradient = call(
@@ -351,12 +352,9 @@
         "total",
         0,
         [(keys.shape, jnp.bfloat16)] * 2,
-        here,
         own,
-        other,
         two_back,
         four_back,
-        scalars=1,
     )
     attn_out = jnp.transpose(got, (1, 0, 2)).reshape(got.shape[1], -1)
     return (attn_out, d_queries, key_gradient, value_gradient)

time: 70 us -> 73.9 us (1.056)
  Pallas kernels: 25.5 us -> 27.2 us
  waiting for transfers between devices: 9.33 us -> 11 us
    ppermute x9, waiting for transfers between devices: 8.55 us -> 10.6 us  [moved(): lax.ppermute(value, 'seq', [(source, to(source) % count) for source in ra...]
    pallas_call x7, Pallas kernels: 25.5 us -> 27.2 us  [call(): pl.pallas_call(functools.partial(kernel, 1.0 / math.sqrt(HEAD_WIDTH)), in...]
    unnamed x24 -> x26, local copies, waits for them, and re-layouts: 6.2 us -> 6.74 us
where the time goes in v9:
time: 73.9 us; the launch traced here: 73.5 us
  Pallas kernels  27.2 us (37%)
  starting transfers between devices  25.6 us (35%)
  waiting for transfers between devices  11 us (15%)
  local copies, waits for them, and re-layouts  9.05 us (12%)
    pallas_call x7, Pallas kernels, call(): pl.pallas_call(functools.partial(kernel, 1.0 / math.sqrt(HEAD_WIDTH)), in...  27.2 us
    ppermute x9, starting transfers between devices, moved(): lax.ppermute(value, 'seq', [(source, to(source) % count) for source in ra...  21.4 us
    ppermute x9, waiting for transfers between devices, moved(): lax.ppermute(value, 'seq', [(source, to(source) % count) for source in ra...  10.6 us
    unnamed x26, local copies, waits for them, and re-layouts  6.74 us
    all_to_all x1, starting transfers between devices, on_device(): lax.all_to_all(out.reshape(split, rows // split, out.shape[1]), 'head', s...  4.26 us
    reshape x1, local copies, waits for them, and re-layouts, on_device(): attn_out = jnp.transpose(got, (1, 0, 2)).reshape(got.shape[1], -1)  2.3 us
  transfers between devices with their start and end apart: 10, of which 4 were waited for; matrix products, arithmetic and copies ran while one was open for 3% of the time, Pallas kernels for 14%

profile of v9, /device:TPU:1, one launch (start us, length us, event | category | flops | bytes accessed | tf_op | source)
XLA Modules:
  0.0 73.5 jit_solution(14206914597625803386)
XLA Ops:
  0.6 2.5 %collective-permute-start.3 = (bf16[256,256]{1,0:T(8,128)(2,1)}, bf16[256,256]{1,0:T(8,128)(2,1)S(1)}, u32[]{:S(2)}, u32[]{:S(2)}) collective-permute-start(bf16[256,256]{1,0:T(8,128)(2,1)} %v_ref.3), channel_id=1, source_target_pairs={{0,8},{4,12},{8,16},{12,20},{16,24},{20,28},{24,32},{28,36},{32,40... | collective-permute-start | bytes 393224 | tf_op jit(solution)/shard_map/ppermute | solution.py:28
  3.2 3.0 %collective-permute-start.4 = (bf16[256,256]{1,0:T(8,128)(2,1)}, bf16[256,256]{1,0:T(8,128)(2,1)S(1)}, u32[]{:S(2)}, u32[]{:S(2)}) collective-permute-start(bf16[256,256]{1,0:T(8,128)(2,1)} %v_ref.3), channel_id=1, source_target_pairs={{0,16},{4,20},{8,24},{12,28},{16,32},{20,36},{24,40},{28,44},{32,4... | collective-permute-start | bytes 393224 | tf_op jit(solution)/shard_map/ppermute | solution.py:28
  6.2 2.8 %collective-permute-start = (bf16[256,256]{1,0:T(8,128)(2,1)}, bf16[256,256]{1,0:T(8,128)(2,1)S(1)}, u32[]{:S(2)}, u32[]{:S(2)}) collective-permute-start(bf16[256,256]{1,0:T(8,128)(2,1)} %k_ref.3), channel_id=1, source_target_pairs={{0,8},{4,12},{8,16},{12,20},{16,24},{20,28},{24,32},{28,36},{32,40... | collective-permute-start | bytes 393224 | tf_op jit(solution)/shard_map/ppermute | solution.py:28
  9.0 1.2 %collective-permute-start.1 = (bf16[256,256]{1,0:T(8,128)(2,1)}, bf16[256,256]{1,0:T(8,128)(2,1)S(1)}, u32[]{:S(2)}, u32[]{:S(2)}) collective-permute-start(bf16[256,256]{1,0:T(8,128)(2,1)} %k_ref.3), channel_id=1, source_target_pairs={{0,16},{4,20},{8,24},{12,28},{16,32},{20,36},{24,40},{28,44},{32,4... | collective-permute-start | bytes 393224 | tf_op jit(solution)/shard_map/ppermute | solution.py:28
  10.2 1.2 %copy-done = bf16[256,2048]{1,0:T(8,128)(2,1)S(1)} copy-done((bf16[256,2048]{1,0:T(8,128)(2,1)S(1)}, bf16[256,2048]{1,0:T(8,128)(2,1)}, u32[]{:S(2)}) %copy-start) | copy-done | bytes 1048600
  11.4 0.9 %copy-done.6 = bf16[256,256]{1,0:T(8,128)(2,1)S(1)} copy-done((bf16[256,256]{1,0:T(8,128)(2,1)S(1)}, bf16[256,256]{1,0:T(8,128)(2,1)}, u32[]{:S(2)}) %copy-start.6) | copy-done | bytes 131096
  12.3 0.9 %copy-done.8 = bf16[256,256]{1,0:T(8,128)(2,1)S(1)} copy-done((bf16[256,256]{1,0:T(8,128)(2,1)S(1)}, bf16[256,256]{1,0:T(8,128)(2,1)}, u32[]{:S(2)}) %copy-start.8) | copy-done | bytes 131096
  13.9 3.3 %own_forward.1 = (f32[256,2048]{1,0:T(8,128)S(1)}, f32[256,2048]{1,0:T(8,128)S(1)}, f32[256,2048]{1,0:T(8,128)S(1)}, f32[256,1024]{1,0:T(8,128)S(1)}) custom-call(s32[32]{0:T(128)S(1)} %copy-done.11, s32[1]{0:T(128)} %bitcast.here.place, bf16[256,2048]{1,0:T(8,128)(2,1)S(1)} %copy-done, bf16[256,256]{1,0:T(8,128)(2,1)S(1)} %copy-done.6, ...), custom_call_target="tpu_custom_call" | custom-call | flops 536870912 | bytes 1048576 | tf_op jit(solution)/shard_map/own_forward/pallas_call | solution.py:238
  17.3 4.4 %collective-permute-start.5 = (bf16[256,512]{1,0:T(8,128)(2,1)S(1)}, bf16[256,512]{1,0:T(8,128)(2,1)S(1)}, u32[]{:S(2)}, u32[]{:S(2)}) collective-permute-start(bf16[256,512]{1,0:T(8,128)(2,1)S(1)} %choose.3), channel_id=1, source_target_pairs={{0,4},{4,0},{8,12},{12,8},{16,20},{20,16},{24,28},{28,24},{32,36},... | collective-permute-start | bytes 786440 | tf_op jit(solution)/shard_map/ppermute | solution.py:28
  21.7 4.0 %collective-permute-done.1.four_ref.refs_7_ = bf16[256,256]{1,0:T(8,128)(2,1)S(1)} collective-permute-done((bf16[256,256]{1,0:T(8,128)(2,1)}, bf16[256,256]{1,0:T(8,128)(2,1)S(1)}, u32[]{:S(2)}, u32[]{:S(2)}) %collective-permute-start.1) | collective-permute-done | bytes 131104 | tf_op jit(solution)/shard_map/ppermute | solution.py:28
  25.7 1.9 %collective-permute-start.2 = (bf16[256,512]{1,0:T(8,128)(2,1)S(1)}, bf16[256,512]{1,0:T(8,128)(2,1)S(1)}, u32[]{:S(2)}, u32[]{:S(2)}) collective-permute-start(bf16[256,512]{1,0:T(8,128)(2,1)S(1)} %choose.2), channel_id=1, source_target_pairs={{0,4},{4,0},{8,12},{12,8},{16,20},{20,16},{24,28},{28,24},{32,36},... | collective-permute-start | bytes 786440 | tf_op jit(solution)/shard_map/ppermute | solution.py:28
  27.6 1.2 %collective-permute-done.2.refs_8_ = bf16[256,512]{1,0:T(8,128)(2,1)S(1)} collective-permute-done((bf16[256,512]{1,0:T(8,128)(2,1)S(1)}, bf16[256,512]{1,0:T(8,128)(2,1)S(1)}, u32[]{:S(2)}, u32[]{:S(2)}) %collective-permute-start.2) | collective-permute-done | bytes 262176 | tf_op jit(solution)/shard_map/ppermute | solution.py:28
  28.7 14.7 %far.1 = (bf16[256,2048]{1,0:T(8,128)(2,1)}, bf16[256,2048]{1,0:T(8,128)(2,1)}, f32[256,128]{1,0:T(8,128)}, f32[256,512]{1,0:T(8,128)S(1)}, f32[256,512]{1,0:T(8,128)S(1)}, /*index=5*/bf16[256,1024]{1,0:T(8,128)(2,1)}) custom-call(bf16[256,2048]{1,0:T(8,128)(2,1)S(1)} %copy-done.1, bf16[256,2048]{1,0:T(8,128)(2,1)S(1)} %copy-done.2, ...), custom_call_target="tpu_custom_call" | custom-call | flops 6442450944 | bytes 1048576 | tf_op jit(solution)/shard_map/far/pallas_call | solution.py:238
  43.5 0.8 %copy-done.4 = f32[256,512]{1,0:T(8,128)} copy-done((f32[256,512]{1,0:T(8,128)}, f32[256,512]{1,0:T(8,128)S(1)}, u32[]{:S(2)}) %copy-start.4) | copy-done | bytes 524312
  44.8 4.3 %all-to-all-start = ((bf16[4,64,2048]{2,1,0:T(8,128)(2,1)}), bf16[4,64,2048]{2,1,0:T(8,128)(2,1)}, u32[]{:S(2)}, u32[]{:S(2)}) async-start(bf16[4,64,2048]{2,1,0:T(8,128)(2,1)} %bitcast.5), calls=%async_computation | async-start | bytes 2097152 | tf_op jit(solution)/shard_map/all_to_all | solution.py:330
  49.1 1.0 %copy-done.5 = f32[256,512]{1,0:T(8,128)S(1)} copy-done((f32[256,512]{1,0:T(8,128)S(1)}, f32[256,512]{1,0:T(8,128)}, u32[]{:S(2)}) %copy-start.5) | copy-done | bytes 524312
  50.1 0.9 %join.1 = (bf16[256,512]{1,0:T(8,128)(2,1)}, bf16[256,512]{1,0:T(8,128)(2,1)}) custom-call(s32[1]{0:T(128)} %bitcast.here.place, f32[256,512]{1,0:T(8,128)S(1)} %get-tuple-element.34.two_ref, f32[256,512]{1,0:T(8,128)S(1)} %copy-done.5, bf16[256,1024]{1,0:T(8,128)(2,1)S(1)} %collective-permute-done.6.other_ref), custom_call_target="tpu_custom_call" | custom-call | bytes 1048576 | tf_op jit(solution)/shard_map/join/pallas_call | solution.py:238
  51.0 1.0 %collective-permute-start.8 = (bf16[256,512]{1,0:T(8,128)(2,1)}, bf16[256,512]{1,0:T(8,128)(2,1)}, u32[]{:S(2)}, u32[]{:S(2)}) collective-permute-start(bf16[256,512]{1,0:T(8,128)(2,1)} %get-tuple-element.41), channel_id=1, source_target_pairs={{0,240},{4,244},{8,248},{12,252},{16,0},{20,4},{24,8},{28,12},{32,... | collective-permute-start | bytes 786440 | tf_op jit(solution)/shard_map/ppermute | solution.py:28
  52.0 4.1 %collective-permute-start.7 = (bf16[256,512]{1,0:T(8,128)(2,1)}, bf16[256,512]{1,0:T(8,128)(2,1)}, u32[]{:S(2)}, u32[]{:S(2)}) collective-permute-start(bf16[256,512]{1,0:T(8,128)(2,1)} %get-tuple-element.37), channel_id=1, source_target_pairs={{0,248},{4,252},{8,0},{12,4},{16,8},{20,12},{24,16},{28,20},{32,24... | collective-permute-start | bytes 786440 | tf_op jit(solution)/shard_map/ppermute | solution.py:28
  56.0 1.2 %copy-done.3 = bf16[256,2048]{1,0:T(8,128)(2,1)S(1)} copy-done((bf16[256,2048]{1,0:T(8,128)(2,1)S(1)}, bf16[256,2048]{1,0:T(8,128)(2,1)}, u32[]{:S(2)}) %copy-start.3) | copy-done | bytes 1048600
  57.3 6.3 %own_backward.1 = (bf16[256,2048]{1,0:T(8,128)(2,1)}, f32[256,512]{1,0:T(8,128)S(1)}) custom-call(s32[32]{0:T(128)S(1)} %copy-done.12, s32[1]{0:T(128)} %bitcast.here.place, bf16[256,2048]{1,0:T(8,128)(2,1)S(1)} %copy-done.1, bf16[256,2048]{1,0:T(8,128)(2,1)S(1)} %copy-done.2, bf16[256,2048]{1,0:T(8,128)(2,1)S(1)} %copy-done.3, f32[256,128]{1,0:T(8,128)S(1)} %copy-done.10, ...), custom_call_target="tpu_custom_call" | custom-call | flops 1073741824 | bytes 1048576 | tf_op jit(solution)/shard_map/own_backward/pallas_call | solution.py:238
  63.9 2.3 %copy.10 = bf16[4,8,8,2048]{3,2,0,1:T(8,128)(2,1)} copy(bf16[4,8,8,2048]{3,2,1,0:T(8,128)(2,1)} %bitcast.3) | data formatting | bytes 2097152 | tf_op jit(solution)/shard_map/reshape | solution.py:359
  66.2 5.5 %collective-permute-done.7.two_ref = bf16[256,512]{1,0:T(8,128)(2,1)} collective-permute-done((bf16[256,512]{1,0:T(8,128)(2,1)}, bf16[256,512]{1,0:T(8,128)(2,1)}, u32[]{:S(2)}, u32[]{:S(2)}) %collective-permute-start.7) | collective-permute-done | bytes 262176 | tf_op jit(solution)/shard_map/ppermute | solution.py:28
  71.7 1.8 %total.1 = (bf16[256,256]{1,0:T(8,128)(2,1)}, bf16[256,256]{1,0:T(8,128)(2,1)}) custom-call(f32[256,512]{1,0:T(8,128)S(1)} %get-tuple-element.40.own_ref, bf16[256,512]{1,0:T(8,128)(2,1)} %collective-permute-done.7.two_ref, bf16[256,512]{1,0:T(8,128)(2,1)} %collective-permute-done.8.four_ref), custom_call_target="tpu_custom_call" | custom-call | bytes 1048576 | tf_op jit(solution)/shard_map/total/pallas_call | solution.py:238
  (30 shorter events, 1.6 us)
Async XLA Ops:
  0.6 16.6 %collective-permute-start.3 = (bf16[256,256]{1,0:T(8,128)(2,1)}, bf16[256,256]{1,0:T(8,128)(2,1)S(1)}, u32[]{:S(2)}, u32[]{:S(2)}) collective-permute-start(bf16[256,256]{1,0:T(8,128)(2,1)} %v_ref.3), channel_id=1, source_target_pairs={{0,8},{4,12},{8,16},{12,20},{16,24},{20,28},{24,32},{28,36},{32,40... | collective-permute-start | bytes 393224 | tf_op jit(solution)/shard_map/ppermute | solution.py:28
  3.2 14.1 %collective-permute-start.4 = (bf16[256,256]{1,0:T(8,128)(2,1)}, bf16[256,256]{1,0:T(8,128)(2,1)S(1)}, u32[]{:S(2)}, u32[]{:S(2)}) collective-permute-start(bf16[256,256]{1,0:T(8,128)(2,1)} %v_ref.3), channel_id=1, source_target_pairs={{0,16},{4,20},{8,24},{12,28},{16,32},{20,36},{24,40},{28,44},{32,4... | collective-permute-start | bytes 393224 | tf_op jit(solution)/shard_map/ppermute | solution.py:28
  6.2 15.6 %collective-permute-start = (bf16[256,256]{1,0:T(8,128)(2,1)}, bf16[256,256]{1,0:T(8,128)(2,1)S(1)}, u32[]{:S(2)}, u32[]{:S(2)}) collective-permute-start(bf16[256,256]{1,0:T(8,128)(2,1)} %k_ref.3), channel_id=1, source_target_pairs={{0,8},{4,12},{8,16},{12,20},{16,24},{20,28},{24,32},{28,36},{32,40... | collective-permute-start | bytes 393224 | tf_op jit(solution)/shard_map/ppermute | solution.py:28
  9.0 16.7 %collective-permute-start.1 = (bf16[256,256]{1,0:T(8,128)(2,1)}, bf16[256,256]{1,0:T(8,128)(2,1)S(1)}, u32[]{:S(2)}, u32[]{:S(2)}) collective-permute-start(bf16[256,256]{1,0:T(8,128)(2,1)} %k_ref.3), channel_id=1, source_target_pairs={{0,16},{4,20},{8,24},{12,28},{16,32},{20,36},{24,40},{28,44},{32,4... | collective-permute-start | bytes 393224 | tf_op jit(solution)/shard_map/ppermute | solution.py:28
  10.2 1.2 %copy-start = (bf16[256,2048]{1,0:T(8,128)(2,1)S(1)}, bf16[256,2048]{1,0:T(8,128)(2,1)}, u32[]{:S(2)}) copy-start(bf16[256,2048]{1,0:T(8,128)(2,1)} %q_ref.3) | copy-start | bytes 3145732
  11.4 0.9 %copy-start.6 = (bf16[256,256]{1,0:T(8,128)(2,1)S(1)}, bf16[256,256]{1,0:T(8,128)(2,1)}, u32[]{:S(2)}) copy-start(bf16[256,256]{1,0:T(8,128)(2,1)} %k_ref.3) | copy-start | bytes 393220
  12.3 0.9 %copy-start.8 = (bf16[256,256]{1,0:T(8,128)(2,1)S(1)}, bf16[256,256]{1,0:T(8,128)(2,1)}, u32[]{:S(2)}) copy-start(bf16[256,256]{1,0:T(8,128)(2,1)} %v_ref.3) | copy-start | bytes 393220
  13.2 0.7 copy-start.11
  13.9 14.8 %copy-start.1 = (bf16[256,2048]{1,0:T(8,128)(2,1)S(1)}, bf16[256,2048]{1,0:T(8,128)(2,1)}, u32[]{:S(2)}) copy-start(bf16[256,2048]{1,0:T(8,128)(2,1)} %q_ref.3) | copy-start | bytes 3145732
  13.9 14.8 %copy-start.2 = (bf16[256,2048]{1,0:T(8,128)(2,1)S(1)}, bf16[256,2048]{1,0:T(8,128)(2,1)}, u32[]{:S(2)}) copy-start(bf16[256,2048]{1,0:T(8,128)(2,1)} %g_ref.1) | copy-start | bytes 3145732
  17.3 10.3 %collective-permute-start.5 = (bf16[256,512]{1,0:T(8,128)(2,1)S(1)}, bf16[256,512]{1,0:T(8,128)(2,1)S(1)}, u32[]{:S(2)}, u32[]{:S(2)}) collective-permute-start(bf16[256,512]{1,0:T(8,128)(2,1)S(1)} %choose.3), channel_id=1, source_target_pairs={{0,4},{4,0},{8,12},{12,8},{16,20},{20,16},{24,28},{28,24},{32,36},... | collective-permute-start | bytes 786440 | tf_op jit(solution)/shard_map/ppermute | solution.py:28
  25.7 3.0 %collective-permute-start.2 = (bf16[256,512]{1,0:T(8,128)(2,1)S(1)}, bf16[256,512]{1,0:T(8,128)(2,1)S(1)}, u32[]{:S(2)}, u32[]{:S(2)}) collective-permute-start(bf16[256,512]{1,0:T(8,128)(2,1)S(1)} %choose.2), channel_id=1, source_target_pairs={{0,4},{4,0},{8,12},{12,8},{16,20},{20,16},{24,28},{28,24},{32,36},... | collective-permute-start | bytes 786440 | tf_op jit(solution)/shard_map/ppermute | solution.py:28
  43.5 0.8 %copy-start.4 = (f32[256,512]{1,0:T(8,128)}, f32[256,512]{1,0:T(8,128)S(1)}, u32[]{:S(2)}) copy-start(f32[256,512]{1,0:T(8,128)S(1)} %get-tuple-element.35.four_ref) | copy-start | bytes 1572868
  44.3 11.7 %copy-start.7 = (bf16[256,256]{1,0:T(8,128)(2,1)S(1)}, bf16[256,256]{1,0:T(8,128)(2,1)}, u32[]{:S(2)}) copy-start(bf16[256,256]{1,0:T(8,128)(2,1)} %k_ref.3) | copy-start | bytes 393220
  44.3 11.7 %copy-start.9 = (bf16[256,256]{1,0:T(8,128)(2,1)S(1)}, bf16[256,256]{1,0:T(8,128)(2,1)}, u32[]{:S(2)}) copy-start(bf16[256,256]{1,0:T(8,128)(2,1)} %v_ref.3) | copy-start | bytes 393220
  44.3 11.7 %copy-start.10 = (f32[256,128]{1,0:T(8,128)S(1)}, f32[256,128]{1,0:T(8,128)}, u32[]{:S(2)}) copy-start(f32[256,128]{1,0:T(8,128)} %get-tuple-element.38.keep_ref) | copy-start | bytes 393220
  44.3 11.7 %copy-start.12 = (s32[32]{0:T(128)S(1)}, s32[32]{0:T(128)}, u32[]{:S(2)}) copy-start(s32[32]{0:T(128)} %lens.3) | copy-start | bytes 388
  44.3 4.7 %collective-permute-start.6 = (bf16[256,1024]{1,0:T(8,128)(2,1)}, bf16[256,1024]{1,0:T(8,128)(2,1)S(1)}, u32[]{:S(2)}, u32[]{:S(2)}) collective-permute-start(bf16[256,1024]{1,0:T(8,128)(2,1)} %get-tuple-element.36), channel_id=1, source_target_pairs={{0,4},{4,0},{8,12},{12,8},{16,20},{20,16},{24,28},{28,24},{32,36},... | collective-permute-start | bytes 1572872 | tf_op jit(solution)/shard_map/ppermute | solution.py:28
  44.8 19.1 %all-to-all-start = ((bf16[4,64,2048]{2,1,0:T(8,128)(2,1)}), bf16[4,64,2048]{2,1,0:T(8,128)(2,1)}, u32[]{:S(2)}, u32[]{:S(2)}) async-start(bf16[4,64,2048]{2,1,0:T(8,128)(2,1)} %bitcast.5), calls=%async_computation | async-start | bytes 2097152 | tf_op jit(solution)/shard_map/all_to_all | solution.py:330
  49.1 1.0 %copy-start.5 = (f32[256,512]{1,0:T(8,128)S(1)}, f32[256,512]{1,0:T(8,128)}, u32[]{:S(2)}) copy-start(f32[256,512]{1,0:T(8,128)} %copy-done.4) | copy-start | bytes 1572868
  51.0 15.2 %collective-permute-start.8 = (bf16[256,512]{1,0:T(8,128)(2,1)}, bf16[256,512]{1,0:T(8,128)(2,1)}, u32[]{:S(2)}, u32[]{:S(2)}) collective-permute-start(bf16[256,512]{1,0:T(8,128)(2,1)} %get-tuple-element.41), channel_id=1, source_target_pairs={{0,240},{4,244},{8,248},{12,252},{16,0},{20,4},{24,8},{28,12},{32,... | collective-permute-start | bytes 786440 | tf_op jit(solution)/shard_map/ppermute | solution.py:28
  52.0 19.7 %collective-permute-start.7 = (bf16[256,512]{1,0:T(8,128)(2,1)}, bf16[256,512]{1,0:T(8,128)(2,1)}, u32[]{:S(2)}, u32[]{:S(2)}) collective-permute-start(bf16[256,512]{1,0:T(8,128)(2,1)} %get-tuple-element.37), channel_id=1, source_target_pairs={{0,248},{4,252},{8,0},{12,4},{16,8},{20,12},{24,16},{28,20},{32,24... | collective-permute-start | bytes 786440 | tf_op jit(solution)/shard_map/ppermute | solution.py:28
  56.0 1.2 %copy-start.3 = (bf16[256,2048]{1,0:T(8,128)(2,1)S(1)}, bf16[256,2048]{1,0:T(8,128)(2,1)}, u32[]{:S(2)}) copy-start(bf16[256,2048]{1,0:T(8,128)(2,1)} %get-tuple-element.32.far_ref) | copy-start | bytes 3145732
